TPU v7x, 32 devices: a whole 2x2x4 slice. The times are simulated.
32 devices in a mesh: rows: 8 (over z, y), sub: 4 (over x, core).
Axes of the slice: x: 2, y: 2, z: 4, core: 2. Of those that a mesh axis runs over, the one named last changes fastest.
Arguments:
- panel: float32 [12288, 256], P(('rows', 'sub'))
- trailing: float32 [12288, 1024], P(('rows', 'sub')), may hold values from -6 to 6
- live_rows: int32 [32], P(('rows', 'sub')), may hold values from 192 to 384, as said below
Outputs:
- basis: float32 [12288, 256], P(('rows', 'sub'))
- top_block: float32 [256, 1024], P(None, 'sub')
- remainder: float32 [12288, 1024], P(('rows', 'sub'))
Inputs may be any that keep to these rules, and one draw needn't show every extreme that they name: `live_rows`: the live cells of a list are its first slots; the others are padding. Some list is full and some list holds exactly 192 cells.
All inputs are finite; a program needn't handle non-finite values.
Results may differ from a plain program's by a relative error of at most 0.00014.
Values sent between devices are 32-bit elements; how exact they have to be, the bound alone decides.
No kernel may reach another device: no remote copies, remote signals or barrier semaphores. Data moves between devices by JAX's collectives and lax.ppermute only.
A program may use at most 64 MiB of HBM per device.

v0:
```python
import jax
import jax.numpy as jnp
from jax import lax
from jax.sharding import PartitionSpec as P

TILE = 128


def accumulate(left, right, tile_count):
    start_value = jnp.zeros((left.shape[1], right.shape[1]), jnp.float32)

    def add_tile(which, running):
        left_rows = lax.dynamic_slice_in_dim(left, which * TILE, TILE, 0)
        right_rows = lax.dynamic_slice_in_dim(right, which * TILE, TILE, 0)
        return running + jnp.dot(
            left_rows.T,
            right_rows,
            precision=lax.Precision.HIGHEST,
            preferred_element_type=jnp.float32,
        )

    return lax.fori_loop(0, tile_count, add_tile, start_value)


def body(panel, trailing, live_rows):
    rows_here = panel.shape[0]
    live_count = live_rows[0]
    row_index = lax.broadcasted_iota(jnp.int32, (rows_here, 1), 0)
    live_mask = row_index < live_count
    masked_panel = jnp.where(live_mask, panel, jnp.zeros_like(panel))
    masked_trail = jnp.where(live_mask, trailing, jnp.zeros_like(trailing))
    live_share = live_rows.astype(jnp.float32)
    tile_count = (live_count + TILE - 1) // TILE
    gram = accumulate(masked_panel, masked_panel, tile_count)
    gram, total = lax.psum((gram, live_share), ("rows", "sub"))
    factor = jnp.linalg.cholesky(gram / total[0])
    root_total = jnp.sqrt(total[0])
    basis = jax.scipy.linalg.solve_triangular(factor, masked_panel.T, lower=True).T
    local_top = jnp.dot(
        basis.T, masked_trail, precision=lax.Precision.HIGHEST, preferred_element_type=jnp.float32
    )
    top_whole = lax.psum(local_top, ("rows", "sub")) / root_total
    remainder = (
        masked_trail
        - jnp.dot(
            basis, top_whole, precision=lax.Precision.HIGHEST, preferred_element_type=jnp.float32
        )
        / root_total
    )
    column_width = top_whole.shape[1] // lax.axis_size("sub")
    top_block = lax.dynamic_slice_in_dim(
        top_whole, lax.axis_index("sub") * column_width, column_width, 1
    )
    return (basis, top_block, remainder)


def solution(mesh):
    in_specs = (P(("rows", "sub"), None), P(("rows", "sub"), None), P(("rows", "sub")))
    out_specs = (P(("rows", "sub"), None), P(None, "sub"), P(("rows", "sub"), None))
    return jax.shard_map(body, mesh=mesh, in_specs=in_specs, out_specs=out_specs, check_vma=False)
```

profile of v0, /device:TPU:0, one launch (start us, length us, event | category | flops | bytes accessed | tf_op | source)
XLA Modules:
  0.0 350.2 jit_solution(10997142111719962875)
XLA Ops:
  7.9 1.1 broadcast_select_fusion
  9.1 1.5 while.11
  10.6 0.8 copy.6
  11.6 42.2 %psum.22 = f32[]{:T(128)} all-reduce(f32[]{:T(128)} %bitcast.1), channel_id=1, replica_groups=mesh['rows'=8,'sub'=4] {'rows','sub'}, use_global_device_ids=true, to_apply=%region_3.4 | all-reduce | flops 1 | bytes 8 | tf_op jit(solution)/shard_map/psum | solution.py:35
  53.8 88.0 %all-reduce.4.cloned.1.call-done = f32[256,256]{0,1:T(8,128)} async-done(((f32[256,256]{0,1:T(8,128)}), f32[256,256]{0,1:T(8,128)}) %all-reduce.4.cloned.1.call-update) | async-done | bytes 262160 | tf_op jit(solution)/shard_map/psum | solution.py:35
  141.8 1.7 broadcast_divide_fusion.1
  143.6 1.7 fusion.6
  145.3 11.7 %cholesky.49 = f32[128,128]{1,0:T(8,128)S(1)} custom-call(f32[128,128]{1,0:T(8,128)S(1)} %cholesky.115), custom_call_target="Cholesky" | custom-call | tf_op jit(solution)/shard_map/jit(cholesky)/cholesky | solution.py:36
  157.1 9.8 %custom-call.15 = f32[1,128,128]{1,2,0:T(8,128)S(1)} custom-call(f32[1,128,128]{2,1,0:T(8,128)S(1)} %get-tuple-element.59), custom_call_target="InvertDiagBlocksLowerTriangular" | custom-call | tf_op jit(solution)/shard_map/jit(cholesky)/cholesky | solution.py:36
  167.4 11.7 %cholesky.103 = f32[128,128]{1,0:T(8,128)S(1)} custom-call(f32[128,128]{1,0:T(8,128)S(1)} %convolution_subtract_fusion.1), custom_call_target="Cholesky" | custom-call | tf_op jit(solution)/shard_map/jit(cholesky)/cholesky | solution.py:36
  179.2 0.6 compare_reduce_fusion
  181.2 4.0 %while.12 = (s32[]{:T(128)}, f32[256,256]{1,0:T(8,128)S(1)}, s32[2,2]{1,0:T(2,128)S(1)}, f32[2,128,128]{2,1,0:T(8,128)S(1)}, s32[]{:T(128)}) while((s32[]{:T(128)}, f32[256,256]{1,0:T(8,128)S(1)}, s32[2,2]{1,0:T(2,128)S(1)}, f32[2,128,128]{2,1,0:T(8,128)S(1)}, s32[]{:T(128)}) %tuple.44), condition=%wide.while_cond, body=%wide.while_body.sunk | while | flops 2 | bytes 131189 | solution.py:38
  181.2 0.6 fusion.27
  181.8 1.4 bitcast_dynamic-update-slice_fusion.2
  183.2 0.6 fusion.27
  183.8 1.4 bitcast_dynamic-update-slice_fusion.2
  185.2 19.9 %custom-call.16 = f32[2,128,128]{1,2,0:T(8,128)S(1)} custom-call(f32[2,128,128]{2,1,0:T(8,128)S(1)} %get-tuple-element.34), custom_call_target="InvertDiagBlocksLowerTriangular" | custom-call | tf_op jit(solution)/shard_map/jit(_solve_triangular)/triangular_solve | solution.py:38
  205.5 0.5 convolution_subtract_fusion
  206.4 3.0 fusion.2
  210.2 0.9 copy.8
  211.1 127.4 %all-reduce.6.cloned.1.call-done = f32[256,1024]{1,0:T(8,128)} async-done(((f32[256,1024]{1,0:T(8,128)}), f32[256,1024]{1,0:T(8,128)}) %all-reduce.6.cloned.1.call-update) | async-done | bytes 1048592 | tf_op jit(solution)/shard_map/psum | solution.py:42
  338.4 1.4 broadcast_divide_fusion
  339.9 0.7 constant_dynamic-slice_fusion.1
  340.6 2.7 divide_subtract_fusion
  (32 shorter events, 3.3 us)
Async XLA Ops:
  7.2 134.7 %all-reduce.4.cloned.1.call-start = ((), (), s32[]{:S(2)}) async-start(), calls=%async_computation | async-start | bytes 524288 | tf_op jit(solution)/shard_map/psum | solution.py:35
  9.0 2.5 copy-start.1
  11.5 327.0 %all-reduce.6.cloned.1.call-start = ((), (), s32[]{:S(2)}) async-start(), calls=%async_computation.1 | async-start | bytes 2097152 | tf_op jit(solution)/shard_map/psum | solution.py:42
  167.4 39.0 %copy-start = (f32[384,1024]{1,0:T(8,128)S(1)}, f32[384,1024]{1,0:T(8,128)}, u32[]{:S(2)}) copy-start(f32[384,1024]{1,0:T(8,128)} %param.6) | copy-start | bytes 4718596
  338.4 2.2 copy-start.2
Sparse Core Ops, SparseCore 0:
  14.1 127.7 all-reduce.3
  209.5 128.8 all-reduce.5
where the time goes:
time: 351 us; the launch traced here: 350 us
  waiting for transfers between devices  215 us (61%)
  other arithmetic  59.9 us (17%)
  blocking collectives  42.2 us (12%)
  between operations  16.9 us (5%)
  matrix products  8.9 us (3%)
  local copies, waits for them, and re-layouts  6.69 us (2%)
    psum x1, waiting for transfers between devices, body(): top_whole = lax.psum(local_top, ('rows', 'sub')) / root_total  127 us
    psum x1, waiting for transfers between devices, body(): gram, total = lax.psum((gram, live_share), ('rows', 'sub'))  88 us
    psum x1, blocking collectives, body(): gram, total = lax.psum((gram, live_share), ('rows', 'sub'))  42.2 us
    another operation x6, other arithmetic, body(): factor = jnp.linalg.cholesky(gram / total[0])  33.9 us
    another operation x3, other arithmetic, body(): jax.scipy.linalg.solve_triangular(factor, masked_panel.T, lower=True)  19.9 us
  transfers between devices with their start and end apart: 2, of which 2 were waited for; matrix products, arithmetic and copies ran while one was open for 0% of the time, Pallas kernels for 0%

commit v1 on v0

v1 whole, which is shorter than its diff:
```python
import functools

import jax
import jax.numpy as jnp
from jax import lax
from jax.experimental import pallas as pl
from jax.experimental.pallas import tpu as pltpu
from jax.sharding import Mesh
from jax.sharding import PartitionSpec as P

CHIPS = ("z", "y", "x")
AXES = ("z", "y", "x", "core")
HIGHEST = lax.Precision.HIGHEST


def dot(left, right, contract, precision=HIGHEST):
    return lax.dot_general(
        left, right, (contract, ((), ())), precision=precision, preferred_element_type=jnp.float32
    )


def live_rows_mask(rows, live):
    return lax.broadcasted_iota(jnp.int32, (rows, 1), 0) < live


def products_kernel(core_ref, live_ref, panel_ref, trail_ref, keep_ref, send_ref):
    rows, width = panel_ref.shape
    half = width // 2
    live = live_ref[0]
    mine = live_rows_mask(rows, live)
    first = pl.multiple_of(core_ref[0] * half, half)
    second = pl.multiple_of((1 - core_ref[0]) * half, half)
    panel = jnp.where(mine, panel_ref[...], 0.0)
    trail = jnp.where(mine, trail_ref[...], 0.0)
    ordered = jnp.concatenate(
        [panel_ref[:, pl.ds(first, half)], panel_ref[:, pl.ds(second, half)]], axis=1
    )
    ordered = jnp.where(mine, ordered, 0.0)
    gram = dot(ordered, panel, ((0,), (0,)))
    cross = dot(ordered, trail, ((0,), (0,)))
    keep_ref[:, :width] = gram[:half]
    keep_ref[:, width:] = cross[:half]
    send_ref[:, :width] = gram[half:]
    send_ref[:, width:] = cross[half:]
    count = jnp.full((half, half), live, jnp.int32).astype(jnp.float32)

    @pl.when(core_ref[0] == 0)
    def _():
        keep_ref[:, half:width] = count

    @pl.when(core_ref[0] != 0)
    def _():
        send_ref[:, half:width] = count


def products(core, live, panel, trail):
    rows, width = panel.shape
    columns = width + trail.shape[1]
    out = jax.ShapeDtypeStruct((width // 2, columns), jnp.float32)
    return pl.pallas_call(
        products_kernel,
        out_shape=(out, out),
        in_specs=[
            pl.BlockSpec(memory_space=pltpu.SMEM),
            pl.BlockSpec(memory_space=pltpu.SMEM),
            pl.BlockSpec(memory_space=pltpu.VMEM),
            pl.BlockSpec(memory_space=pltpu.VMEM),
        ],
        out_specs=(pl.BlockSpec(memory_space=pltpu.VMEM),) * 2,
    )(core, live, panel, trail)


def final_kernel(
    core_ref, sub_ref, live_ref, total_ref, inverse_ref, own_ref, other_ref, panel_ref, trail_ref,
    basis_ref, top_ref, rest_ref, top_scr,
):
    rows, width = panel_ref.shape
    half = width // 2
    mine = live_rows_mask(rows, live_ref[0])
    panel = jnp.where(mine, panel_ref[...], 0.0)
    trail = jnp.where(mine, trail_ref[...], 0.0)
    first = pl.multiple_of(core_ref[0] * half, half)
    second = pl.multiple_of((1 - core_ref[0]) * half, half)
    unit = dot(panel, inverse_ref[...], ((1,), (1,)))
    basis_ref[...] = unit * jnp.sqrt(total_ref[0, 0])
    top = dot(inverse_ref[:, pl.ds(first, half)], own_ref[:, width:], ((1,), (0,))) + dot(
        inverse_ref[:, pl.ds(second, half)], other_ref[:, width:], ((1,), (0,))
    )
    top_scr[...] = top
    rest_ref[...] = trail - dot(unit, top, ((1,), (0,)))
    wide = top_ref.shape[1]
    top_ref[...] = top_scr[:, pl.ds(pl.multiple_of(sub_ref[0] * wide, wide), wide)]


def final(core, sub, live, total, inverse, own, other, panel, trail, wide):
    rows, width = panel.shape
    columns = trail.shape[1]
    f32 = jnp.float32
    return pl.pallas_call(
        final_kernel,
        out_shape=(
            jax.ShapeDtypeStruct((rows, width), f32),
            jax.ShapeDtypeStruct((width, wide), f32),
            jax.ShapeDtypeStruct((rows, columns), f32),
        ),
        in_specs=[pl.BlockSpec(memory_space=pltpu.SMEM)] * 3
        + [pl.BlockSpec(memory_space=pltpu.VMEM)] * 6,
        out_specs=(pl.BlockSpec(memory_space=pltpu.VMEM),) * 3,
        scratch_shapes=[pltpu.VMEM((width, columns), f32)],
    )(core, sub, live, total, inverse, own, other, panel, trail)


def swap(x):
    return lax.ppermute(x, "core", [(0, 1), (1, 0)])


def body(chips, panel, trailing, live_rows):
    width = panel.shape[1]
    half = width // 2
    core = lax.axis_index("core")
    sub = lax.axis_index("x") * 2 + core
    subs = lax.axis_size("x") * 2
    core_s, sub_s = core[None], sub[None]
    keep, send = products(core_s, live_rows, panel, trailing)
    mine = keep + swap(send)
    shape = mine.shape
    if half % chips == 0:
        chunks = mine.reshape(chips, half // chips, shape[1])
    else:
        chunks = mine.reshape(chips, -1)
    parts = lax.all_to_all(chunks, CHIPS, 0, 0, tiled=True)
    summed = jnp.broadcast_to(jnp.sum(parts, axis=0, keepdims=True), chunks.shape)
    own = lax.all_to_all(summed, CHIPS, 0, 0, tiled=True).reshape(shape)
    other = swap(own)
    low = jnp.where(core == 0, own[:, :width], other[:, :width])
    high = jnp.where(core == 0, other[:, :width], own[:, :width])
    total = low[0:1, half : half + 1]
    gram = jnp.concatenate(
        [jnp.concatenate([low[:, :half], high[:, :half].T], axis=1), high], axis=0
    )
    factor = jnp.linalg.cholesky(gram, symmetrize_input=False)
    inverse = jax.scipy.linalg.solve_triangular(factor, jnp.eye(width, dtype=jnp.float32), lower=True)
    return final(
        core_s, sub_s, live_rows, total, inverse, own, other, panel, trailing,
        trailing.shape[1] // subs,
    )


def solution(mesh):
    rows, subs = mesh.shape["rows"], mesh.shape["sub"]
    grid = Mesh(mesh.devices.reshape(rows // 2, 2, subs // 2, 2), AXES)
    chips = rows * subs // 2
    in_specs = (P(AXES, None), P(AXES, None), P(AXES))
    out_specs = (P(AXES, None), P(None, ("x", "core")), P(AXES, None))
    return jax.shard_map(
        functools.partial(body, chips),
        mesh=grid,
        in_specs=in_specs,
        out_specs=out_specs,
        check_vma=False,
    )
```

time: 351 us -> 130 us (0.37)
  waiting for transfers between devices: 215 us -> 3.99 us
  between operations: 16.9 us -> 2.69 us
  Pallas kernels: 0 us -> 12.6 us
  matrix products: 8.9 us -> 1.31 us
  blocking collectives: 42.2 us -> 48.3 us
  other arithmetic: 59.9 us -> 55.9 us
    psum x2 -> x0, waiting for transfers between devices: 215 us -> none  [the longest x1 127 us: body(): top_whole = lax.psum(local_top, ('rows', 'sub')) / root_total]
    all_to_all x0 -> x2, blocking collectives: none -> 48.3 us  [the longest x1 27.1 us: body(): parts = lax.all_to_all(chunks, CHIPS, 0, 0, tiled=True)]
    psum x1 -> x0, blocking collectives: 42.2 us -> none  [body(): gram, total = lax.psum((gram, live_share), ('rows', 'sub'))]
    pallas_call x0 -> x2, Pallas kernels: none -> 12.6 us  [the longest x1 7.7 us: final(): pl.pallas_call(final_kernel, out_shape=(jax.ShapeDtypeStruct((rows, width...]
    dot_general x5 -> x0, matrix products: 7.14 us -> none  [the longest x1 2.96 us: body(): jnp.dot(basis.T, masked_trail, precision=lax.Precision.HIGHEST, preferred...]
    div x3 -> x0, other arithmetic: 4.79 us -> none  [the longest x2 3.34 us: body(): factor = jnp.linalg.cholesky(gram / total[0])]
    ppermute x0 -> x2, waiting for transfers between devices: none -> 3.99 us  [swap(): return lax.ppermute(x, 'core', [(0, 1), (1, 0)])]
    another operation x9 -> x10, other arithmetic: 53.8 us -> 54.6 us  [the longest x6 33.9 us: body(): factor = jnp.linalg.cholesky(gram, symmetrize_input=False)]
where the time goes in v1:
time: 130 us
  other arithmetic  55.9 us (43%)
  blocking collectives  48.3 us (37%)
  Pallas kernels  12.6 us (10%)
  local copies, waits for them, and re-layouts  4.68 us (4%)
  waiting for transfers between devices  3.99 us (3%)
  between operations  2.69 us (2%)
  matrix products  1.31 us (1%)
    another operation x6, other arithmetic, body(): factor = jnp.linalg.cholesky(gram, symmetrize_input=False)  33.9 us
    all_to_all x1, blocking collectives, body(): parts = lax.all_to_all(chunks, CHIPS, 0, 0, tiled=True)  27.1 us
    all_to_all x1, blocking collectives, body(): own = lax.all_to_all(summed, CHIPS, 0, 0, tiled=True).reshape(shape)  21.2 us
    another operation x4, other arithmetic, body(): jax.scipy.linalg.solve_triangular(factor, jnp.eye(width, dtype=jnp.float3...  20.7 us
    pallas_call x1, Pallas kernels, final(): pl.pallas_call(final_kernel, out_shape=(jax.ShapeDtypeStruct((rows, width...  7.7 us
    pallas_call x1, Pallas kernels, products(): pl.pallas_call(products_kernel, out_shape=(out, out), in_specs=[pl.BlockS...  4.91 us
    ppermute x2, waiting for transfers between devices, swap(): return lax.ppermute(x, 'core', [(0, 1), (1, 0)])  3.99 us
    another operation x6, local copies, waits for them, and re-layouts  3.95 us
  transfers between devices with their start and end apart: 2, of which 2 were waited for; matrix products, arithmetic and copies ran while one was open for 0% of the time, Pallas kernels for 0%

profile of v1, /device:TPU:0, one launch (start us, length us, event | category | flops | bytes accessed | tf_op | source)
XLA Modules:
  0.0 129.9 jit_solution(8303534845293388747)
XLA Ops:
  1.3 4.9 %shard_map.58 = (f32[128,1280]{1,0:T(8,128)}, f32[128,1280]{1,0:T(8,128)}) custom-call(s32[1]{0:T(128)} %bitcast.core_ref, s32[1]{0:T(128)S(6)} %copy.17.live_ref, f32[384,256]{1,0:T(8,128)} %panel_ref.3, f32[384,1024]{1,0:T(8,128)} %trail_ref.3), custom_call_target="tpu_custom_call" | custom-call | tf_op jit(solution)/shard_map/pallas_call | solution.py:60
  6.2 0.5 collective-permute-start
  6.6 1.9 %collective-permute-done = f32[128,1280]{1,0:T(8,128)S(1)} collective-permute-done((f32[128,1280]{1,0:T(8,128)}, f32[128,1280]{1,0:T(8,128)S(1)}, u32[]{:S(2)}, u32[]{:S(2)}) %collective-permute-start) | collective-permute-done | bytes 655392 | tf_op jit(solution)/shard_map/ppermute | solution.py:114
  8.6 1.2 add_bitcast_fusion
  9.7 27.1 %all_to_all.10 = f32[16,8,1280]{2,1,0:T(8,128)S(1)} all-to-all(f32[16,8,1280]{2,1,0:T(8,128)S(1)} %add_bitcast_fusion), channel_id=1, replica_groups=mesh['z'=4,'y'=2,'x'=2,'core'=2] {'z','y','x'}, dimensions={0} | all-to-all | bytes 1310720 | tf_op jit(solution)/shard_map/all_to_all | solution.py:131
  36.9 21.2 %all_to_all.11 = f32[16,8,1280]{2,1,0:T(8,128)S(1)} all-to-all(f32[16,8,1280]{2,1,0:T(8,128)S(1)} %broadcast_in_dim.16), channel_id=1, replica_groups=mesh['z'=4,'y'=2,'x'=2,'core'=2] {'z','y','x'}, dimensions={0} | all-to-all | bytes 1310720 | tf_op jit(solution)/shard_map/all_to_all | solution.py:133
  58.2 2.1 %collective-permute-done.1.other_ref = f32[128,1280]{1,0:T(8,128)S(1)} collective-permute-done((f32[128,1280]{1,0:T(8,128)S(1)}, f32[128,1280]{1,0:T(8,128)S(1)}, u32[]{:S(2)}, u32[]{:S(2)}) %collective-permute-start.1) | collective-permute-done | bytes 655392 | tf_op jit(solution)/shard_map/ppermute | solution.py:114
  60.2 0.6 slice.83.total_ref
  60.8 11.7 %cholesky.48 = f32[128,128]{1,0:T(8,128)S(1)} custom-call(f32[128,128]{1,0:T(8,128)S(1)} %slice.84), custom_call_target="Cholesky" | custom-call | tf_op jit(solution)/shard_map/jit(cholesky)/cholesky | solution.py:141
  72.6 9.8 %custom-call.15 = f32[1,128,128]{1,2,0:T(8,128)S(1)} custom-call(f32[1,128,128]{2,1,0:T(8,128)S(1)} %get-tuple-element.30), custom_call_target="InvertDiagBlocksLowerTriangular" | custom-call | tf_op jit(solution)/shard_map/jit(cholesky)/cholesky | solution.py:141
  82.6 0.3 slice_subtract_fusion
  82.9 11.7 %cholesky.102 = f32[128,128]{1,0:T(8,128)S(1)} custom-call(f32[128,128]{1,0:T(8,128)S(1)} %slice_subtract_fusion), custom_call_target="Cholesky" | custom-call | tf_op jit(solution)/shard_map/jit(cholesky)/cholesky | solution.py:141
  94.7 0.6 compare_reduce_fusion
  96.7 4.0 %while.1 = (s32[]{:T(128)}, f32[256,256]{1,0:T(8,128)S(1)}, s32[2,2]{1,0:T(2,128)S(1)}, f32[2,128,128]{2,1,0:T(8,128)S(1)}, s32[]{:T(128)}) while((s32[]{:T(128)}, f32[256,256]{1,0:T(8,128)S(1)}, s32[2,2]{1,0:T(2,128)S(1)}, f32[2,128,128]{2,1,0:T(8,128)S(1)}, s32[]{:T(128)}) %tuple.26), condition=%wide.while_cond, body=%wide.while_body.sunk | while | flops 2 | bytes 131189 | solution.py:142
  96.7 0.6 fusion.13
  97.3 1.4 %bitcast_dynamic-update-slice_fusion.2 = f32[2,128,128]{2,1,0:T(8,128)S(1)} fusion(f32[2,128,128]{2,1,0:T(8,128)S(1)} %get-tuple-element.72, s32[]{:T(128)S(6)} %copy.11, f32[256,256]{1,0:T(8,128)S(1)} %get-tuple-element.75, s32[]{:T(128)} %bitcast.30, s32[]{:T(128)} %bitcast.31), kind=kLoop, calls=%fused_computation.clone.1 | loop fusion | bytes 131084 | tf_op jit(solution)/shard_map/jit(_solve_triangular)/triangular_solve
  98.7 0.6 fusion.13
  99.3 1.4 %bitcast_dynamic-update-slice_fusion.2 = f32[2,128,128]{2,1,0:T(8,128)S(1)} fusion(f32[2,128,128]{2,1,0:T(8,128)S(1)} %get-tuple-element.72, s32[]{:T(128)S(6)} %copy.11, f32[256,256]{1,0:T(8,128)S(1)} %get-tuple-element.75, s32[]{:T(128)} %bitcast.30, s32[]{:T(128)} %bitcast.31), kind=kLoop, calls=%fused_computation.clone.1 | loop fusion | bytes 131084 | tf_op jit(solution)/shard_map/jit(_solve_triangular)/triangular_solve
  100.7 19.9 %custom-call.16 = f32[2,128,128]{1,2,0:T(8,128)S(1)} custom-call(f32[2,128,128]{2,1,0:T(8,128)S(1)} %get-tuple-element.14), custom_call_target="InvertDiagBlocksLowerTriangular" | custom-call | tf_op jit(solution)/shard_map/jit(_solve_triangular)/triangular_solve | solution.py:142
  120.6 0.3 fusion
  120.9 0.3 convolution_subtract_fusion
  121.2 0.3 fusion.3
  121.5 0.7 pad_maximum_fusion.inverse_ref
  122.2 7.7 %shard_map.59 = (f32[384,256]{1,0:T(8,128)}, f32[256,256]{1,0:T(8,128)}, f32[384,1024]{1,0:T(8,128)}) custom-call(s32[1]{0:T(128)} %bitcast.core_ref, s32[1]{0:T(128)} %bitcast.1.sub_ref, s32[1]{0:T(128)S(6)} %copy.17.live_ref, f32[1,1]{1,0:T(1,128)} %slice.83.total_ref, f32[256,256]{1,0:T(8,128)} %pad_maximum_fusion.inverse_ref, f32[128,1280]{1,0:T(8,128)} %bitcast.34, ...), custom_call_target="tpu_custom_call" | custom-call | tf_op jit(solution)/shard_map/pallas_call | solution.py:99
  (20 shorter events, 0.6 us)
Async XLA Ops:
  6.2 2.4 %collective-permute-start = (f32[128,1280]{1,0:T(8,128)}, f32[128,1280]{1,0:T(8,128)S(1)}, u32[]{:S(2)}, u32[]{:S(2)}) collective-permute-start(f32[128,1280]{1,0:T(8,128)} %get-tuple-element.6), channel_id=1, source_target_pairs={{0,1},{1,0},{2,3},{3,2},{4,5},{5,4},{6,7},{7,6},{8,9},{9,8},{10,11... | collective-permute-start | bytes 1966088 | tf_op jit(solution)/shard_map/ppermute | solution.py:114
  58.1 38.6 %copy-start = (f32[16,8,1280]{2,1,0:T(8,128)}, f32[16,8,1280]{2,1,0:T(8,128)S(1)}, u32[]{:S(2)}) copy-start(f32[16,8,1280]{2,1,0:T(8,128)S(1)} %all_to_all.11) | copy-start | bytes 1966084
  58.1 2.1 %collective-permute-start.1 = (f32[128,1280]{1,0:T(8,128)S(1)}, f32[128,1280]{1,0:T(8,128)S(1)}, u32[]{:S(2)}, u32[]{:S(2)}) collective-permute-start(f32[128,1280]{1,0:T(8,128)S(1)} %bitcast.32), channel_id=1, source_target_pairs={{0,1},{1,0},{2,3},{3,2},{4,5},{5,4},{6,7},{7,6},{8,9},{9,8},{10,11... | collective-permute-start | bytes 1966088 | tf_op jit(solution)/shard_map/ppermute | solution.py:114
  60.2 36.5 %copy-start.1 = (f32[128,1280]{1,0:T(8,128)}, f32[128,1280]{1,0:T(8,128)S(1)}, u32[]{:S(2)}) copy-start(f32[128,1280]{1,0:T(8,128)S(1)} %collective-permute-done.1.other_ref) | copy-start | bytes 1966084

commit v2 on v0

v2 whole, which is shorter than its diff:
```python
import functools

import jax
import jax.numpy as jnp
from jax import lax
from jax.experimental import pallas as pl
from jax.experimental.pallas import tpu as pltpu
from jax.sharding import Mesh
from jax.sharding import PartitionSpec as P

AXES = ("far", "z", "y", "x", "core")
SLOTS = 4
PARTS = 4
HIGHEST = lax.Precision.HIGHEST
F32 = jnp.float32
BF16 = jnp.bfloat16
LANES = 128
BLOCK = 32
BATCH = 16
SMEM = pl.BlockSpec(memory_space=pltpu.SMEM)
VMEM = pl.BlockSpec(memory_space=pltpu.VMEM)
ANY = pl.BlockSpec(memory_space=pl.ANY)


def dot(left, right, contract):
    return lax.dot_general(
        left, right, (contract, ((), ())), precision=HIGHEST, preferred_element_type=F32
    )


def masked(ref, live_ref, columns=slice(None)):
    rows = ref.shape[0]
    live = lax.broadcasted_iota(jnp.int32, (rows, 1), 0) < live_ref[0]
    return jnp.where(live, ref[:, columns], 0.0)


def struct(*shape):
    return jax.ShapeDtypeStruct(shape, F32)


def cost(flops, transferred):
    return pl.CostEstimate(flops=flops, bytes_accessed=transferred, transcendentals=0)


def products_kernel(other, place_ref, live_ref, panel_ref, trail_ref, out_ref, cross_scr):
    rows, width = panel_ref.shape
    columns = trail_ref.shape[1]
    core, chip, depth = place_ref[0], place_ref[1], place_ref[2]
    side = 1 - core if other else core
    panel = masked(panel_ref, live_ref)
    tall = width // SLOTS
    part = width // PARTS
    half = masked(panel_ref, live_ref, pl.ds(pl.multiple_of(side * LANES, LANES), LANES))
    start = pl.multiple_of(side * (columns // 2), LANES)
    trail = masked(trail_ref, live_ref, pl.ds(start, columns // 2))
    product = dot(panel, jnp.concatenate([half, trail], axis=1), ((0,), (0,)))
    for tile in range(SLOTS + 1):
        cross_scr[tile] = product[:, tile * LANES : (tile + 1) * LANES]

    @pl.when(side == 0)
    def _():
        count = jnp.full((width - LANES, LANES), live_ref[0], jnp.int32)
        cross_scr[0, LANES:, :] = count.astype(F32)

    for slot in range(SLOTS):
        chunk = jnp.bitwise_xor(chip, slot)
        out_ref[slot, :tall, :] = cross_scr[0, pl.ds(pl.multiple_of(chunk * tall, 8), tall), :]
        for piece in range(PARTS):
            at = pl.multiple_of(jnp.bitwise_xor(depth, piece) * part, 8)
            to = tall + piece * part
            out_ref[slot, to : to + part, :] = cross_scr[chunk + 1, pl.ds(at, part), :]


def products_of(other, place, live, panel, trail):
    rows, width = panel.shape
    columns = trail.shape[1]
    return pl.pallas_call(
        functools.partial(products_kernel, other),
        out_shape=struct(SLOTS, width // SLOTS + width, LANES),
        in_specs=[SMEM, SMEM, VMEM, VMEM],
        out_specs=VMEM,
        scratch_shapes=[pltpu.VMEM((SLOTS + 1, width, LANES), F32)],
        cost_estimate=cost(12 * rows * width * (columns + width) // 2, 2 * rows * columns),
        name="products_other" if other else "products_own",
    )(place, live, panel, trail)


def parts_of(x):
    high = x.astype(BF16)
    rest = x - high.astype(F32)
    middle = rest.astype(BF16)
    return high, middle, (rest - middle.astype(F32)).astype(BF16)


def update_product(left, right):
    a, b, c = parts_of(left)
    d, e, f = parts_of(right)
    return lax.dot_general(
        jnp.concatenate([a, a, b, a, c, b], axis=0),
        jnp.concatenate([d, e, d, f, d, e], axis=0),
        (((0,), (0,)), ((), ())),
        preferred_element_type=F32,
    )


def across(x, lane):
    return jnp.broadcast_to(x[:, lane : lane + 1], (8, LANES))


def down(x, row):
    return jnp.broadcast_to(x[row : row + 1, :], (8, LANES))


def eliminate(rows, first):
    groups = len(rows)
    index = lax.broadcasted_iota(jnp.int32, (8, LANES), 0)
    pivots = [jnp.ones((8, LANES), F32) for _ in range(groups)]
    for start in range(0, BLOCK, BATCH):
        columns = {
            (group, j): across(rows[group][0], first + j)
            for j in range(start, start + BATCH)
            for group in range(j // 8, groups)
        }
        for j in range(start, start + BATCH):
            home, place = divmod(j, 8)
            pivot = down(columns[home, j], place)
            pivots[home] = jnp.where(index == place, pivot, pivots[home])
            inverse = 1.0 / pivot
            factors = {}
            for group in range(home, groups):
                column = columns[group, j]
                if group == home:
                    if place == 7:
                        continue
                    column = jnp.where(index > place, column, 0.0)
                factors[group] = column * inverse
            for m in range(j + 1, start + BATCH):
                value = down(columns[m // 8, j], m % 8)
                for group in range(m // 8, groups):
                    if group in factors:
                        columns[group, m] = columns[group, m] - factors[group] * value
            for tile in range(len(rows[0])):
                value = down(rows[home][tile], place)
                for group in factors:
                    rows[group][tile] = rows[group][tile] - factors[group] * value
    return pivots


def factor_inverse(gram_ref, inverse_ref):
    size = gram_ref.shape[0]
    row = lax.broadcasted_iota(jnp.int32, (size, size), 0)
    column = lax.broadcasted_iota(jnp.int32, (size, size), 1)
    inverse_ref[...] = jnp.where(row == column, 1.0, 0.0)
    tiles = size // LANES
    groups = BLOCK // 8

    def tile_of(index):
        return slice(index * LANES, (index + 1) * LANES)

    for start in range(0, size, BLOCK):
        stop = start + BLOCK
        here = start // LANES
        rows = []
        for group in range(groups):
            at = slice(start + 8 * group, start + 8 * group + 8)
            rows.append(
                [gram_ref[at, tile_of(t)] for t in range(here, tiles)]
                + [inverse_ref[at, tile_of(t)] for t in range(here + 1)]
            )
        pivots = eliminate(rows, start % LANES)
        for group in range(groups):
            scale = lax.rsqrt(pivots[group])
            rows[group] = [value * scale for value in rows[group]]
            at = slice(start + 8 * group, start + 8 * group + 8)
            for t in range(here + 1):
                inverse_ref[at, tile_of(t)] = rows[group][tiles - here + t]
        if stop == size:
            break
        base = stop // LANES
        stacked = [
            jnp.concatenate([rows[group][i] for group in range(groups)], axis=0)
            for i in range(base - here, len(rows[0]))
        ]
        left = jnp.concatenate(stacked[: tiles - base], axis=1)
        product = update_product(left, jnp.concatenate(stacked, axis=1))[stop - base * LANES :]
        for i, t in enumerate(range(base, tiles)):
            gram_ref[stop:, tile_of(t)] -= product[:, tile_of(i)]
        for t in range(here + 1):
            inverse_ref[stop:, tile_of(t)] -= product[:, tile_of(tiles - base + t)]


def factor_kernel(
    place_ref, live_ref, own_ref, other_ref, panel_ref, inverse_ref, unit_ref, basis_ref, gram_ref
):
    core, chip = place_ref[0], place_ref[1]
    tall = own_ref.shape[1]
    for side, ref in ((core, own_ref), (1 - core, other_ref)):
        at = pl.ds(pl.multiple_of(side * LANES, LANES), LANES)
        for slot in range(SLOTS):
            row = pl.multiple_of(jnp.bitwise_xor(chip, slot) * tall, 8)
            gram_ref[pl.ds(row, tall), at] = ref[slot]
    root = jnp.sqrt(gram_ref[LANES : LANES + 8, 0:LANES])[0:1, 0:1]
    factor_inverse(gram_ref, inverse_ref)
    unit = dot(masked(panel_ref, live_ref), inverse_ref[...], ((1,), (1,)))
    unit_ref[...] = unit
    basis_ref[...] = unit * root


def factor_of(place, live, own, other, panel):
    rows, width = panel.shape
    return pl.pallas_call(
        factor_kernel,
        out_shape=(struct(width, width), struct(rows, width), struct(rows, width)),
        in_specs=[SMEM, SMEM, VMEM, VMEM, VMEM],
        out_specs=(VMEM,) * 3,
        scratch_shapes=[pltpu.VMEM((width, width), F32)],
        cost_estimate=cost(6 * 10**9, 4 * rows * width),
        name="factor",
    )(place, live, own, other, panel)


def rest_kernel(other, place_ref, live_ref, inverse_ref, unit_ref, cross_ref, trail_ref, *refs):
    width = inverse_ref.shape[0]
    half = trail_ref.shape[1] // 2
    core, chip, depth = place_ref[0], place_ref[1], place_ref[2]
    if other:
        top_before_ref, _, top_ref, rest_ref, top_scr, cross_scr, rest_scr, sem = refs
        side = 1 - core
    else:
        top_ref, rest_ref, top_scr, cross_scr, rest_scr, sem = refs
        side = core
    start = pl.multiple_of(side * half, half)
    part = width // PARTS
    for slot in range(SLOTS):
        lane = pl.multiple_of(jnp.bitwise_xor(chip, slot) * LANES, LANES)
        for piece in range(PARTS):
            row = pl.multiple_of(jnp.bitwise_xor(depth, piece) * part, 8)
            cross_scr[pl.ds(row, part), pl.ds(lane, LANES)] = cross_ref[
                slot, piece * part : (piece + 1) * part, :
            ]
    top = dot(inverse_ref[...], cross_scr[...], ((1,), (0,)))
    rest_scr[...] = masked(trail_ref, live_ref, pl.ds(start, half)) - dot(
        unit_ref[...], top, ((1,), (0,))
    )
    copy = pltpu.make_async_copy(rest_scr, rest_ref.at[:, pl.ds(start, half)], sem)
    copy.start()
    top_scr[...] = top
    wide = top_ref.shape[1]
    mine = top_scr[:, pl.ds(pl.multiple_of(place_ref[4], LANES), wide)]
    if other:
        top_ref[...] = jnp.where(place_ref[3] == side, mine, top_before_ref[...])
    else:
        top_ref[...] = mine
    copy.wait()


def rest_of(other, place, live, inverse, unit, cross, trail, wide, before):
    rows, width = unit.shape
    columns = trail.shape[1]
    half = columns // 2
    return pl.pallas_call(
        functools.partial(rest_kernel, other),
        out_shape=(struct(width, wide), struct(rows, columns)),
        in_specs=[SMEM] * 2 + [VMEM] * 4 + ([VMEM, ANY] if other else []),
        out_specs=(VMEM, ANY),
        scratch_shapes=[
            pltpu.VMEM((width, half), F32),
            pltpu.VMEM((width, half), F32),
            pltpu.VMEM((rows, half), F32),
            pltpu.SemaphoreType.DMA,
        ],
        input_output_aliases={7: 1} if other else {},
        cost_estimate=cost(12 * (rows + width) * width * half, 8 * rows * half),
        name="rest_other" if other else "rest_own",
    )(place, live, inverse, unit, cross, trail, *before)


def swap(x):
    return lax.ppermute(x, "core", [(0, 1), (1, 0)])


def send(x, axes, size, shift):
    return lax.ppermute(x, axes, [(i, i ^ shift) for i in range(size)])


def tree(parts):
    return (parts[0] + parts[1]) + (parts[2] + parts[3])


def body(panel, trailing, live_rows):
    width, columns = panel.shape[1], trailing.shape[1]
    flat, deep = ("y", "x"), "z"
    core = lax.axis_index("core")
    wide = columns // (lax.axis_size("x") * 2)
    begin = (lax.axis_index("x") * 2 + core) * wide
    side = begin // (columns // 2)
    place = jnp.stack(
        [
            core,
            lax.axis_index(flat),
            lax.axis_index(deep),
            side,
            begin - side * (columns // 2),
        ]
    )
    tall, part = width // SLOTS, width // PARTS

    theirs = products_of(True, place, live_rows, panel, trailing)
    ours = products_of(False, place, live_rows, panel, trailing)
    pair = ours + swap(theirs)
    slots = [pair[0]] + [send(pair[k], flat, SLOTS, k) for k in range(1, SLOTS)]
    summed = tree(slots)
    gram = summed[:tall]
    pieces = [
        jnp.concatenate([gram, summed[tall + j * part : tall + (j + 1) * part]])
        for j in range(PARTS)
    ]
    pieces = [pieces[0]] + [send(pieces[j], deep, PARTS, j) for j in range(1, PARTS)]
    summed = tree(pieces)
    if lax.axis_size("far") > 1:
        summed = lax.psum(summed, "far")
    gram, cross = summed[:tall], summed[tall:]
    gram_own = jnp.stack([gram] + [send(gram, flat, SLOTS, k) for k in range(1, SLOTS)])
    cross = jnp.concatenate([cross] + [send(cross, deep, PARTS, j) for j in range(1, PARTS)])
    cross_own = [cross] + [send(cross, flat, SLOTS, k) for k in range(1, SLOTS)]
    inverse, unit, basis = factor_of(place, live_rows, gram_own, swap(gram_own), panel)
    *cross_own, inverse = lax.optimization_barrier((*cross_own, inverse))
    cross_own = jnp.stack(cross_own)
    cross_other = swap(cross_own)
    args = (place, live_rows, inverse, unit)
    before = rest_of(False, *args, cross_own, trailing, wide, ())
    top, rest = rest_of(True, *args, cross_other, trailing, wide, before)
    return basis, top, rest


def solution(mesh):
    rows, subs = mesh.shape["rows"], mesh.shape["sub"]
    grid = Mesh(mesh.devices.reshape(rows // (2 * PARTS), PARTS, 2, subs // 2, 2), AXES)
    in_specs = (P(AXES, None), P(AXES, None), P(AXES))
    out_specs = (P(AXES, None), P(None, ("x", "core")), P(AXES, None))
    return jax.shard_map(
        body, mesh=grid, in_specs=in_specs, out_specs=out_specs, check_vma=False
    )
```

time: 351 us -> 68.7 us (0.20)
  waiting for transfers between devices: 215 us -> 16 us
  other arithmetic: 59.9 us -> 1.28 us
  blocking collectives: 42.2 us -> 0 us
  Pallas kernels: 0 us -> 26.1 us
  starting transfers between devices: 0.08 us -> 20.7 us
  between operations: 16.9 us -> 1.6 us
  matrix products: 8.9 us -> 0 us
  local copies, waits for them, and re-layouts: 6.69 us -> 2.81 us
    psum x2 -> x0, waiting for transfers between devices: 215 us -> none  [the longest x1 127 us: body(): top_whole = lax.psum(local_top, ('rows', 'sub')) / root_total]
    another operation x9 -> x2, other arithmetic: 53.8 us -> 0.05 us  [the longest x1 0.04 us: body(): cross_own = jnp.stack(cross_own)]
    psum x1 -> x0, blocking collectives: 42.2 us -> none  [body(): gram, total = lax.psum((gram, live_share), ('rows', 'sub'))]
    pallas_call x0 -> x5, Pallas kernels: none -> 26.1 us  [the longest x2 9.74 us: rest_of(): pl.pallas_call(functools.partial(rest_kernel, other), out_shape=(struct(w...]
    ppermute x0 -> x18, starting transfers between devices: none -> 20.7 us  [the longest x15 20.1 us: send(): return lax.ppermute(x, axes, [(i, i ^ shift) for i in range(size)])]
    ppermute x0 -> x18, waiting for transfers between devices: none -> 16 us  [the longest x15 15.9 us: send(): return lax.ppermute(x, axes, [(i, i ^ shift) for i in range(size)])]
    dot_general x5 -> x0, matrix products: 7.14 us -> none  [the longest x1 2.96 us: body(): jnp.dot(basis.T, masked_trail, precision=lax.Precision.HIGHEST, preferred...]
    div x3 -> x0, other arithmetic: 4.79 us -> none  [the longest x2 3.34 us: body(): factor = jnp.linalg.cholesky(gram / total[0])]
  transfers between devices with their start and end apart: 2 -> 18, of which waited for: 2 -> 7; matrix products, arithmetic and copies ran while one was open for 0% -> 0% of each run, Pallas kernels for 0% -> 25%
where the time goes in v2:
time: 68.7 us; the launch traced here: 68.4 us
  Pallas kernels  26.1 us (38%)
  starting transfers between devices  20.7 us (30%)
  waiting for transfers between devices  16 us (23%)
  local copies, waits for them, and re-layouts  2.81 us (4%)
  between operations  1.6 us (2%)
  other arithmetic  1.28 us (2%)
    ppermute x15, starting transfers between devices, send(): return lax.ppermute(x, axes, [(i, i ^ shift) for i in range(size)])  20.1 us
    ppermute x15, waiting for transfers between devices, send(): return lax.ppermute(x, axes, [(i, i ^ shift) for i in range(size)])  15.9 us
    pallas_call x2, Pallas kernels, rest_of(): pl.pallas_call(functools.partial(rest_kernel, other), out_shape=(struct(w...  9.74 us
    pallas_call x1, Pallas kernels, factor_of(): pl.pallas_call(factor_kernel, out_shape=(struct(width, width), struct(row...  8.54 us
    pallas_call x2, Pallas kernels, products_of(): pl.pallas_call(functools.partial(products_kernel, other), out_shape=struc...  7.79 us
    unnamed x8, local copies, waits for them, and re-layouts  2.19 us
  transfers between devices with their start and end apart: 18, of which 7 were waited for; matrix products, arithmetic and copies ran while one was open for 0% of the time, Pallas kernels for 25%

profile of v2, /device:TPU:0, one launch (start us, length us, event | category | flops | bytes accessed | tf_op | source)
XLA Modules:
  0.0 68.4 jit_solution(9582983306980502256)
XLA Ops:
  1.9 3.8 %products_other.1 = f32[4,320,128]{2,1,0:T(8,128)} custom-call(s32[5]{0:T(128)} %stack.53.place_ref, s32[1]{0:T(128)S(6)} %copy.8.live_ref, f32[384,256]{1,0:T(8,128)} %panel_ref.5, f32[384,1024]{1,0:T(8,128)} %trail_ref.7), custom_call_target="tpu_custom_call" | custom-call | flops 754974720 | bytes 786432 | tf_op jit(solution)/shard_map/products_other/pallas_call | solution.py:77
  6.1 4.0 %products_own.1 = f32[4,320,128]{2,1,0:T(8,128)} custom-call(s32[5]{0:T(128)} %stack.53.place_ref, s32[1]{0:T(128)S(6)} %copy.8.live_ref, f32[384,256]{1,0:T(8,128)} %panel_ref.5, f32[384,1024]{1,0:T(8,128)} %trail_ref.7), custom_call_target="tpu_custom_call" | custom-call | flops 754974720 | bytes 786432 | tf_op jit(solution)/shard_map/products_own/pallas_call | solution.py:77
  10.1 1.2 %add.30 = f32[4,320,128]{2,1,0:T(8,128)S(1)} add(f32[4,320,128]{2,1,0:T(8,128)} %products_own.1, f32[4,320,128]{2,1,0:T(8,128)S(1)} %collective-permute-done) | non-fusion elementwise | flops 163840 | bytes 1966080 | tf_op jit(solution)/shard_map/add | solution.py:310
  11.3 3.5 %collective-permute-start.3 = (f32[320,128]{1,0:T(8,128)S(1)}, f32[320,128]{1,0:T(8,128)S(1)}, u32[]{:S(2)}, u32[]{:S(2)}) collective-permute-start(f32[320,128]{1,0:T(8,128)S(1)} %get-tuple-element.27), channel_id=1, source_target_pairs={{0,6},{2,4},{4,2},{6,0},{1,7},{3,5},{5,3},{7,1},{8,14},{10,12},{12... | collective-permute-start | bytes 491528 | tf_op jit(solution)/shard_map/ppermute | solution.py:283
  15.5 4.5 %collective-permute-done.3 = f32[320,128]{1,0:T(8,128)S(1)} collective-permute-done((f32[320,128]{1,0:T(8,128)S(1)}, f32[320,128]{1,0:T(8,128)S(1)}, u32[]{:S(2)}, u32[]{:S(2)}) %collective-permute-start.3) | collective-permute-done | bytes 163872 | tf_op jit(solution)/shard_map/ppermute | solution.py:283
  19.9 3.3 %collective-permute-done.2 = f32[320,128]{1,0:T(8,128)S(1)} collective-permute-done((f32[320,128]{1,0:T(8,128)S(1)}, f32[320,128]{1,0:T(8,128)S(1)}, u32[]{:S(2)}, u32[]{:S(2)}) %collective-permute-start.2) | collective-permute-done | bytes 163872 | tf_op jit(solution)/shard_map/ppermute | solution.py:283
  23.6 3.7 %collective-permute-start.6 = (f32[128,128]{1,0:T(8,128)S(1)}, f32[128,128]{1,0:T(8,128)S(1)}, u32[]{:S(2)}, u32[]{:S(2)}) collective-permute-start(f32[128,128]{1,0:T(8,128)S(1)} %get-tuple-element.37), channel_id=1, source_target_pairs={{0,24},{8,16},{16,8},{24,0},{1,25},{9,17},{17,9},{25,1},{2,26},{10... | collective-permute-start | bytes 196616 | tf_op jit(solution)/shard_map/ppermute | solution.py:283
  27.3 0.8 %collective-permute-start.4 = (f32[128,128]{1,0:T(8,128)S(1)}, f32[128,128]{1,0:T(8,128)S(1)}, u32[]{:S(2)}, u32[]{:S(2)}) collective-permute-start(f32[128,128]{1,0:T(8,128)S(1)} %get-tuple-element.39), channel_id=1, source_target_pairs={{0,8},{8,0},{16,24},{24,16},{1,9},{9,1},{17,25},{25,17},{2,10},{10... | collective-permute-start | bytes 196616 | tf_op jit(solution)/shard_map/ppermute | solution.py:283
  28.0 2.1 %collective-permute-done.6 = f32[128,128]{1,0:T(8,128)S(1)} collective-permute-done((f32[128,128]{1,0:T(8,128)S(1)}, f32[128,128]{1,0:T(8,128)S(1)}, u32[]{:S(2)}, u32[]{:S(2)}) %collective-permute-start.6) | collective-permute-done | bytes 65568 | tf_op jit(solution)/shard_map/ppermute | solution.py:283
  30.2 2.8 %collective-permute-done.5 = f32[128,128]{1,0:T(8,128)S(1)} collective-permute-done((f32[128,128]{1,0:T(8,128)S(1)}, f32[128,128]{1,0:T(8,128)S(1)}, u32[]{:S(2)}, u32[]{:S(2)}) %collective-permute-start.5) | collective-permute-done | bytes 65568 | tf_op jit(solution)/shard_map/ppermute | solution.py:283
  33.0 1.6 %collective-permute-start.8 = (f32[64,128]{1,0:T(8,128)S(1)}, f32[64,128]{1,0:T(8,128)S(1)}, u32[]{:S(2)}, u32[]{:S(2)}) collective-permute-start(f32[64,128]{1,0:T(8,128)S(1)} %get-tuple-element.36), channel_id=1, source_target_pairs={{0,4},{2,6},{4,0},{6,2},{1,5},{3,7},{5,1},{7,3},{8,12},{10,14},{12... | collective-permute-start | bytes 98312 | tf_op jit(solution)/shard_map/ppermute | solution.py:283
  35.0 1.6 %collective-permute-start.9 = (f32[64,128]{1,0:T(8,128)S(1)}, f32[64,128]{1,0:T(8,128)S(1)}, u32[]{:S(2)}, u32[]{:S(2)}) collective-permute-start(f32[64,128]{1,0:T(8,128)S(1)} %get-tuple-element.36), channel_id=1, source_target_pairs={{0,6},{2,4},{4,2},{6,0},{1,7},{3,5},{5,3},{7,1},{8,14},{10,12},{12... | collective-permute-start | bytes 98312 | tf_op jit(solution)/shard_map/ppermute | solution.py:283
  36.6 2.6 %collective-permute-start.13 = (f32[64,128]{1,0:T(8,128)S(1)}, f32[64,128]{1,0:T(8,128)S(1)}, u32[]{:S(2)}, u32[]{:S(2)}) collective-permute-start(f32[64,128]{1,0:T(8,128)S(1)} %get-tuple-element.34), channel_id=1, source_target_pairs={{0,24},{8,16},{16,8},{24,0},{1,25},{9,17},{17,9},{25,1},{2,26},{10... | collective-permute-start | bytes 98312 | tf_op jit(solution)/shard_map/ppermute | solution.py:283
  39.2 1.7 %collective-permute-start.11 = (f32[64,128]{1,0:T(8,128)S(1)}, f32[64,128]{1,0:T(8,128)S(1)}, u32[]{:S(2)}, u32[]{:S(2)}) collective-permute-start(f32[64,128]{1,0:T(8,128)S(1)} %get-tuple-element.34), channel_id=1, source_target_pairs={{0,8},{8,0},{16,24},{24,16},{1,9},{9,1},{17,25},{25,17},{2,10},{10... | collective-permute-start | bytes 98312 | tf_op jit(solution)/shard_map/ppermute | solution.py:283
  41.1 1.4 %collective-permute-done.13 = f32[64,128]{1,0:T(8,128)S(1)} collective-permute-done((f32[64,128]{1,0:T(8,128)S(1)}, f32[64,128]{1,0:T(8,128)S(1)}, u32[]{:S(2)}, u32[]{:S(2)}) %collective-permute-start.13) | collective-permute-done | bytes 32800 | tf_op jit(solution)/shard_map/ppermute | solution.py:283
  42.5 1.5 %collective-permute-done.12 = f32[64,128]{1,0:T(8,128)S(1)} collective-permute-done((f32[64,128]{1,0:T(8,128)S(1)}, f32[64,128]{1,0:T(8,128)S(1)}, u32[]{:S(2)}, u32[]{:S(2)}) %collective-permute-start.12) | collective-permute-done | bytes 32800 | tf_op jit(solution)/shard_map/ppermute | solution.py:283
  44.0 1.3 %collective-permute-start.16 = (f32[256,128]{1,0:T(8,128)S(1)}, f32[256,128]{1,0:T(8,128)S(1)}, u32[]{:S(2)}, u32[]{:S(2)}) collective-permute-start(f32[256,128]{1,0:T(8,128)S(1)} %pad_maximum_fusion.2), channel_id=1, source_target_pairs={{0,6},{2,4},{4,2},{6,0},{1,7},{3,5},{5,3},{7,1},{8,14},{10,12},{12... | collective-permute-start | bytes 393224 | tf_op jit(solution)/shard_map/ppermute | solution.py:283
  45.4 1.7 %collective-permute-start.15 = (f32[256,128]{1,0:T(8,128)S(1)}, f32[256,128]{1,0:T(8,128)S(1)}, u32[]{:S(2)}, u32[]{:S(2)}) collective-permute-start(f32[256,128]{1,0:T(8,128)S(1)} %pad_maximum_fusion.2), channel_id=1, source_target_pairs={{0,4},{2,6},{4,0},{6,2},{1,5},{3,7},{5,1},{7,3},{8,12},{10,14},{12... | collective-permute-start | bytes 393224 | tf_op jit(solution)/shard_map/ppermute | solution.py:283
  47.6 0.7 copy-done.3
  48.3 8.5 %factor.1 = (f32[256,256]{1,0:T(8,128)}, f32[384,256]{1,0:T(8,128)}, f32[384,256]{1,0:T(8,128)}) custom-call(s32[5]{0:T(128)} %stack.53.place_ref, s32[1]{0:T(128)S(6)} %copy.8.live_ref, f32[4,64,128]{2,1,0:T(8,128)} %copy-done.2, f32[4,64,128]{2,1,0:T(8,128)} %copy-done.3, f32[384,256]{1,0:T(8,128)} %panel_ref.5), custom_call_target="tpu_custom_call" | custom-call | flops 6000000000 | bytes 393216 | tf_op jit(solution)/shard_map/factor/pallas_call | solution.py:211
  57.0 0.7 %copy-done.1 = f32[4,256,128]{2,1,0:T(8,128)} copy-done((f32[4,256,128]{2,1,0:T(8,128)}, f32[4,256,128]{2,1,0:T(8,128)S(1)}, u32[]{:S(2)}) %copy-start.1) | copy-done | bytes 524312
  57.7 4.9 %rest_own.1 = (f32[256,256]{1,0:T(8,128)}, f32[384,1024]{1,0:T(8,128)}) custom-call(s32[5]{0:T(128)} %stack.53.place_ref, s32[1]{0:T(128)S(6)} %copy.8.live_ref, f32[256,256]{1,0:T(8,128)} %get-tuple-element.17.inverse_ref, f32[384,256]{1,0:T(8,128)} %get-tuple-element.18.unit_ref, f32[4,256,128]{2,1,0:T(8,128)} %copy-done.1, f32[384,1024]{1,0:T(8,128)} %trail_ref.7), custom_call_target="tpu_custom_call" | custom-call | flops 1006632960 | bytes 1572864 | tf_op jit(solution)/shard_map/rest_own/pallas_call | solution.py:261
  62.6 0.8 %copy-done = f32[4,256,128]{2,1,0:T(8,128)} copy-done((f32[4,256,128]{2,1,0:T(8,128)}, f32[4,256,128]{2,1,0:T(8,128)S(1)}, u32[]{:S(2)}) %copy-start) | copy-done | bytes 524312
  63.4 4.9 %rest_other.1 = (f32[256,256]{1,0:T(8,128)}, f32[384,1024]{1,0:T(8,128)}) custom-call(s32[5]{0:T(128)} %stack.53.place_ref, s32[1]{0:T(128)S(6)} %copy.8.live_ref, f32[256,256]{1,0:T(8,128)} %get-tuple-element.17.inverse_ref, f32[384,256]{1,0:T(8,128)} %get-tuple-element.18.unit_ref, f32[4,256,128]{2,1,0:T(8,128)} %copy-done, ...), custom_call_target="tpu_custom_call", output_to_operand_aliasing={{1}: (7, {})} | custom-call | flops 1006632960 | bytes 1572864 | tf_op jit(solution)/shard_map/rest_other/pallas_call | solution.py:261
  (36 shorter events, 3.3 us)
Async XLA Ops:
  5.7 4.4 %collective-permute-start = (f32[4,320,128]{2,1,0:T(8,128)}, f32[4,320,128]{2,1,0:T(8,128)S(1)}, u32[]{:S(2)}, u32[]{:S(2)}) collective-permute-start(f32[4,320,128]{2,1,0:T(8,128)} %products_other.1), channel_id=1, source_target_pairs={{0,1},{1,0},{2,3},{3,2},{4,5},{5,4},{6,7},{7,6},{8,9},{9,8},{10,11... | collective-permute-start | bytes 1966088 | tf_op jit(solution)/shard_map/ppermute | solution.py:279
  11.3 8.6 %collective-permute-start.3 = (f32[320,128]{1,0:T(8,128)S(1)}, f32[320,128]{1,0:T(8,128)S(1)}, u32[]{:S(2)}, u32[]{:S(2)}) collective-permute-start(f32[320,128]{1,0:T(8,128)S(1)} %get-tuple-element.27), channel_id=1, source_target_pairs={{0,6},{2,4},{4,2},{6,0},{1,7},{3,5},{5,3},{7,1},{8,14},{10,12},{12... | collective-permute-start | bytes 491528 | tf_op jit(solution)/shard_map/ppermute | solution.py:283
  14.8 8.4 %collective-permute-start.2 = (f32[320,128]{1,0:T(8,128)S(1)}, f32[320,128]{1,0:T(8,128)S(1)}, u32[]{:S(2)}, u32[]{:S(2)}) collective-permute-start(f32[320,128]{1,0:T(8,128)S(1)} %get-tuple-element.28), channel_id=1, source_target_pairs={{0,4},{2,6},{4,0},{6,2},{1,5},{3,7},{5,1},{7,3},{8,12},{10,14},{12... | collective-permute-start | bytes 491528 | tf_op jit(solution)/shard_map/ppermute | solution.py:283
  15.3 8.2 %collective-permute-start.1 = (f32[320,128]{1,0:T(8,128)S(1)}, f32[320,128]{1,0:T(8,128)S(1)}, u32[]{:S(2)}, u32[]{:S(2)}) collective-permute-start(f32[320,128]{1,0:T(8,128)S(1)} %get-tuple-element.29), channel_id=1, source_target_pairs={{0,2},{2,0},{4,6},{6,4},{1,3},{3,1},{5,7},{7,5},{8,10},{10,8},{12,... | collective-permute-start | bytes 491528 | tf_op jit(solution)/shard_map/ppermute | solution.py:283
  23.6 6.6 %collective-permute-start.6 = (f32[128,128]{1,0:T(8,128)S(1)}, f32[128,128]{1,0:T(8,128)S(1)}, u32[]{:S(2)}, u32[]{:S(2)}) collective-permute-start(f32[128,128]{1,0:T(8,128)S(1)} %get-tuple-element.37), channel_id=1, source_target_pairs={{0,24},{8,16},{16,8},{24,0},{1,25},{9,17},{17,9},{25,1},{2,26},{10... | collective-permute-start | bytes 196616 | tf_op jit(solution)/shard_map/ppermute | solution.py:283
  27.3 5.7 %collective-permute-start.5 = (f32[128,128]{1,0:T(8,128)S(1)}, f32[128,128]{1,0:T(8,128)S(1)}, u32[]{:S(2)}, u32[]{:S(2)}) collective-permute-start(f32[128,128]{1,0:T(8,128)S(1)} %get-tuple-element.38), channel_id=1, source_target_pairs={{0,16},{8,24},{16,0},{24,8},{1,17},{9,25},{17,1},{25,9},{2,18},{10... | collective-permute-start | bytes 196616 | tf_op jit(solution)/shard_map/ppermute | solution.py:283
  27.3 5.7 %collective-permute-start.4 = (f32[128,128]{1,0:T(8,128)S(1)}, f32[128,128]{1,0:T(8,128)S(1)}, u32[]{:S(2)}, u32[]{:S(2)}) collective-permute-start(f32[128,128]{1,0:T(8,128)S(1)} %get-tuple-element.39), channel_id=1, source_target_pairs={{0,8},{8,0},{16,24},{24,16},{1,9},{9,1},{17,25},{25,17},{2,10},{10... | collective-permute-start | bytes 196616 | tf_op jit(solution)/shard_map/ppermute | solution.py:283
  33.0 6.2 %collective-permute-start.8 = (f32[64,128]{1,0:T(8,128)S(1)}, f32[64,128]{1,0:T(8,128)S(1)}, u32[]{:S(2)}, u32[]{:S(2)}) collective-permute-start(f32[64,128]{1,0:T(8,128)S(1)} %get-tuple-element.36), channel_id=1, source_target_pairs={{0,4},{2,6},{4,0},{6,2},{1,5},{3,7},{5,1},{7,3},{8,12},{10,14},{12... | collective-permute-start | bytes 98312 | tf_op jit(solution)/shard_map/ppermute | solution.py:283
  34.6 6.4 %collective-permute-start.7 = (f32[64,128]{1,0:T(8,128)S(1)}, f32[64,128]{1,0:T(8,128)S(1)}, u32[]{:S(2)}, u32[]{:S(2)}) collective-permute-start(f32[64,128]{1,0:T(8,128)S(1)} %get-tuple-element.36), channel_id=1, source_target_pairs={{0,2},{2,0},{4,6},{6,4},{1,3},{3,1},{5,7},{7,5},{8,10},{10,8},{12,... | collective-permute-start | bytes 98312 | tf_op jit(solution)/shard_map/ppermute | solution.py:283
  35.0 6.0 %collective-permute-start.9 = (f32[64,128]{1,0:T(8,128)S(1)}, f32[64,128]{1,0:T(8,128)S(1)}, u32[]{:S(2)}, u32[]{:S(2)}) collective-permute-start(f32[64,128]{1,0:T(8,128)S(1)} %get-tuple-element.36), channel_id=1, source_target_pairs={{0,6},{2,4},{4,2},{6,0},{1,7},{3,5},{5,3},{7,1},{8,14},{10,12},{12... | collective-permute-start | bytes 98312 | tf_op jit(solution)/shard_map/ppermute | solution.py:283
  36.6 5.9 %collective-permute-start.13 = (f32[64,128]{1,0:T(8,128)S(1)}, f32[64,128]{1,0:T(8,128)S(1)}, u32[]{:S(2)}, u32[]{:S(2)}) collective-permute-start(f32[64,128]{1,0:T(8,128)S(1)} %get-tuple-element.34), channel_id=1, source_target_pairs={{0,24},{8,16},{16,8},{24,0},{1,25},{9,17},{17,9},{25,1},{2,26},{10... | collective-permute-start | bytes 98312 | tf_op jit(solution)/shard_map/ppermute | solution.py:283
  39.2 4.8 %collective-permute-start.12 = (f32[64,128]{1,0:T(8,128)S(1)}, f32[64,128]{1,0:T(8,128)S(1)}, u32[]{:S(2)}, u32[]{:S(2)}) collective-permute-start(f32[64,128]{1,0:T(8,128)S(1)} %get-tuple-element.34), channel_id=1, source_target_pairs={{0,16},{8,24},{16,0},{24,8},{1,17},{9,25},{17,1},{25,9},{2,18},{10... | collective-permute-start | bytes 98312 | tf_op jit(solution)/shard_map/ppermute | solution.py:283
  39.2 4.8 %collective-permute-start.11 = (f32[64,128]{1,0:T(8,128)S(1)}, f32[64,128]{1,0:T(8,128)S(1)}, u32[]{:S(2)}, u32[]{:S(2)}) collective-permute-start(f32[64,128]{1,0:T(8,128)S(1)} %get-tuple-element.34), channel_id=1, source_target_pairs={{0,8},{8,0},{16,24},{24,16},{1,9},{9,1},{17,25},{25,17},{2,10},{10... | collective-permute-start | bytes 98312 | tf_op jit(solution)/shard_map/ppermute | solution.py:283
  41.0 6.6 %copy-start.2 = (f32[4,64,128]{2,1,0:T(8,128)}, f32[4,64,128]{2,1,0:T(8,128)S(1)}, u32[]{:S(2)}) copy-start(f32[4,64,128]{2,1,0:T(8,128)S(1)} %pad_maximum_fusion.1.own_ref) | copy-start | bytes 393220
  41.0 6.6 %collective-permute-start.10 = (f32[4,64,128]{2,1,0:T(8,128)S(1)}, f32[4,64,128]{2,1,0:T(8,128)S(1)}, u32[]{:S(2)}, u32[]{:S(2)}) collective-permute-start(f32[4,64,128]{2,1,0:T(8,128)S(1)} %pad_maximum_fusion.1.own_ref), channel_id=1, source_target_pairs={{0,1},{1,0},{2,3},{3,2},{4,5},{5,4},{6,7},{7,6},{8,9},{9,8},{10,11... | collective-permute-start | bytes 393224 | tf_op jit(solution)/shard_map/ppermute | solution.py:279
  44.0 12.8 %collective-permute-start.16 = (f32[256,128]{1,0:T(8,128)S(1)}, f32[256,128]{1,0:T(8,128)S(1)}, u32[]{:S(2)}, u32[]{:S(2)}) collective-permute-start(f32[256,128]{1,0:T(8,128)S(1)} %pad_maximum_fusion.2), channel_id=1, source_target_pairs={{0,6},{2,4},{4,2},{6,0},{1,7},{3,5},{5,3},{7,1},{8,14},{10,12},{12... | collective-permute-start | bytes 393224 | tf_op jit(solution)/shard_map/ppermute | solution.py:283
  45.4 11.4 %collective-permute-start.15 = (f32[256,128]{1,0:T(8,128)S(1)}, f32[256,128]{1,0:T(8,128)S(1)}, u32[]{:S(2)}, u32[]{:S(2)}) collective-permute-start(f32[256,128]{1,0:T(8,128)S(1)} %pad_maximum_fusion.2), channel_id=1, source_target_pairs={{0,4},{2,6},{4,0},{6,2},{1,5},{3,7},{5,1},{7,3},{8,12},{10,14},{12... | collective-permute-start | bytes 393224 | tf_op jit(solution)/shard_map/ppermute | solution.py:283
  47.1 9.8 %collective-permute-start.14 = (f32[256,128]{1,0:T(8,128)S(1)}, f32[256,128]{1,0:T(8,128)S(1)}, u32[]{:S(2)}, u32[]{:S(2)}) collective-permute-start(f32[256,128]{1,0:T(8,128)S(1)} %pad_maximum_fusion.2), channel_id=1, source_target_pairs={{0,2},{2,0},{4,6},{6,4},{1,3},{3,1},{5,7},{7,5},{8,10},{10,8},{12,... | collective-permute-start | bytes 393224 | tf_op jit(solution)/shard_map/ppermute | solution.py:283
  47.6 0.7 copy-start.3
  56.9 0.8 %copy-start.1 = (f32[4,256,128]{2,1,0:T(8,128)}, f32[4,256,128]{2,1,0:T(8,128)S(1)}, u32[]{:S(2)}) copy-start(f32[4,256,128]{2,1,0:T(8,128)S(1)} %pad_maximum_fusion.cross_ref) | copy-start | bytes 1572868
  56.9 5.7 %collective-permute-start.17 = (f32[4,256,128]{2,1,0:T(8,128)S(1)}, f32[4,256,128]{2,1,0:T(8,128)S(1)}, u32[]{:S(2)}, u32[]{:S(2)}) collective-permute-start(f32[4,256,128]{2,1,0:T(8,128)S(1)} %pad_maximum_fusion.cross_ref), channel_id=1, source_target_pairs={{0,1},{1,0},{2,3},{3,2},{4,5},{5,4},{6,7},{7,6},{8,9},{9,8},{10,11... | collective-permute-start | bytes 1572872 | tf_op jit(solution)/shard_map/ppermute | solution.py:279
  62.6 0.8 %copy-start = (f32[4,256,128]{2,1,0:T(8,128)}, f32[4,256,128]{2,1,0:T(8,128)S(1)}, u32[]{:S(2)}) copy-start(f32[4,256,128]{2,1,0:T(8,128)S(1)} %collective-permute-done.17.cross_ref) | copy-start | bytes 1572868

commit v3 on v2

--- a/solution.py
+++ b/solution.py
@@ -11,7 +11,6 @@
 AXES = ("far", "z", "y", "x", "core")
 SLOTS = 4
 PARTS = 4
-HIGHEST = lax.Precision.HIGHEST
 F32 = jnp.float32
 BF16 = jnp.bfloat16
 LANES = 128
@@ -20,12 +19,33 @@
 SMEM = pl.BlockSpec(memory_space=pltpu.SMEM)
 VMEM = pl.BlockSpec(memory_space=pltpu.VMEM)
 ANY = pl.BlockSpec(memory_space=pl.ANY)
-
-
-def dot(left, right, contract):
-    return lax.dot_general(
-        left, right, (contract, ((), ())), precision=HIGHEST, preferred_element_type=F32
-    )
+PARAMS = pltpu.CompilerParams(vmem_limit_bytes=16 << 20)
+
+
+def place_of(ref):
+    number = ref[0]
+    return number % 2, number // 2 % SLOTS, number // (2 * SLOTS) % PARTS
+
+
+def parts_of(x):
+    high = x.astype(BF16)
+    rest = x - high.astype(F32)
+    middle = rest.astype(BF16)
+    return high, middle, (rest - middle.astype(F32)).astype(BF16)
+
+
+def left_of(x, axis, count=3):
+    a, b, c = parts_of(x)
+    return jnp.concatenate([a, a, b, a, c, b][:count], axis=axis)
+
+
+def right_of(x, count=3):
+    a, b, c = parts_of(x)
+    return jnp.concatenate([a, b, a, c, a, b][:count], axis=0)
+
+
+def dot(left, right, contract=((1,), (0,))):
+    return lax.dot_general(left, right, (contract, ((), ())), preferred_element_type=F32)
 
 
 def masked(ref, live_ref, columns=slice(None)):
@@ -45,17 +65,18 @@
 def products_kernel(other, place_ref, live_ref, panel_ref, trail_ref, out_ref, cross_scr):
     rows, width = panel_ref.shape
     columns = trail_ref.shape[1]
-    core, chip, depth = place_ref[0], place_ref[1], place_ref[2]
+    core, chip, depth = place_of(place_ref)
     side = 1 - core if other else core
-    panel = masked(panel_ref, live_ref)
     tall = width // SLOTS
     part = width // PARTS
     half = masked(panel_ref, live_ref, pl.ds(pl.multiple_of(side * LANES, LANES), LANES))
     start = pl.multiple_of(side * (columns // 2), LANES)
     trail = masked(trail_ref, live_ref, pl.ds(start, columns // 2))
-    product = dot(panel, jnp.concatenate([half, trail], axis=1), ((0,), (0,)))
-    for tile in range(SLOTS + 1):
-        cross_scr[tile] = product[:, tile * LANES : (tile + 1) * LANES]
+    panel = left_of(masked(panel_ref, live_ref).T, 1, 6)
+    cross_scr[0] = dot(panel, right_of(half, 6))
+    product = dot(panel[:, : 3 * rows], right_of(trail))
+    for tile in range(SLOTS):
+        cross_scr[tile + 1] = product[:, tile * LANES : (tile + 1) * LANES]
 
     @pl.when(side == 0)
     def _():
@@ -81,26 +102,9 @@
         out_specs=VMEM,
         scratch_shapes=[pltpu.VMEM((SLOTS + 1, width, LANES), F32)],
         cost_estimate=cost(12 * rows * width * (columns + width) // 2, 2 * rows * columns),
+        compiler_params=PARAMS,
         name="products_other" if other else "products_own",
     )(place, live, panel, trail)
-
-
-def parts_of(x):
-    high = x.astype(BF16)
-    rest = x - high.astype(F32)
-    middle = rest.astype(BF16)
-    return high, middle, (rest - middle.astype(F32)).astype(BF16)
-
-
-def update_product(left, right):
-    a, b, c = parts_of(left)
-    d, e, f = parts_of(right)
-    return lax.dot_general(
-        jnp.concatenate([a, a, b, a, c, b], axis=0),
-        jnp.concatenate([d, e, d, f, d, e], axis=0),
-        (((0,), (0,)), ((), ())),
-        preferred_element_type=F32,
-    )
 
 
 def across(x, lane):
@@ -182,7 +186,9 @@
             for i in range(base - here, len(rows[0]))
         ]
         left = jnp.concatenate(stacked[: tiles - base], axis=1)
-        product = update_product(left, jnp.concatenate(stacked, axis=1))[stop - base * LANES :]
+        product = dot(
+            left_of(left, 0, 6), right_of(jnp.concatenate(stacked, axis=1), 6), ((0,), (0,))
+        )[stop - base * LANES :]
         for i, t in enumerate(range(base, tiles)):
             gram_ref[stop:, tile_of(t)] -= product[:, tile_of(i)]
         for t in range(here + 1):
@@ -190,9 +196,10 @@
 
 
 def factor_kernel(
-    place_ref, live_ref, own_ref, other_ref, panel_ref, inverse_ref, unit_ref, basis_ref, gram_ref
+    place_ref, live_ref, own_ref, other_ref, panel_ref, left_ref, unit_ref, basis_ref,
+    gram_ref, inverse_ref,
 ):
-    core, chip = place_ref[0], place_ref[1]
+    core, chip, _ = place_of(place_ref)
     tall = own_ref.shape[1]
     for side, ref in ((core, own_ref), (1 - core, other_ref)):
         at = pl.ds(pl.multiple_of(side * LANES, LANES), LANES)
@@ -201,8 +208,10 @@
             gram_ref[pl.ds(row, tall), at] = ref[slot]
     root = jnp.sqrt(gram_ref[LANES : LANES + 8, 0:LANES])[0:1, 0:1]
     factor_inverse(gram_ref, inverse_ref)
-    unit = dot(masked(panel_ref, live_ref), inverse_ref[...], ((1,), (1,)))
-    unit_ref[...] = unit
+    inverse = inverse_ref[...]
+    left_ref[...] = left_of(inverse, 1)
+    unit = dot(left_of(masked(panel_ref, live_ref), 1), right_of(inverse.T))
+    unit_ref[...] = left_of(unit, 1)
     basis_ref[...] = unit * root
 
 
@@ -210,19 +219,25 @@
     rows, width = panel.shape
     return pl.pallas_call(
         factor_kernel,
-        out_shape=(struct(width, width), struct(rows, width), struct(rows, width)),
+        out_shape=(
+            jax.ShapeDtypeStruct((width, 3 * width), BF16),
+            jax.ShapeDtypeStruct((rows, 3 * width), BF16),
+            struct(rows, width),
+        ),
         in_specs=[SMEM, SMEM, VMEM, VMEM, VMEM],
         out_specs=(VMEM,) * 3,
-        scratch_shapes=[pltpu.VMEM((width, width), F32)],
+        scratch_shapes=[pltpu.VMEM((width, width), F32)] * 2,
         cost_estimate=cost(6 * 10**9, 4 * rows * width),
+        compiler_params=PARAMS,
         name="factor",
     )(place, live, own, other, panel)
 
 
 def rest_kernel(other, place_ref, live_ref, inverse_ref, unit_ref, cross_ref, trail_ref, *refs):
     width = inverse_ref.shape[0]
-    half = trail_ref.shape[1] // 2
-    core, chip, depth = place_ref[0], place_ref[1], place_ref[2]
+    columns = trail_ref.shape[1]
+    half = columns // 2
+    core, chip, depth = place_of(place_ref)
     if other:
         top_before_ref, _, top_ref, rest_ref, top_scr, cross_scr, rest_scr, sem = refs
         side = 1 - core
@@ -238,25 +253,26 @@
             cross_scr[pl.ds(row, part), pl.ds(lane, LANES)] = cross_ref[
                 slot, piece * part : (piece + 1) * part, :
             ]
-    top = dot(inverse_ref[...], cross_scr[...], ((1,), (0,)))
+    top = dot(inverse_ref[...], right_of(cross_scr[...]))
     rest_scr[...] = masked(trail_ref, live_ref, pl.ds(start, half)) - dot(
-        unit_ref[...], top, ((1,), (0,))
+        unit_ref[...], right_of(top)
     )
     copy = pltpu.make_async_copy(rest_scr, rest_ref.at[:, pl.ds(start, half)], sem)
     copy.start()
     top_scr[...] = top
     wide = top_ref.shape[1]
-    mine = top_scr[:, pl.ds(pl.multiple_of(place_ref[4], LANES), wide)]
+    begin = place_ref[0] % (columns // wide) * wide
+    mine = top_scr[:, pl.ds(pl.multiple_of(begin % half, LANES), wide)]
     if other:
-        top_ref[...] = jnp.where(place_ref[3] == side, mine, top_before_ref[...])
+        top_ref[...] = jnp.where(begin // half == side, mine, top_before_ref[...])
     else:
         top_ref[...] = mine
     copy.wait()
 
 
 def rest_of(other, place, live, inverse, unit, cross, trail, wide, before):
-    rows, width = unit.shape
-    columns = trail.shape[1]
+    rows, columns = trail.shape
+    width = inverse.shape[0]
     half = columns // 2
     return pl.pallas_call(
         functools.partial(rest_kernel, other),
@@ -271,6 +287,7 @@
         ],
         input_output_aliases={7: 1} if other else {},
         cost_estimate=cost(12 * (rows + width) * width * half, 8 * rows * half),
+        compiler_params=PARAMS,
         name="rest_other" if other else "rest_own",
     )(place, live, inverse, unit, cross, trail, *before)
 
@@ -290,19 +307,8 @@
 def body(panel, trailing, live_rows):
     width, columns = panel.shape[1], trailing.shape[1]
     flat, deep = ("y", "x"), "z"
-    core = lax.axis_index("core")
     wide = columns // (lax.axis_size("x") * 2)
-    begin = (lax.axis_index("x") * 2 + core) * wide
-    side = begin // (columns // 2)
-    place = jnp.stack(
-        [
-            core,
-            lax.axis_index(flat),
-            lax.axis_index(deep),
-            side,
-            begin - side * (columns // 2),
-        ]
-    )
+    place = lax.axis_index(AXES)[None]
     tall, part = width // SLOTS, width // PARTS
 
     theirs = products_of(True, place, live_rows, panel, trailing)

time: 68.7 us -> 55.3 us (0.80)
  Pallas kernels: 26.1 us -> 13.6 us
  other arithmetic: 1.28 us -> 0.19 us
    pallas_call x2, Pallas kernels: 7.79 us -> 2.02 us  [products_of(): pl.pallas_call(functools.partial(products_kernel, other), out_shape=struc...]
    pallas_call x2, Pallas kernels: 9.74 us -> 4.34 us  [rest_of(): pl.pallas_call(functools.partial(rest_kernel, other), out_shape=(struct(w...]
    pallas_call x1, Pallas kernels: 8.54 us -> 7.23 us  [factor_of(): pl.pallas_call(factor_kernel, out_shape=(jax.ShapeDtypeStruct((width, 3 *...]
    add x1, other arithmetic: 1.15 us -> 0.07 us  [body(): pair = ours + swap(theirs)]
    ppermute x3, waiting for transfers between devices: 0.01 us -> 0.78 us  [swap(): return lax.ppermute(x, 'core', [(0, 1), (1, 0)])]
    unnamed x8 -> x6, local copies, waits for them, and re-layouts: 2.19 us -> 2.4 us
  transfers between devices with their start and end apart: 18 -> 18, of which waited for: 7 -> 9; matrix products, arithmetic and copies ran while one was open for 0% -> 0% of each run, Pallas kernels for 25% -> 18%
where the time goes in v3:
time: 55.3 us; the launch traced here: 55.2 us
  starting transfers between devices  21.1 us (38%)
  waiting for transfers between devices  16.4 us (30%)
  Pallas kernels  13.6 us (25%)
  local copies, waits for them, and re-layouts  2.46 us (4%)
  between operations  1.43 us (3%)
    ppermute x15, starting transfers between devices, send(): return lax.ppermute(x, axes, [(i, i ^ shift) for i in range(size)])  20.5 us
    ppermute x15, waiting for transfers between devices, send(): return lax.ppermute(x, axes, [(i, i ^ shift) for i in range(size)])  15.6 us
    pallas_call x1, Pallas kernels, factor_of(): pl.pallas_call(factor_kernel, out_shape=(jax.ShapeDtypeStruct((width, 3 *...  7.23 us
    pallas_call x2, Pallas kernels, rest_of(): pl.pallas_call(functools.partial(rest_kernel, other), out_shape=(struct(w...  4.34 us
    unnamed x6, local copies, waits for them, and re-layouts  2.4 us
    pallas_call x2, Pallas kernels, products_of(): pl.pallas_call(functools.partial(products_kernel, other), out_shape=struc...  2.02 us
  transfers between devices with their start and end apart: 18, of which 9 were waited for; matrix products, arithmetic and copies ran while one was open for 0% of the time, Pallas kernels for 18%

profile of v3, /device:TPU:0, one launch (start us, length us, event | category | flops | bytes accessed | tf_op | source)
XLA Modules:
  0.0 55.2 jit_solution(647911606590238381)
XLA Ops:
  1.3 1.4 %copy-done = f32[384,1024]{1,0:T(8,128)S(1)} copy-done((f32[384,1024]{1,0:T(8,128)S(1)}, f32[384,1024]{1,0:T(8,128)}, u32[]{:S(2)}) %copy-start) | copy-done | bytes 1572888
  2.7 1.0 %copy-done.2 = f32[384,256]{1,0:T(8,128)S(1)} copy-done((f32[384,256]{1,0:T(8,128)S(1)}, f32[384,256]{1,0:T(8,128)}, u32[]{:S(2)}) %copy-start.2) | copy-done | bytes 393240
  3.7 1.0 %products_other.1 = f32[4,320,128]{2,1,0:T(8,128)S(1)} custom-call(s32[1]{0:T(128)} %bitcast.place_ref, s32[1]{0:T(128)S(6)} %copy.8.live_ref, f32[384,256]{1,0:T(8,128)S(1)} %copy-done.2, f32[384,1024]{1,0:T(8,128)S(1)} %copy-done), custom_call_target="tpu_custom_call" | custom-call | flops 754974720 | bytes 786432 | tf_op jit(solution)/shard_map/products_other/pallas_call | solution.py:98
  5.2 1.0 %products_own.1 = f32[4,320,128]{2,1,0:T(8,128)S(1)} custom-call(s32[1]{0:T(128)} %bitcast.place_ref, s32[1]{0:T(128)S(6)} %copy.8.live_ref, f32[384,256]{1,0:T(8,128)S(1)} %copy-done.2, f32[384,1024]{1,0:T(8,128)S(1)} %copy-done), custom_call_target="tpu_custom_call" | custom-call | flops 754974720 | bytes 786432 | tf_op jit(solution)/shard_map/products_own/pallas_call | solution.py:98
  6.2 0.7 %collective-permute-done = f32[4,320,128]{2,1,0:T(8,128)S(1)} collective-permute-done((f32[4,320,128]{2,1,0:T(8,128)S(1)}, f32[4,320,128]{2,1,0:T(8,128)S(1)}, u32[]{:S(2)}, u32[]{:S(2)}) %collective-permute-start) | collective-permute-done | bytes 655392 | tf_op jit(solution)/shard_map/ppermute | solution.py:296
  7.1 3.9 %collective-permute-start.3 = (f32[320,128]{1,0:T(8,128)S(1)}, f32[320,128]{1,0:T(8,128)S(1)}, u32[]{:S(2)}, u32[]{:S(2)}) collective-permute-start(f32[320,128]{1,0:T(8,128)S(1)} %get-tuple-element.27), channel_id=1, source_target_pairs={{0,6},{2,4},{4,2},{6,0},{1,7},{3,5},{5,3},{7,1},{8,14},{10,12},{12... | collective-permute-start | bytes 491528 | tf_op jit(solution)/shard_map/ppermute | solution.py:300
  11.6 4.4 %collective-permute-done.3 = f32[320,128]{1,0:T(8,128)S(1)} collective-permute-done((f32[320,128]{1,0:T(8,128)S(1)}, f32[320,128]{1,0:T(8,128)S(1)}, u32[]{:S(2)}, u32[]{:S(2)}) %collective-permute-start.3) | collective-permute-done | bytes 163872 | tf_op jit(solution)/shard_map/ppermute | solution.py:300
  15.9 3.0 %collective-permute-done.2 = f32[320,128]{1,0:T(8,128)S(1)} collective-permute-done((f32[320,128]{1,0:T(8,128)S(1)}, f32[320,128]{1,0:T(8,128)S(1)}, u32[]{:S(2)}, u32[]{:S(2)}) %collective-permute-start.2) | collective-permute-done | bytes 163872 | tf_op jit(solution)/shard_map/ppermute | solution.py:300
  19.3 3.7 %collective-permute-start.6 = (f32[128,128]{1,0:T(8,128)S(1)}, f32[128,128]{1,0:T(8,128)S(1)}, u32[]{:S(2)}, u32[]{:S(2)}) collective-permute-start(f32[128,128]{1,0:T(8,128)S(1)} %get-tuple-element.37), channel_id=1, source_target_pairs={{0,24},{8,16},{16,8},{24,0},{1,25},{9,17},{17,9},{25,1},{2,26},{10... | collective-permute-start | bytes 196616 | tf_op jit(solution)/shard_map/ppermute | solution.py:300
  23.0 0.8 %collective-permute-start.4 = (f32[128,128]{1,0:T(8,128)S(1)}, f32[128,128]{1,0:T(8,128)S(1)}, u32[]{:S(2)}, u32[]{:S(2)}) collective-permute-start(f32[128,128]{1,0:T(8,128)S(1)} %get-tuple-element.39), channel_id=1, source_target_pairs={{0,8},{8,0},{16,24},{24,16},{1,9},{9,1},{17,25},{25,17},{2,10},{10... | collective-permute-start | bytes 196616 | tf_op jit(solution)/shard_map/ppermute | solution.py:300
  23.8 2.2 %collective-permute-done.6 = f32[128,128]{1,0:T(8,128)S(1)} collective-permute-done((f32[128,128]{1,0:T(8,128)S(1)}, f32[128,128]{1,0:T(8,128)S(1)}, u32[]{:S(2)}, u32[]{:S(2)}) %collective-permute-start.6) | collective-permute-done | bytes 65568 | tf_op jit(solution)/shard_map/ppermute | solution.py:300
  26.0 2.7 %collective-permute-done.5 = f32[128,128]{1,0:T(8,128)S(1)} collective-permute-done((f32[128,128]{1,0:T(8,128)S(1)}, f32[128,128]{1,0:T(8,128)S(1)}, u32[]{:S(2)}, u32[]{:S(2)}) %collective-permute-start.5) | collective-permute-done | bytes 65568 | tf_op jit(solution)/shard_map/ppermute | solution.py:300
  28.7 1.6 %collective-permute-start.8 = (f32[64,128]{1,0:T(8,128)S(1)}, f32[64,128]{1,0:T(8,128)S(1)}, u32[]{:S(2)}, u32[]{:S(2)}) collective-permute-start(f32[64,128]{1,0:T(8,128)S(1)} %get-tuple-element.36), channel_id=1, source_target_pairs={{0,4},{2,6},{4,0},{6,2},{1,5},{3,7},{5,1},{7,3},{8,12},{10,14},{12... | collective-permute-start | bytes 98312 | tf_op jit(solution)/shard_map/ppermute | solution.py:300
  30.6 1.7 %collective-permute-start.9 = (f32[64,128]{1,0:T(8,128)S(1)}, f32[64,128]{1,0:T(8,128)S(1)}, u32[]{:S(2)}, u32[]{:S(2)}) collective-permute-start(f32[64,128]{1,0:T(8,128)S(1)} %get-tuple-element.36), channel_id=1, source_target_pairs={{0,6},{2,4},{4,2},{6,0},{1,7},{3,5},{5,3},{7,1},{8,14},{10,12},{12... | collective-permute-start | bytes 98312 | tf_op jit(solution)/shard_map/ppermute | solution.py:300
  32.3 2.7 %collective-permute-start.13 = (f32[64,128]{1,0:T(8,128)S(1)}, f32[64,128]{1,0:T(8,128)S(1)}, u32[]{:S(2)}, u32[]{:S(2)}) collective-permute-start(f32[64,128]{1,0:T(8,128)S(1)} %get-tuple-element.34), channel_id=1, source_target_pairs={{0,24},{8,16},{16,8},{24,0},{1,25},{9,17},{17,9},{25,1},{2,26},{10... | collective-permute-start | bytes 98312 | tf_op jit(solution)/shard_map/ppermute | solution.py:300
  35.0 1.7 %collective-permute-start.11 = (f32[64,128]{1,0:T(8,128)S(1)}, f32[64,128]{1,0:T(8,128)S(1)}, u32[]{:S(2)}, u32[]{:S(2)}) collective-permute-start(f32[64,128]{1,0:T(8,128)S(1)} %get-tuple-element.34), channel_id=1, source_target_pairs={{0,8},{8,0},{16,24},{24,16},{1,9},{9,1},{17,25},{25,17},{2,10},{10... | collective-permute-start | bytes 98312 | tf_op jit(solution)/shard_map/ppermute | solution.py:300
  36.8 1.4 %collective-permute-done.13 = f32[64,128]{1,0:T(8,128)S(1)} collective-permute-done((f32[64,128]{1,0:T(8,128)S(1)}, f32[64,128]{1,0:T(8,128)S(1)}, u32[]{:S(2)}, u32[]{:S(2)}) %collective-permute-start.13) | collective-permute-done | bytes 32800 | tf_op jit(solution)/shard_map/ppermute | solution.py:300
  38.2 1.6 %collective-permute-done.12 = f32[64,128]{1,0:T(8,128)S(1)} collective-permute-done((f32[64,128]{1,0:T(8,128)S(1)}, f32[64,128]{1,0:T(8,128)S(1)}, u32[]{:S(2)}, u32[]{:S(2)}) %collective-permute-start.12) | collective-permute-done | bytes 32800 | tf_op jit(solution)/shard_map/ppermute | solution.py:300
  39.8 1.1 %collective-permute-start.16 = (f32[256,128]{1,0:T(8,128)S(1)}, f32[256,128]{1,0:T(8,128)S(1)}, u32[]{:S(2)}, u32[]{:S(2)}) collective-permute-start(f32[256,128]{1,0:T(8,128)S(1)} %pad_maximum_fusion.2), channel_id=1, source_target_pairs={{0,6},{2,4},{4,2},{6,0},{1,7},{3,5},{5,3},{7,1},{8,14},{10,12},{12... | collective-permute-start | bytes 393224 | tf_op jit(solution)/shard_map/ppermute | solution.py:300
  40.9 1.9 %collective-permute-start.15 = (f32[256,128]{1,0:T(8,128)S(1)}, f32[256,128]{1,0:T(8,128)S(1)}, u32[]{:S(2)}, u32[]{:S(2)}) collective-permute-start(f32[256,128]{1,0:T(8,128)S(1)} %pad_maximum_fusion.2), channel_id=1, source_target_pairs={{0,4},{2,6},{4,0},{6,2},{1,5},{3,7},{5,1},{7,3},{8,12},{10,14},{12... | collective-permute-start | bytes 393224 | tf_op jit(solution)/shard_map/ppermute | solution.py:300
  42.8 0.5 collective-permute-start.14
  43.4 7.2 %factor.1 = (bf16[256,768]{1,0:T(8,128)(2,1)S(1)}, bf16[384,768]{1,0:T(8,128)(2,1)S(1)}, f32[384,256]{1,0:T(8,128)}) custom-call(s32[1]{0:T(128)} %bitcast.place_ref, s32[1]{0:T(128)S(6)} %copy.8.live_ref, f32[4,64,128]{2,1,0:T(8,128)S(1)} %pad_maximum_fusion.1.own_ref, f32[4,64,128]{2,1,0:T(8,128)S(1)} %collective-permute-done.10.other_ref, ...), custom_call_target="tpu_custom_call" | custom-call | flops 6000000000 | bytes 393216 | tf_op jit(solution)/shard_map/factor/pallas_call | solution.py:220
  50.7 1.8 %rest_own.1 = (f32[256,256]{1,0:T(8,128)S(1)}, f32[384,1024]{1,0:T(8,128)}) custom-call(s32[1]{0:T(128)} %bitcast.place_ref, s32[1]{0:T(128)S(6)} %copy.8.live_ref, bf16[256,768]{1,0:T(8,128)(2,1)S(1)} %get-tuple-element.17.inverse_ref, bf16[384,768]{1,0:T(8,128)(2,1)S(1)} %get-tuple-element.18.unit_ref, f32[4,256,128]{2,1,0:T(8,128)S(1)} %pad_maximum_fusion.cross_ref, ...), custom_call_target="tpu_custom_call" | custom-call | flops 1006632960 | bytes 1572864 | tf_op jit(solution)/shard_map/rest_own/pallas_call | solution.py:277
  52.6 2.5 %rest_other.1 = (f32[256,256]{1,0:T(8,128)}, f32[384,1024]{1,0:T(8,128)}) custom-call(s32[1]{0:T(128)} %bitcast.place_ref, s32[1]{0:T(128)S(6)} %copy.8.live_ref, bf16[256,768]{1,0:T(8,128)(2,1)S(1)} %get-tuple-element.17.inverse_ref, bf16[384,768]{1,0:T(8,128)(2,1)S(1)} %get-tuple-element.18.unit_ref, ...), custom_call_target="tpu_custom_call", output_to_operand_aliasing={{1}: (7, {})} | custom-call | flops 1006632960 | bytes 1572864 | tf_op jit(solution)/shard_map/rest_other/pallas_call | solution.py:277
  (33 shorter events, 2.2 us)
Async XLA Ops:
  1.3 1.4 %copy-start = (f32[384,1024]{1,0:T(8,128)S(1)}, f32[384,1024]{1,0:T(8,128)}, u32[]{:S(2)}) copy-start(f32[384,1024]{1,0:T(8,128)} %trail_ref.7) | copy-start | bytes 4718596
  2.7 1.0 %copy-start.2 = (f32[384,256]{1,0:T(8,128)S(1)}, f32[384,256]{1,0:T(8,128)}, u32[]{:S(2)}) copy-start(f32[384,256]{1,0:T(8,128)} %panel_ref.5) | copy-start | bytes 1179652
  4.7 2.2 %collective-permute-start = (f32[4,320,128]{2,1,0:T(8,128)S(1)}, f32[4,320,128]{2,1,0:T(8,128)S(1)}, u32[]{:S(2)}, u32[]{:S(2)}) collective-permute-start(f32[4,320,128]{2,1,0:T(8,128)S(1)} %products_other.1), channel_id=1, source_target_pairs={{0,1},{1,0},{2,3},{3,2},{4,5},{5,4},{6,7},{7,6},{8,9},{9,8},{10,11... | collective-permute-start | bytes 1966088 | tf_op jit(solution)/shard_map/ppermute | solution.py:296
  7.1 8.9 %collective-permute-start.3 = (f32[320,128]{1,0:T(8,128)S(1)}, f32[320,128]{1,0:T(8,128)S(1)}, u32[]{:S(2)}, u32[]{:S(2)}) collective-permute-start(f32[320,128]{1,0:T(8,128)S(1)} %get-tuple-element.27), channel_id=1, source_target_pairs={{0,6},{2,4},{4,2},{6,0},{1,7},{3,5},{5,3},{7,1},{8,14},{10,12},{12... | collective-permute-start | bytes 491528 | tf_op jit(solution)/shard_map/ppermute | solution.py:300
  10.9 8.0 %collective-permute-start.2 = (f32[320,128]{1,0:T(8,128)S(1)}, f32[320,128]{1,0:T(8,128)S(1)}, u32[]{:S(2)}, u32[]{:S(2)}) collective-permute-start(f32[320,128]{1,0:T(8,128)S(1)} %get-tuple-element.28), channel_id=1, source_target_pairs={{0,4},{2,6},{4,0},{6,2},{1,5},{3,7},{5,1},{7,3},{8,12},{10,14},{12... | collective-permute-start | bytes 491528 | tf_op jit(solution)/shard_map/ppermute | solution.py:300
  11.5 7.8 %collective-permute-start.1 = (f32[320,128]{1,0:T(8,128)S(1)}, f32[320,128]{1,0:T(8,128)S(1)}, u32[]{:S(2)}, u32[]{:S(2)}) collective-permute-start(f32[320,128]{1,0:T(8,128)S(1)} %get-tuple-element.29), channel_id=1, source_target_pairs={{0,2},{2,0},{4,6},{6,4},{1,3},{3,1},{5,7},{7,5},{8,10},{10,8},{12,... | collective-permute-start | bytes 491528 | tf_op jit(solution)/shard_map/ppermute | solution.py:300
  19.3 6.6 %collective-permute-start.6 = (f32[128,128]{1,0:T(8,128)S(1)}, f32[128,128]{1,0:T(8,128)S(1)}, u32[]{:S(2)}, u32[]{:S(2)}) collective-permute-start(f32[128,128]{1,0:T(8,128)S(1)} %get-tuple-element.37), channel_id=1, source_target_pairs={{0,24},{8,16},{16,8},{24,0},{1,25},{9,17},{17,9},{25,1},{2,26},{10... | collective-permute-start | bytes 196616 | tf_op jit(solution)/shard_map/ppermute | solution.py:300
  23.0 5.7 %collective-permute-start.5 = (f32[128,128]{1,0:T(8,128)S(1)}, f32[128,128]{1,0:T(8,128)S(1)}, u32[]{:S(2)}, u32[]{:S(2)}) collective-permute-start(f32[128,128]{1,0:T(8,128)S(1)} %get-tuple-element.38), channel_id=1, source_target_pairs={{0,16},{8,24},{16,0},{24,8},{1,17},{9,25},{17,1},{25,9},{2,18},{10... | collective-permute-start | bytes 196616 | tf_op jit(solution)/shard_map/ppermute | solution.py:300
  23.0 5.7 %collective-permute-start.4 = (f32[128,128]{1,0:T(8,128)S(1)}, f32[128,128]{1,0:T(8,128)S(1)}, u32[]{:S(2)}, u32[]{:S(2)}) collective-permute-start(f32[128,128]{1,0:T(8,128)S(1)} %get-tuple-element.39), channel_id=1, source_target_pairs={{0,8},{8,0},{16,24},{24,16},{1,9},{9,1},{17,25},{25,17},{2,10},{10... | collective-permute-start | bytes 196616 | tf_op jit(solution)/shard_map/ppermute | solution.py:300
  28.7 6.2 %collective-permute-start.8 = (f32[64,128]{1,0:T(8,128)S(1)}, f32[64,128]{1,0:T(8,128)S(1)}, u32[]{:S(2)}, u32[]{:S(2)}) collective-permute-start(f32[64,128]{1,0:T(8,128)S(1)} %get-tuple-element.36), channel_id=1, source_target_pairs={{0,4},{2,6},{4,0},{6,2},{1,5},{3,7},{5,1},{7,3},{8,12},{10,14},{12... | collective-permute-start | bytes 98312 | tf_op jit(solution)/shard_map/ppermute | solution.py:300
  30.3 6.4 %collective-permute-start.7 = (f32[64,128]{1,0:T(8,128)S(1)}, f32[64,128]{1,0:T(8,128)S(1)}, u32[]{:S(2)}, u32[]{:S(2)}) collective-permute-start(f32[64,128]{1,0:T(8,128)S(1)} %get-tuple-element.36), channel_id=1, source_target_pairs={{0,2},{2,0},{4,6},{6,4},{1,3},{3,1},{5,7},{7,5},{8,10},{10,8},{12,... | collective-permute-start | bytes 98312 | tf_op jit(solution)/shard_map/ppermute | solution.py:300
  30.6 6.1 %collective-permute-start.9 = (f32[64,128]{1,0:T(8,128)S(1)}, f32[64,128]{1,0:T(8,128)S(1)}, u32[]{:S(2)}, u32[]{:S(2)}) collective-permute-start(f32[64,128]{1,0:T(8,128)S(1)} %get-tuple-element.36), channel_id=1, source_target_pairs={{0,6},{2,4},{4,2},{6,0},{1,7},{3,5},{5,3},{7,1},{8,14},{10,12},{12... | collective-permute-start | bytes 98312 | tf_op jit(solution)/shard_map/ppermute | solution.py:300
  32.3 5.9 %collective-permute-start.13 = (f32[64,128]{1,0:T(8,128)S(1)}, f32[64,128]{1,0:T(8,128)S(1)}, u32[]{:S(2)}, u32[]{:S(2)}) collective-permute-start(f32[64,128]{1,0:T(8,128)S(1)} %get-tuple-element.34), channel_id=1, source_target_pairs={{0,24},{8,16},{16,8},{24,0},{1,25},{9,17},{17,9},{25,1},{2,26},{10... | collective-permute-start | bytes 98312 | tf_op jit(solution)/shard_map/ppermute | solution.py:300
  35.0 4.8 %collective-permute-start.12 = (f32[64,128]{1,0:T(8,128)S(1)}, f32[64,128]{1,0:T(8,128)S(1)}, u32[]{:S(2)}, u32[]{:S(2)}) collective-permute-start(f32[64,128]{1,0:T(8,128)S(1)} %get-tuple-element.34), channel_id=1, source_target_pairs={{0,16},{8,24},{16,0},{24,8},{1,17},{9,25},{17,1},{25,9},{2,18},{10... | collective-permute-start | bytes 98312 | tf_op jit(solution)/shard_map/ppermute | solution.py:300
  35.0 4.8 %collective-permute-start.11 = (f32[64,128]{1,0:T(8,128)S(1)}, f32[64,128]{1,0:T(8,128)S(1)}, u32[]{:S(2)}, u32[]{:S(2)}) collective-permute-start(f32[64,128]{1,0:T(8,128)S(1)} %get-tuple-element.34), channel_id=1, source_target_pairs={{0,8},{8,0},{16,24},{24,16},{1,9},{9,1},{17,25},{25,17},{2,10},{10... | collective-permute-start | bytes 98312 | tf_op jit(solution)/shard_map/ppermute | solution.py:300
  36.7 6.7 %collective-permute-start.10 = (f32[4,64,128]{2,1,0:T(8,128)S(1)}, f32[4,64,128]{2,1,0:T(8,128)S(1)}, u32[]{:S(2)}, u32[]{:S(2)}) collective-permute-start(f32[4,64,128]{2,1,0:T(8,128)S(1)} %pad_maximum_fusion.1.own_ref), channel_id=1, source_target_pairs={{0,1},{1,0},{2,3},{3,2},{4,5},{5,4},{6,7},{7,6},{8,9},{9,8},{10,11... | collective-permute-start | bytes 393224 | tf_op jit(solution)/shard_map/ppermute | solution.py:296
  39.8 10.9 %copy-start.1 = (f32[384,1024]{1,0:T(8,128)S(1)}, f32[384,1024]{1,0:T(8,128)}, u32[]{:S(2)}) copy-start(f32[384,1024]{1,0:T(8,128)} %trail_ref.7) | copy-start | bytes 4718596
  39.8 10.8 %collective-permute-start.16 = (f32[256,128]{1,0:T(8,128)S(1)}, f32[256,128]{1,0:T(8,128)S(1)}, u32[]{:S(2)}, u32[]{:S(2)}) collective-permute-start(f32[256,128]{1,0:T(8,128)S(1)} %pad_maximum_fusion.2), channel_id=1, source_target_pairs={{0,6},{2,4},{4,2},{6,0},{1,7},{3,5},{5,3},{7,1},{8,14},{10,12},{12... | collective-permute-start | bytes 393224 | tf_op jit(solution)/shard_map/ppermute | solution.py:300
  40.9 9.7 %collective-permute-start.15 = (f32[256,128]{1,0:T(8,128)S(1)}, f32[256,128]{1,0:T(8,128)S(1)}, u32[]{:S(2)}, u32[]{:S(2)}) collective-permute-start(f32[256,128]{1,0:T(8,128)S(1)} %pad_maximum_fusion.2), channel_id=1, source_target_pairs={{0,4},{2,6},{4,0},{6,2},{1,5},{3,7},{5,1},{7,3},{8,12},{10,14},{12... | collective-permute-start | bytes 393224 | tf_op jit(solution)/shard_map/ppermute | solution.py:300
  42.8 7.8 %collective-permute-start.14 = (f32[256,128]{1,0:T(8,128)S(1)}, f32[256,128]{1,0:T(8,128)S(1)}, u32[]{:S(2)}, u32[]{:S(2)}) collective-permute-start(f32[256,128]{1,0:T(8,128)S(1)} %pad_maximum_fusion.2), channel_id=1, source_target_pairs={{0,2},{2,0},{4,6},{6,4},{1,3},{3,1},{5,7},{7,5},{8,10},{10,8},{12,... | collective-permute-start | bytes 393224 | tf_op jit(solution)/shard_map/ppermute | solution.py:300
  50.7 2.0 %collective-permute-start.17 = (f32[4,256,128]{2,1,0:T(8,128)S(1)}, f32[4,256,128]{2,1,0:T(8,128)S(1)}, u32[]{:S(2)}, u32[]{:S(2)}) collective-permute-start(f32[4,256,128]{2,1,0:T(8,128)S(1)} %pad_maximum_fusion.cross_ref), channel_id=1, source_target_pairs={{0,1},{1,0},{2,3},{3,2},{4,5},{5,4},{6,7},{7,6},{8,9},{9,8},{10,11... | collective-permute-start | bytes 1572872 | tf_op jit(solution)/shard_map/ppermute | solution.py:296

commit v4 on v3

--- a/solution.py
+++ b/solution.py
@@ -16,10 +16,16 @@
 LANES = 128
 BLOCK = 32
 BATCH = 16
+STRIP = 256
 SMEM = pl.BlockSpec(memory_space=pltpu.SMEM)
 VMEM = pl.BlockSpec(memory_space=pltpu.VMEM)
 ANY = pl.BlockSpec(memory_space=pl.ANY)
+HBM = pl.BlockSpec(memory_space=pltpu.HBM)
 PARAMS = pltpu.CompilerParams(vmem_limit_bytes=16 << 20)
+
+
+def in_hbm(x):
+    return pltpu.with_memory_space_constraint(x, pltpu.HBM)
 
 
 def place_of(ref):
@@ -39,9 +45,9 @@
     return jnp.concatenate([a, a, b, a, c, b][:count], axis=axis)
 
 
-def right_of(x, count=3):
+def right_of(x, count=3, axis=0):
     a, b, c = parts_of(x)
-    return jnp.concatenate([a, b, a, c, a, b][:count], axis=0)
+    return jnp.concatenate([a, b, a, c, a, b][:count], axis=axis)
 
 
 def dot(left, right, contract=((1,), (0,))):
@@ -62,21 +68,14 @@
     return pl.CostEstimate(flops=flops, bytes_accessed=transferred, transcendentals=0)
 
 
-def products_kernel(other, place_ref, live_ref, panel_ref, trail_ref, out_ref, cross_scr):
-    rows, width = panel_ref.shape
-    columns = trail_ref.shape[1]
-    core, chip, depth = place_of(place_ref)
-    side = 1 - core if other else core
+def place_products(side, place_ref, live_ref, gram, cross, out_ref, cross_scr):
+    width = gram.shape[0]
+    _, chip, depth = place_of(place_ref)
     tall = width // SLOTS
     part = width // PARTS
-    half = masked(panel_ref, live_ref, pl.ds(pl.multiple_of(side * LANES, LANES), LANES))
-    start = pl.multiple_of(side * (columns // 2), LANES)
-    trail = masked(trail_ref, live_ref, pl.ds(start, columns // 2))
-    panel = left_of(masked(panel_ref, live_ref).T, 1, 6)
-    cross_scr[0] = dot(panel, right_of(half, 6))
-    product = dot(panel[:, : 3 * rows], right_of(trail))
+    cross_scr[0] = gram
     for tile in range(SLOTS):
-        cross_scr[tile + 1] = product[:, tile * LANES : (tile + 1) * LANES]
+        cross_scr[tile + 1] = cross[:, tile * LANES : (tile + 1) * LANES]
 
     @pl.when(side == 0)
     def _():
@@ -92,19 +91,83 @@
             out_ref[slot, to : to + part, :] = cross_scr[chunk + 1, pl.ds(at, part), :]
 
 
-def products_of(other, place, live, panel, trail):
+def other_kernel(
+    place_ref, live_ref, panel_ref, trail_ref, out_ref, left_ref, gram_ref, half_ref,
+    cross_scr, panel_scr, trail_scr, panel_sem, trail_sem, half_sem,
+):
+    columns = trail_ref.shape[1]
+    core = place_of(place_ref)[0]
+    wide = columns // 2
+
+    def columns_of(side):
+        return trail_ref.at[:, pl.ds(pl.multiple_of(side * wide, LANES), wide)]
+
+    copy_panel = pltpu.make_async_copy(panel_ref, panel_scr, panel_sem)
+    copy_trail = pltpu.make_async_copy(columns_of(1 - core), trail_scr, trail_sem)
+    copy_half = pltpu.make_async_copy(columns_of(core), half_ref, half_sem)
+    copy_panel.start()
+    copy_trail.start()
+    copy_half.start()
+    copy_panel.wait()
+    rows = panel_scr.shape[0]
+    panel = masked(panel_scr, live_ref)
+    left = left_of(panel.T, 1, 6)
+    left_ref[...] = left[:, : 3 * rows]
+    gram = dot(left, right_of(panel, 6))
+    panel_scr[: gram.shape[0], :] = gram
+    own = pl.ds(pl.multiple_of(core * LANES, LANES), LANES)
+    rest = pl.ds(pl.multiple_of((1 - core) * LANES, LANES), LANES)
+    gram_ref[...] = panel_scr[: gram.shape[0], own]
+    copy_trail.wait()
+    cross = dot(left[:, : 3 * rows], right_of(masked(trail_scr, live_ref)))
+    gram = panel_scr[: gram.shape[0], rest]
+    place_products(1 - core, place_ref, live_ref, gram, cross, out_ref, cross_scr)
+    copy_half.wait()
+
+
+def own_kernel(place_ref, live_ref, left_ref, gram_ref, half_ref, out_ref, cross_scr):
+    cross = dot(left_ref[...], right_of(masked(half_ref, live_ref)))
+    side = place_of(place_ref)[0]
+    place_products(side, place_ref, live_ref, gram_ref[...], cross, out_ref, cross_scr)
+
+
+def products_of(place, live, panel, trail):
     rows, width = panel.shape
     columns = trail.shape[1]
-    return pl.pallas_call(
-        functools.partial(products_kernel, other),
-        out_shape=struct(SLOTS, width // SLOTS + width, LANES),
-        in_specs=[SMEM, SMEM, VMEM, VMEM],
+    out = struct(SLOTS, width // SLOTS + width, LANES)
+    work = cost(6 * rows * width * columns // 2, 2 * rows * columns)
+    cross_scr = pltpu.VMEM((SLOTS + 1, width, LANES), F32)
+    theirs, *handed = pl.pallas_call(
+        other_kernel,
+        out_shape=(
+            out,
+            jax.ShapeDtypeStruct((width, 3 * rows), BF16),
+            struct(width, LANES),
+            struct(rows, columns // 2),
+        ),
+        in_specs=[SMEM, SMEM, HBM, HBM],
+        out_specs=(VMEM,) * 4,
+        scratch_shapes=[
+            cross_scr,
+            pltpu.VMEM((rows, width), F32),
+            pltpu.VMEM((rows, columns // 2), F32),
+        ]
+        + [pltpu.SemaphoreType.DMA] * 3,
+        cost_estimate=work,
+        compiler_params=PARAMS,
+        name="products_other",
+    )(place, live, in_hbm(panel), in_hbm(trail))
+    ours = pl.pallas_call(
+        own_kernel,
+        out_shape=out,
+        in_specs=[SMEM, SMEM] + [VMEM] * 3,
         out_specs=VMEM,
-        scratch_shapes=[pltpu.VMEM((SLOTS + 1, width, LANES), F32)],
-        cost_estimate=cost(12 * rows * width * (columns + width) // 2, 2 * rows * columns),
+        scratch_shapes=[cross_scr],
+        cost_estimate=work,
         compiler_params=PARAMS,
-        name="products_other" if other else "products_own",
-    )(place, live, panel, trail)
+        name="products_own",
+    )(place, live, *handed)
+    return theirs, ours
 
 
 def across(x, lane):
@@ -125,28 +188,43 @@
             for j in range(start, start + BATCH)
             for group in range(j // 8, groups)
         }
-        for j in range(start, start + BATCH):
+        for j in range(start, start + BATCH, 2):
             home, place = divmod(j, 8)
-            pivot = down(columns[home, j], place)
-            pivots[home] = jnp.where(index == place, pivot, pivots[home])
-            inverse = 1.0 / pivot
-            factors = {}
+            a = down(columns[home, j], place)
+            b = down(columns[home, j], place + 1)
+            c = down(columns[home, j + 1], place + 1)
+            minor = a * c - b * b
+            over_a, over_minor = 1.0 / a, 1.0 / minor
+            ratio = b * over_a
+            pivots[home] = jnp.where(index == place, a, pivots[home])
+            pivots[home] = jnp.where(index == place + 1, minor * over_a, pivots[home])
+            first_factor, second_factor = {}, {}
             for group in range(home, groups):
-                column = columns[group, j]
+                one = columns[group, j]
+                two = columns[group, j + 1] * a - one * b
                 if group == home:
-                    if place == 7:
-                        continue
-                    column = jnp.where(index > place, column, 0.0)
-                factors[group] = column * inverse
-            for m in range(j + 1, start + BATCH):
+                    one = jnp.where(index > place, one, 0.0)
+                    two = jnp.where(index > place + 1, two, 0.0)
+                first_factor[group] = one * over_a
+                second_factor[group] = two * over_minor
+            for m in range(j + 2, start + BATCH):
                 value = down(columns[m // 8, j], m % 8)
+                other = down(columns[m // 8, j + 1], m % 8) - ratio * value
                 for group in range(m // 8, groups):
-                    if group in factors:
-                        columns[group, m] = columns[group, m] - factors[group] * value
+                    columns[group, m] = (
+                        columns[group, m]
+                        - first_factor[group] * value
+                        - second_factor[group] * other
+                    )
             for tile in range(len(rows[0])):
                 value = down(rows[home][tile], place)
-                for group in factors:
-                    rows[group][tile] = rows[group][tile] - factors[group] * value
+                other = down(rows[home][tile], place + 1) - ratio * value
+                for group in first_factor:
+                    rows[group][tile] = (
+                        rows[group][tile]
+                        - first_factor[group] * value
+                        - second_factor[group] * other
+                    )
     return pivots
 
 
@@ -210,7 +288,7 @@
     factor_inverse(gram_ref, inverse_ref)
     inverse = inverse_ref[...]
     left_ref[...] = left_of(inverse, 1)
-    unit = dot(left_of(masked(panel_ref, live_ref), 1), right_of(inverse.T))
+    unit = dot(left_of(masked(panel_ref, live_ref), 1), right_of(inverse, axis=1), ((1,), (1,)))
     unit_ref[...] = left_of(unit, 1)
     basis_ref[...] = unit * root
 
@@ -253,13 +331,16 @@
             cross_scr[pl.ds(row, part), pl.ds(lane, LANES)] = cross_ref[
                 slot, piece * part : (piece + 1) * part, :
             ]
-    top = dot(inverse_ref[...], right_of(cross_scr[...]))
-    rest_scr[...] = masked(trail_ref, live_ref, pl.ds(start, half)) - dot(
-        unit_ref[...], right_of(top)
-    )
-    copy = pltpu.make_async_copy(rest_scr, rest_ref.at[:, pl.ds(start, half)], sem)
-    copy.start()
-    top_scr[...] = top
+    pieces = half // STRIP
+    copies = []
+    for piece in range(pieces):
+        at = slice(piece * STRIP, (piece + 1) * STRIP)
+        to = pl.ds(start + piece * STRIP, STRIP)
+        top = dot(inverse_ref[...], right_of(cross_scr[:, at]))
+        top_scr[:, at] = top
+        rest_scr[:, at] = masked(trail_ref, live_ref, to) - dot(unit_ref[...], right_of(top))
+        copies.append(pltpu.make_async_copy(rest_scr.at[:, at], rest_ref.at[:, to], sem.at[piece]))
+        copies[piece].start()
     wide = top_ref.shape[1]
     begin = place_ref[0] % (columns // wide) * wide
     mine = top_scr[:, pl.ds(pl.multiple_of(begin % half, LANES), wide)]
@@ -267,7 +348,8 @@
         top_ref[...] = jnp.where(begin // half == side, mine, top_before_ref[...])
     else:
         top_ref[...] = mine
-    copy.wait()
+    for copy in copies:
+        copy.wait()
 
 
 def rest_of(other, place, live, inverse, unit, cross, trail, wide, before):
@@ -283,7 +365,7 @@
             pltpu.VMEM((width, half), F32),
             pltpu.VMEM((width, half), F32),
             pltpu.VMEM((rows, half), F32),
-            pltpu.SemaphoreType.DMA,
+            pltpu.SemaphoreType.DMA((half // STRIP,)),
         ],
         input_output_aliases={7: 1} if other else {},
         cost_estimate=cost(12 * (rows + width) * width * half, 8 * rows * half),
@@ -311,8 +393,7 @@
     place = lax.axis_index(AXES)[None]
     tall, part = width // SLOTS, width // PARTS
 
-    theirs = products_of(True, place, live_rows, panel, trailing)
-    ours = products_of(False, place, live_rows, panel, trailing)
+    theirs, ours = products_of(place, live_rows, panel, trailing)
     pair = ours + swap(theirs)
     slots = [pair[0]] + [send(pair[k], flat, SLOTS, k) for k in range(1, SLOTS)]
     summed = tree(slots)

time: 55.3 us -> 55.2 us (level)
  local copies, waits for them, and re-layouts: 2.46 us -> 0.07 us
  Pallas kernels: 13.6 us -> 15.5 us
    unnamed x6 -> x4, local copies, waits for them, and re-layouts: 2.4 us -> 0.01 us
    pallas_call x2, Pallas kernels: 2.02 us -> 3.35 us  [the longest x1 2.75 us: products_of(): pl.pallas_call(other_kernel, out_shape=(out, jax.ShapeDtypeStruct((width,...]
  transfers between devices with their start and end apart: 18 -> 18, of which waited for: 9 -> 8; matrix products, arithmetic and copies ran while one was open for 0% -> 0% of each run, Pallas kernels for 18% -> 18%
where the time goes in v4:
time: 55.2 us; the launch traced here: 55 us
  starting transfers between devices  21.1 us (38%)
  waiting for transfers between devices  16.7 us (30%)
  Pallas kernels  15.5 us (28%)
  between operations  1.44 us (3%)
    ppermute x15, starting transfers between devices, send(): return lax.ppermute(x, axes, [(i, i ^ shift) for i in range(size)])  20.5 us
    ppermute x15, waiting for transfers between devices, send(): return lax.ppermute(x, axes, [(i, i ^ shift) for i in range(size)])  15.6 us
    pallas_call x1, Pallas kernels, factor_of(): pl.pallas_call(factor_kernel, out_shape=(jax.ShapeDtypeStruct((width, 3 *...  7.29 us
    pallas_call x2, Pallas kernels, rest_of(): pl.pallas_call(functools.partial(rest_kernel, other), out_shape=(struct(w...  4.86 us
    pallas_call x1, Pallas kernels, products_of(): pl.pallas_call(other_kernel, out_shape=(out, jax.ShapeDtypeStruct((width,...  2.75 us
    ppermute x3, waiting for transfers between devices, swap(): return lax.ppermute(x, 'core', [(0, 1), (1, 0)])  1.12 us
  transfers between devices with their start and end apart: 18, of which 8 were waited for; matrix products, arithmetic and copies ran while one was open for 0% of the time, Pallas kernels for 18%

profile of v4, /device:TPU:0, one launch (start us, length us, event | category | flops | bytes accessed | tf_op | source)
XLA Modules:
  0.0 55.0 jit_solution(4071865035551393997)
XLA Ops:
  1.3 2.7 %products_other.1 = (f32[4,320,128]{2,1,0:T(8,128)S(1)}, bf16[256,1152]{1,0:T(8,128)(2,1)S(1)}, f32[256,128]{1,0:T(8,128)S(1)}, f32[384,512]{1,0:T(8,128)S(1)}) custom-call(s32[1]{0:T(128)} %bitcast.place_ref, s32[1]{0:T(128)S(6)} %copy.8.live_ref, f32[384,256]{1,0:T(8,128)} %panel_ref.3, f32[384,1024]{1,0:T(8,128)} %trail_ref.5), custom_call_target="tpu_custom_call" | custom-call | flops 301989888 | bytes 786432 | tf_op jit(solution)/shard_map/products_other/pallas_call | solution.py:140
  4.0 0.5 collective-permute-start
  4.6 0.6 %products_own.1 = f32[4,320,128]{2,1,0:T(8,128)S(1)} custom-call(s32[1]{0:T(128)} %bitcast.place_ref, s32[1]{0:T(128)S(6)} %copy.8.live_ref, bf16[256,1152]{1,0:T(8,128)(2,1)S(1)} %get-tuple-element.19.left_ref, f32[256,128]{1,0:T(8,128)S(1)} %get-tuple-element.20.gram_ref, f32[384,512]{1,0:T(8,128)S(1)} %get-tuple-element.21.half_ref), custom_call_target="tpu_custom_call" | custom-call | flops 301989888 | bytes 786432 | tf_op jit(solution)/shard_map/products_own/pallas_call | solution.py:160
  5.2 1.1 %collective-permute-done = f32[4,320,128]{2,1,0:T(8,128)S(1)} collective-permute-done((f32[4,320,128]{2,1,0:T(8,128)S(1)}, f32[4,320,128]{2,1,0:T(8,128)S(1)}, u32[]{:S(2)}, u32[]{:S(2)}) %collective-permute-start) | collective-permute-done | bytes 655392 | tf_op jit(solution)/shard_map/ppermute | solution.py:378
  6.4 3.9 %collective-permute-start.3 = (f32[320,128]{1,0:T(8,128)S(1)}, f32[320,128]{1,0:T(8,128)S(1)}, u32[]{:S(2)}, u32[]{:S(2)}) collective-permute-start(f32[320,128]{1,0:T(8,128)S(1)} %get-tuple-element.35), channel_id=1, source_target_pairs={{0,6},{2,4},{4,2},{6,0},{1,7},{3,5},{5,3},{7,1},{8,14},{10,12},{12... | collective-permute-start | bytes 491528 | tf_op jit(solution)/shard_map/ppermute | solution.py:382
  10.3 0.5 collective-permute-start.2
  10.9 4.4 %collective-permute-done.3 = f32[320,128]{1,0:T(8,128)S(1)} collective-permute-done((f32[320,128]{1,0:T(8,128)S(1)}, f32[320,128]{1,0:T(8,128)S(1)}, u32[]{:S(2)}, u32[]{:S(2)}) %collective-permute-start.3) | collective-permute-done | bytes 163872 | tf_op jit(solution)/shard_map/ppermute | solution.py:382
  15.3 3.0 %collective-permute-done.2 = f32[320,128]{1,0:T(8,128)S(1)} collective-permute-done((f32[320,128]{1,0:T(8,128)S(1)}, f32[320,128]{1,0:T(8,128)S(1)}, u32[]{:S(2)}, u32[]{:S(2)}) %collective-permute-start.2) | collective-permute-done | bytes 163872 | tf_op jit(solution)/shard_map/ppermute | solution.py:382
  18.7 3.7 %collective-permute-start.6 = (f32[128,128]{1,0:T(8,128)S(1)}, f32[128,128]{1,0:T(8,128)S(1)}, u32[]{:S(2)}, u32[]{:S(2)}) collective-permute-start(f32[128,128]{1,0:T(8,128)S(1)} %get-tuple-element.45), channel_id=1, source_target_pairs={{0,24},{8,16},{16,8},{24,0},{1,25},{9,17},{17,9},{25,1},{2,26},{10... | collective-permute-start | bytes 196616 | tf_op jit(solution)/shard_map/ppermute | solution.py:382
  22.3 0.8 %collective-permute-start.4 = (f32[128,128]{1,0:T(8,128)S(1)}, f32[128,128]{1,0:T(8,128)S(1)}, u32[]{:S(2)}, u32[]{:S(2)}) collective-permute-start(f32[128,128]{1,0:T(8,128)S(1)} %get-tuple-element.47), channel_id=1, source_target_pairs={{0,8},{8,0},{16,24},{24,16},{1,9},{9,1},{17,25},{25,17},{2,10},{10... | collective-permute-start | bytes 196616 | tf_op jit(solution)/shard_map/ppermute | solution.py:382
  23.1 2.2 %collective-permute-done.6 = f32[128,128]{1,0:T(8,128)S(1)} collective-permute-done((f32[128,128]{1,0:T(8,128)S(1)}, f32[128,128]{1,0:T(8,128)S(1)}, u32[]{:S(2)}, u32[]{:S(2)}) %collective-permute-start.6) | collective-permute-done | bytes 65568 | tf_op jit(solution)/shard_map/ppermute | solution.py:382
  25.3 2.7 %collective-permute-done.5 = f32[128,128]{1,0:T(8,128)S(1)} collective-permute-done((f32[128,128]{1,0:T(8,128)S(1)}, f32[128,128]{1,0:T(8,128)S(1)}, u32[]{:S(2)}, u32[]{:S(2)}) %collective-permute-start.5) | collective-permute-done | bytes 65568 | tf_op jit(solution)/shard_map/ppermute | solution.py:382
  28.1 1.6 %collective-permute-start.8 = (f32[64,128]{1,0:T(8,128)S(1)}, f32[64,128]{1,0:T(8,128)S(1)}, u32[]{:S(2)}, u32[]{:S(2)}) collective-permute-start(f32[64,128]{1,0:T(8,128)S(1)} %get-tuple-element.44), channel_id=1, source_target_pairs={{0,4},{2,6},{4,0},{6,2},{1,5},{3,7},{5,1},{7,3},{8,12},{10,14},{12... | collective-permute-start | bytes 98312 | tf_op jit(solution)/shard_map/ppermute | solution.py:382
  30.0 1.7 %collective-permute-start.9 = (f32[64,128]{1,0:T(8,128)S(1)}, f32[64,128]{1,0:T(8,128)S(1)}, u32[]{:S(2)}, u32[]{:S(2)}) collective-permute-start(f32[64,128]{1,0:T(8,128)S(1)} %get-tuple-element.44), channel_id=1, source_target_pairs={{0,6},{2,4},{4,2},{6,0},{1,7},{3,5},{5,3},{7,1},{8,14},{10,12},{12... | collective-permute-start | bytes 98312 | tf_op jit(solution)/shard_map/ppermute | solution.py:382
  31.6 2.7 %collective-permute-start.13 = (f32[64,128]{1,0:T(8,128)S(1)}, f32[64,128]{1,0:T(8,128)S(1)}, u32[]{:S(2)}, u32[]{:S(2)}) collective-permute-start(f32[64,128]{1,0:T(8,128)S(1)} %get-tuple-element.42), channel_id=1, source_target_pairs={{0,24},{8,16},{16,8},{24,0},{1,25},{9,17},{17,9},{25,1},{2,26},{10... | collective-permute-start | bytes 98312 | tf_op jit(solution)/shard_map/ppermute | solution.py:382
  34.3 1.7 %collective-permute-start.11 = (f32[64,128]{1,0:T(8,128)S(1)}, f32[64,128]{1,0:T(8,128)S(1)}, u32[]{:S(2)}, u32[]{:S(2)}) collective-permute-start(f32[64,128]{1,0:T(8,128)S(1)} %get-tuple-element.42), channel_id=1, source_target_pairs={{0,8},{8,0},{16,24},{24,16},{1,9},{9,1},{17,25},{25,17},{2,10},{10... | collective-permute-start | bytes 98312 | tf_op jit(solution)/shard_map/ppermute | solution.py:382
  36.1 1.4 %collective-permute-done.13 = f32[64,128]{1,0:T(8,128)S(1)} collective-permute-done((f32[64,128]{1,0:T(8,128)S(1)}, f32[64,128]{1,0:T(8,128)S(1)}, u32[]{:S(2)}, u32[]{:S(2)}) %collective-permute-start.13) | collective-permute-done | bytes 32800 | tf_op jit(solution)/shard_map/ppermute | solution.py:382
  37.5 1.6 %collective-permute-done.12 = f32[64,128]{1,0:T(8,128)S(1)} collective-permute-done((f32[64,128]{1,0:T(8,128)S(1)}, f32[64,128]{1,0:T(8,128)S(1)}, u32[]{:S(2)}, u32[]{:S(2)}) %collective-permute-start.12) | collective-permute-done | bytes 32800 | tf_op jit(solution)/shard_map/ppermute | solution.py:382
  39.1 1.1 %collective-permute-start.16 = (f32[256,128]{1,0:T(8,128)S(1)}, f32[256,128]{1,0:T(8,128)S(1)}, u32[]{:S(2)}, u32[]{:S(2)}) collective-permute-start(f32[256,128]{1,0:T(8,128)S(1)} %pad_maximum_fusion.2), channel_id=1, source_target_pairs={{0,6},{2,4},{4,2},{6,0},{1,7},{3,5},{5,3},{7,1},{8,14},{10,12},{12... | collective-permute-start | bytes 393224 | tf_op jit(solution)/shard_map/ppermute | solution.py:382
  40.3 1.9 %collective-permute-start.15 = (f32[256,128]{1,0:T(8,128)S(1)}, f32[256,128]{1,0:T(8,128)S(1)}, u32[]{:S(2)}, u32[]{:S(2)}) collective-permute-start(f32[256,128]{1,0:T(8,128)S(1)} %pad_maximum_fusion.2), channel_id=1, source_target_pairs={{0,4},{2,6},{4,0},{6,2},{1,5},{3,7},{5,1},{7,3},{8,12},{10,14},{12... | collective-permute-start | bytes 393224 | tf_op jit(solution)/shard_map/ppermute | solution.py:382
  42.2 0.5 collective-permute-start.14
  42.7 7.3 %factor.1 = (bf16[256,768]{1,0:T(8,128)(2,1)S(1)}, bf16[384,768]{1,0:T(8,128)(2,1)S(1)}, f32[384,256]{1,0:T(8,128)}) custom-call(s32[1]{0:T(128)} %bitcast.place_ref, s32[1]{0:T(128)S(6)} %copy.8.live_ref, f32[4,64,128]{2,1,0:T(8,128)S(1)} %pad_maximum_fusion.1.own_ref, f32[4,64,128]{2,1,0:T(8,128)S(1)} %collective-permute-done.10.other_ref, ...), custom_call_target="tpu_custom_call" | custom-call | flops 6000000000 | bytes 393216 | tf_op jit(solution)/shard_map/factor/pallas_call | solution.py:298
  50.1 2.1 %rest_own.1 = (f32[256,256]{1,0:T(8,128)S(1)}, f32[384,1024]{1,0:T(8,128)}) custom-call(s32[1]{0:T(128)} %bitcast.place_ref, s32[1]{0:T(128)S(6)} %copy.8.live_ref, bf16[256,768]{1,0:T(8,128)(2,1)S(1)} %get-tuple-element.25.inverse_ref, bf16[384,768]{1,0:T(8,128)(2,1)S(1)} %get-tuple-element.26.unit_ref, f32[4,256,128]{2,1,0:T(8,128)S(1)} %pad_maximum_fusion.cross_ref, ...), custom_call_target="tpu_custom_call" | custom-call | flops 1006632960 | bytes 1572864 | tf_op jit(solution)/shard_map/rest_own/pallas_call | solution.py:359
  52.2 2.8 %rest_other.1 = (f32[256,256]{1,0:T(8,128)}, f32[384,1024]{1,0:T(8,128)}) custom-call(s32[1]{0:T(128)} %bitcast.place_ref, s32[1]{0:T(128)S(6)} %copy.8.live_ref, bf16[256,768]{1,0:T(8,128)(2,1)S(1)} %get-tuple-element.25.inverse_ref, bf16[384,768]{1,0:T(8,128)(2,1)S(1)} %get-tuple-element.26.unit_ref, ...), custom_call_target="tpu_custom_call", output_to_operand_aliasing={{1}: (7, {})} | custom-call | flops 1006632960 | bytes 1572864 | tf_op jit(solution)/shard_map/rest_other/pallas_call | solution.py:359
  (31 shorter events, 1.2 us)
Async XLA Ops:
  4.0 2.2 %collective-permute-start = (f32[4,320,128]{2,1,0:T(8,128)S(1)}, f32[4,320,128]{2,1,0:T(8,128)S(1)}, u32[]{:S(2)}, u32[]{:S(2)}) collective-permute-start(f32[4,320,128]{2,1,0:T(8,128)S(1)} %get-tuple-element.22), channel_id=1, source_target_pairs={{0,1},{1,0},{2,3},{3,2},{4,5},{5,4},{6,7},{7,6},{8,9},{9,8},{10,11... | collective-permute-start | bytes 1966088 | tf_op jit(solution)/shard_map/ppermute | solution.py:378
  6.4 36.4 %copy-start.1 = (f32[384,256]{1,0:T(8,128)S(1)}, f32[384,256]{1,0:T(8,128)}, u32[]{:S(2)}) copy-start(f32[384,256]{1,0:T(8,128)} %panel_ref.3) | copy-start | bytes 1179652
  6.4 8.9 %collective-permute-start.3 = (f32[320,128]{1,0:T(8,128)S(1)}, f32[320,128]{1,0:T(8,128)S(1)}, u32[]{:S(2)}, u32[]{:S(2)}) collective-permute-start(f32[320,128]{1,0:T(8,128)S(1)} %get-tuple-element.35), channel_id=1, source_target_pairs={{0,6},{2,4},{4,2},{6,0},{1,7},{3,5},{5,3},{7,1},{8,14},{10,12},{12... | collective-permute-start | bytes 491528 | tf_op jit(solution)/shard_map/ppermute | solution.py:382
  10.3 8.0 %collective-permute-start.2 = (f32[320,128]{1,0:T(8,128)S(1)}, f32[320,128]{1,0:T(8,128)S(1)}, u32[]{:S(2)}, u32[]{:S(2)}) collective-permute-start(f32[320,128]{1,0:T(8,128)S(1)} %get-tuple-element.36), channel_id=1, source_target_pairs={{0,4},{2,6},{4,0},{6,2},{1,5},{3,7},{5,1},{7,3},{8,12},{10,14},{12... | collective-permute-start | bytes 491528 | tf_op jit(solution)/shard_map/ppermute | solution.py:382
  10.8 7.8 %collective-permute-start.1 = (f32[320,128]{1,0:T(8,128)S(1)}, f32[320,128]{1,0:T(8,128)S(1)}, u32[]{:S(2)}, u32[]{:S(2)}) collective-permute-start(f32[320,128]{1,0:T(8,128)S(1)} %get-tuple-element.37), channel_id=1, source_target_pairs={{0,2},{2,0},{4,6},{6,4},{1,3},{3,1},{5,7},{7,5},{8,10},{10,8},{12,... | collective-permute-start | bytes 491528 | tf_op jit(solution)/shard_map/ppermute | solution.py:382
  18.7 6.6 %collective-permute-start.6 = (f32[128,128]{1,0:T(8,128)S(1)}, f32[128,128]{1,0:T(8,128)S(1)}, u32[]{:S(2)}, u32[]{:S(2)}) collective-permute-start(f32[128,128]{1,0:T(8,128)S(1)} %get-tuple-element.45), channel_id=1, source_target_pairs={{0,24},{8,16},{16,8},{24,0},{1,25},{9,17},{17,9},{25,1},{2,26},{10... | collective-permute-start | bytes 196616 | tf_op jit(solution)/shard_map/ppermute | solution.py:382
  22.3 5.7 %collective-permute-start.5 = (f32[128,128]{1,0:T(8,128)S(1)}, f32[128,128]{1,0:T(8,128)S(1)}, u32[]{:S(2)}, u32[]{:S(2)}) collective-permute-start(f32[128,128]{1,0:T(8,128)S(1)} %get-tuple-element.46), channel_id=1, source_target_pairs={{0,16},{8,24},{16,0},{24,8},{1,17},{9,25},{17,1},{25,9},{2,18},{10... | collective-permute-start | bytes 196616 | tf_op jit(solution)/shard_map/ppermute | solution.py:382
  22.3 5.7 %collective-permute-start.4 = (f32[128,128]{1,0:T(8,128)S(1)}, f32[128,128]{1,0:T(8,128)S(1)}, u32[]{:S(2)}, u32[]{:S(2)}) collective-permute-start(f32[128,128]{1,0:T(8,128)S(1)} %get-tuple-element.47), channel_id=1, source_target_pairs={{0,8},{8,0},{16,24},{24,16},{1,9},{9,1},{17,25},{25,17},{2,10},{10... | collective-permute-start | bytes 196616 | tf_op jit(solution)/shard_map/ppermute | solution.py:382
  28.1 6.2 %collective-permute-start.8 = (f32[64,128]{1,0:T(8,128)S(1)}, f32[64,128]{1,0:T(8,128)S(1)}, u32[]{:S(2)}, u32[]{:S(2)}) collective-permute-start(f32[64,128]{1,0:T(8,128)S(1)} %get-tuple-element.44), channel_id=1, source_target_pairs={{0,4},{2,6},{4,0},{6,2},{1,5},{3,7},{5,1},{7,3},{8,12},{10,14},{12... | collective-permute-start | bytes 98312 | tf_op jit(solution)/shard_map/ppermute | solution.py:382
  29.7 6.4 %collective-permute-start.7 = (f32[64,128]{1,0:T(8,128)S(1)}, f32[64,128]{1,0:T(8,128)S(1)}, u32[]{:S(2)}, u32[]{:S(2)}) collective-permute-start(f32[64,128]{1,0:T(8,128)S(1)} %get-tuple-element.44), channel_id=1, source_target_pairs={{0,2},{2,0},{4,6},{6,4},{1,3},{3,1},{5,7},{7,5},{8,10},{10,8},{12,... | collective-permute-start | bytes 98312 | tf_op jit(solution)/shard_map/ppermute | solution.py:382
  30.0 6.1 %collective-permute-start.9 = (f32[64,128]{1,0:T(8,128)S(1)}, f32[64,128]{1,0:T(8,128)S(1)}, u32[]{:S(2)}, u32[]{:S(2)}) collective-permute-start(f32[64,128]{1,0:T(8,128)S(1)} %get-tuple-element.44), channel_id=1, source_target_pairs={{0,6},{2,4},{4,2},{6,0},{1,7},{3,5},{5,3},{7,1},{8,14},{10,12},{12... | collective-permute-start | bytes 98312 | tf_op jit(solution)/shard_map/ppermute | solution.py:382
  31.6 5.9 %collective-permute-start.13 = (f32[64,128]{1,0:T(8,128)S(1)}, f32[64,128]{1,0:T(8,128)S(1)}, u32[]{:S(2)}, u32[]{:S(2)}) collective-permute-start(f32[64,128]{1,0:T(8,128)S(1)} %get-tuple-element.42), channel_id=1, source_target_pairs={{0,24},{8,16},{16,8},{24,0},{1,25},{9,17},{17,9},{25,1},{2,26},{10... | collective-permute-start | bytes 98312 | tf_op jit(solution)/shard_map/ppermute | solution.py:382
  34.3 4.8 %collective-permute-start.12 = (f32[64,128]{1,0:T(8,128)S(1)}, f32[64,128]{1,0:T(8,128)S(1)}, u32[]{:S(2)}, u32[]{:S(2)}) collective-permute-start(f32[64,128]{1,0:T(8,128)S(1)} %get-tuple-element.42), channel_id=1, source_target_pairs={{0,16},{8,24},{16,0},{24,8},{1,17},{9,25},{17,1},{25,9},{2,18},{10... | collective-permute-start | bytes 98312 | tf_op jit(solution)/shard_map/ppermute | solution.py:382
  34.3 4.8 %collective-permute-start.11 = (f32[64,128]{1,0:T(8,128)S(1)}, f32[64,128]{1,0:T(8,128)S(1)}, u32[]{:S(2)}, u32[]{:S(2)}) collective-permute-start(f32[64,128]{1,0:T(8,128)S(1)} %get-tuple-element.42), channel_id=1, source_target_pairs={{0,8},{8,0},{16,24},{24,16},{1,9},{9,1},{17,25},{25,17},{2,10},{10... | collective-permute-start | bytes 98312 | tf_op jit(solution)/shard_map/ppermute | solution.py:382
  36.0 6.7 %collective-permute-start.10 = (f32[4,64,128]{2,1,0:T(8,128)S(1)}, f32[4,64,128]{2,1,0:T(8,128)S(1)}, u32[]{:S(2)}, u32[]{:S(2)}) collective-permute-start(f32[4,64,128]{2,1,0:T(8,128)S(1)} %pad_maximum_fusion.1.own_ref), channel_id=1, source_target_pairs={{0,1},{1,0},{2,3},{3,2},{4,5},{5,4},{6,7},{7,6},{8,9},{9,8},{10,11... | collective-permute-start | bytes 393224 | tf_op jit(solution)/shard_map/ppermute | solution.py:378
  39.1 11.0 %copy-start = (f32[384,1024]{1,0:T(8,128)S(1)}, f32[384,1024]{1,0:T(8,128)}, u32[]{:S(2)}) copy-start(f32[384,1024]{1,0:T(8,128)} %trail_ref.5) | copy-start | bytes 4718596
  39.1 10.9 %collective-permute-start.16 = (f32[256,128]{1,0:T(8,128)S(1)}, f32[256,128]{1,0:T(8,128)S(1)}, u32[]{:S(2)}, u32[]{:S(2)}) collective-permute-start(f32[256,128]{1,0:T(8,128)S(1)} %pad_maximum_fusion.2), channel_id=1, source_target_pairs={{0,6},{2,4},{4,2},{6,0},{1,7},{3,5},{5,3},{7,1},{8,14},{10,12},{12... | collective-permute-start | bytes 393224 | tf_op jit(solution)/shard_map/ppermute | solution.py:382
  40.3 9.7 %collective-permute-start.15 = (f32[256,128]{1,0:T(8,128)S(1)}, f32[256,128]{1,0:T(8,128)S(1)}, u32[]{:S(2)}, u32[]{:S(2)}) collective-permute-start(f32[256,128]{1,0:T(8,128)S(1)} %pad_maximum_fusion.2), channel_id=1, source_target_pairs={{0,4},{2,6},{4,0},{6,2},{1,5},{3,7},{5,1},{7,3},{8,12},{10,14},{12... | collective-permute-start | bytes 393224 | tf_op jit(solution)/shard_map/ppermute | solution.py:382
  42.2 7.8 %collective-permute-start.14 = (f32[256,128]{1,0:T(8,128)S(1)}, f32[256,128]{1,0:T(8,128)S(1)}, u32[]{:S(2)}, u32[]{:S(2)}) collective-permute-start(f32[256,128]{1,0:T(8,128)S(1)} %pad_maximum_fusion.2), channel_id=1, source_target_pairs={{0,2},{2,0},{4,6},{6,4},{1,3},{3,1},{5,7},{7,5},{8,10},{10,8},{12,... | collective-permute-start | bytes 393224 | tf_op jit(solution)/shard_map/ppermute | solution.py:382
  50.0 2.2 %collective-permute-start.17 = (f32[4,256,128]{2,1,0:T(8,128)S(1)}, f32[4,256,128]{2,1,0:T(8,128)S(1)}, u32[]{:S(2)}, u32[]{:S(2)}) collective-permute-start(f32[4,256,128]{2,1,0:T(8,128)S(1)} %pad_maximum_fusion.cross_ref), channel_id=1, source_target_pairs={{0,1},{1,0},{2,3},{3,2},{4,5},{5,4},{6,7},{7,6},{8,9},{9,8},{10,11... | collective-permute-start | bytes 1572872 | tf_op jit(solution)/shard_map/ppermute | solution.py:378

commit v5 on v4

--- a/solution.py
+++ b/solution.py
@@ -16,7 +16,8 @@
 LANES = 128
 BLOCK = 32
 BATCH = 16
-STRIP = 256
+STRIP = 512
+EXTRA = 8
 SMEM = pl.BlockSpec(memory_space=pltpu.SMEM)
 VMEM = pl.BlockSpec(memory_space=pltpu.VMEM)
 ANY = pl.BlockSpec(memory_space=pl.ANY)
@@ -68,27 +69,52 @@
     return pl.CostEstimate(flops=flops, bytes_accessed=transferred, transcendentals=0)
 
 
-def place_products(side, place_ref, live_ref, gram, cross, out_ref, cross_scr):
-    width = gram.shape[0]
+def place_products(place_ref, gram, cross, out_ref, cross_scr):
+    width = cross.shape[0]
     _, chip, depth = place_of(place_ref)
-    tall = width // SLOTS
+    tall = LANES // SLOTS
     part = width // PARTS
-    cross_scr[0] = gram
     for tile in range(SLOTS):
-        cross_scr[tile + 1] = cross[:, tile * LANES : (tile + 1) * LANES]
-
-    @pl.when(side == 0)
-    def _():
-        count = jnp.full((width - LANES, LANES), live_ref[0], jnp.int32)
-        cross_scr[0, LANES:, :] = count.astype(F32)
-
+        cross_scr[tile] = cross[:, tile * LANES : (tile + 1) * LANES]
     for slot in range(SLOTS):
         chunk = jnp.bitwise_xor(chip, slot)
-        out_ref[slot, :tall, :] = cross_scr[0, pl.ds(pl.multiple_of(chunk * tall, 8), tall), :]
+        out_ref[slot, :tall, :] = gram[pl.ds(pl.multiple_of(chunk * tall, 8), tall), :]
+        out_ref[slot, tall : tall + EXTRA, :] = gram[LANES:, :]
         for piece in range(PARTS):
             at = pl.multiple_of(jnp.bitwise_xor(depth, piece) * part, 8)
-            to = tall + piece * part
-            out_ref[slot, to : to + part, :] = cross_scr[chunk + 1, pl.ds(at, part), :]
+            to = tall + EXTRA + piece * part
+            out_ref[slot, to : to + part, :] = cross_scr[chunk, pl.ds(at, part), :]
+
+
+def triangle():
+    shape = (LANES, LANES)
+    row = lax.broadcasted_iota(jnp.int32, shape, 0)
+    column = lax.broadcasted_iota(jnp.int32, shape, 1)
+    return row, column
+
+
+def pack_gram(gram, live, gram_ref):
+    row, column = triangle()
+    second = gram[LANES:, LANES:]
+    gram_ref[0, :LANES, :] = gram[:LANES, LANES:]
+    gram_ref[1, :LANES, :] = jnp.where(row <= column, gram[:LANES, :LANES], second)
+    diagonal = jnp.sum(jnp.where(row == column, second, 0.0), axis=0, keepdims=True)
+    count = jnp.full((EXTRA, LANES), live, jnp.int32).astype(F32)
+    index = lax.broadcasted_iota(jnp.int32, (EXTRA, LANES), 0)
+    for side in range(2):
+        gram_ref[side, LANES:, :] = jnp.where(index == 0, diagonal, count)
+
+
+def unpack_gram(packed_ref, gram_ref):
+    row, column = triangle()
+    packed = packed_ref[1, :LANES, :]
+    turned = packed.T
+    diagonal = packed_ref[1, LANES : LANES + 1, :]
+    gram_ref[:LANES, :LANES] = jnp.where(row <= column, packed, turned)
+    gram_ref[:LANES, LANES:] = packed_ref[0, :LANES, :]
+    second = jnp.where(row > column, packed, turned)
+    gram_ref[LANES:, LANES:] = jnp.where(row == column, diagonal, second)
+    return packed_ref[1, LANES + 1 : LANES + 2, 0:1]
 
 
 def other_kernel(
@@ -113,36 +139,31 @@
     panel = masked(panel_scr, live_ref)
     left = left_of(panel.T, 1, 6)
     left_ref[...] = left[:, : 3 * rows]
-    gram = dot(left, right_of(panel, 6))
-    panel_scr[: gram.shape[0], :] = gram
-    own = pl.ds(pl.multiple_of(core * LANES, LANES), LANES)
-    rest = pl.ds(pl.multiple_of((1 - core) * LANES, LANES), LANES)
-    gram_ref[...] = panel_scr[: gram.shape[0], own]
+    pack_gram(dot(left, right_of(panel, 6)), live_ref[0], gram_ref)
     copy_trail.wait()
     cross = dot(left[:, : 3 * rows], right_of(masked(trail_scr, live_ref)))
-    gram = panel_scr[: gram.shape[0], rest]
-    place_products(1 - core, place_ref, live_ref, gram, cross, out_ref, cross_scr)
+    place_products(place_ref, gram_ref.at[1 - core], cross, out_ref, cross_scr)
     copy_half.wait()
 
 
 def own_kernel(place_ref, live_ref, left_ref, gram_ref, half_ref, out_ref, cross_scr):
     cross = dot(left_ref[...], right_of(masked(half_ref, live_ref)))
-    side = place_of(place_ref)[0]
-    place_products(side, place_ref, live_ref, gram_ref[...], cross, out_ref, cross_scr)
+    core = place_of(place_ref)[0]
+    place_products(place_ref, gram_ref.at[core], cross, out_ref, cross_scr)
 
 
 def products_of(place, live, panel, trail):
     rows, width = panel.shape
     columns = trail.shape[1]
-    out = struct(SLOTS, width // SLOTS + width, LANES)
+    out = struct(SLOTS, LANES // SLOTS + EXTRA + width, LANES)
     work = cost(6 * rows * width * columns // 2, 2 * rows * columns)
-    cross_scr = pltpu.VMEM((SLOTS + 1, width, LANES), F32)
+    cross_scr = pltpu.VMEM((SLOTS, width, LANES), F32)
     theirs, *handed = pl.pallas_call(
         other_kernel,
         out_shape=(
             out,
             jax.ShapeDtypeStruct((width, 3 * rows), BF16),
-            struct(width, LANES),
+            struct(2, LANES + EXTRA, LANES),
             struct(rows, columns // 2),
         ),
         in_specs=[SMEM, SMEM, HBM, HBM],
@@ -275,16 +296,21 @@
 
 def factor_kernel(
     place_ref, live_ref, own_ref, other_ref, panel_ref, left_ref, unit_ref, basis_ref,
-    gram_ref, inverse_ref,
+    gram_ref, inverse_ref, packed_ref,
 ):
     core, chip, _ = place_of(place_ref)
-    tall = own_ref.shape[1]
+    tall = LANES // SLOTS
     for side, ref in ((core, own_ref), (1 - core, other_ref)):
-        at = pl.ds(pl.multiple_of(side * LANES, LANES), LANES)
         for slot in range(SLOTS):
-            row = pl.multiple_of(jnp.bitwise_xor(chip, slot) * tall, 8)
-            gram_ref[pl.ds(row, tall), at] = ref[slot]
-    root = jnp.sqrt(gram_ref[LANES : LANES + 8, 0:LANES])[0:1, 0:1]
+            chunk = jnp.bitwise_xor(chip, slot)
+            row = pl.multiple_of(chunk * tall, 8)
+            packed_ref[side, pl.ds(row, tall), :] = ref[slot, :tall, :]
+
+            @pl.when(chunk == 0)
+            def _(side=side, ref=ref, slot=slot):
+                packed_ref[side, LANES:, :] = ref[slot, tall:, :]
+
+    root = jnp.sqrt(unpack_gram(packed_ref, gram_ref))
     factor_inverse(gram_ref, inverse_ref)
     inverse = inverse_ref[...]
     left_ref[...] = left_of(inverse, 1)
@@ -304,7 +330,8 @@
         ),
         in_specs=[SMEM, SMEM, VMEM, VMEM, VMEM],
         out_specs=(VMEM,) * 3,
-        scratch_shapes=[pltpu.VMEM((width, width), F32)] * 2,
+        scratch_shapes=[pltpu.VMEM((width, width), F32)] * 2
+        + [pltpu.VMEM((2, LANES + EXTRA, LANES), F32)],
         cost_estimate=cost(6 * 10**9, 4 * rows * width),
         compiler_params=PARAMS,
         name="factor",
@@ -391,7 +418,7 @@
     flat, deep = ("y", "x"), "z"
     wide = columns // (lax.axis_size("x") * 2)
     place = lax.axis_index(AXES)[None]
-    tall, part = width // SLOTS, width // PARTS
+    tall, part = LANES // SLOTS + EXTRA, width // PARTS
 
     theirs, ours = products_of(place, live_rows, panel, trailing)
     pair = ours + swap(theirs)

time: 55.2 us -> 53.2 us (0.964)
  waiting for transfers between devices: 16.7 us -> 15.3 us
    ppermute x15, waiting for transfers between devices: 15.6 us -> 14.1 us  [send(): return lax.ppermute(x, axes, [(i, i ^ shift) for i in range(size)])]
  transfers between devices with their start and end apart: 18 -> 18, of which waited for: 8 -> 9; matrix products, arithmetic and copies ran while one was open for 0% -> 0% of each run, Pallas kernels for 18% -> 18%
where the time goes in v5:
time: 53.2 us; the launch traced here: 53.1 us
  starting transfers between devices  21.1 us (40%)
  waiting for transfers between devices  15.3 us (29%)
  Pallas kernels  15 us (28%)
  between operations  1.43 us (3%)
    ppermute x15, starting transfers between devices, send(): return lax.ppermute(x, axes, [(i, i ^ shift) for i in range(size)])  20.5 us
    ppermute x15, waiting for transfers between devices, send(): return lax.ppermute(x, axes, [(i, i ^ shift) for i in range(size)])  14.1 us
    pallas_call x1, Pallas kernels, factor_of(): pl.pallas_call(factor_kernel, out_shape=(jax.ShapeDtypeStruct((width, 3 *...  7.36 us
    pallas_call x2, Pallas kernels, rest_of(): pl.pallas_call(functools.partial(rest_kernel, other), out_shape=(struct(w...  4.34 us
    pallas_call x1, Pallas kernels, products_of(): pl.pallas_call(other_kernel, out_shape=(out, jax.ShapeDtypeStruct((width,...  2.71 us
    ppermute x3, waiting for transfers between devices, swap(): return lax.ppermute(x, 'core', [(0, 1), (1, 0)])  1.12 us
  transfers between devices with their start and end apart: 18, of which 9 were waited for; matrix products, arithmetic and copies ran while one was open for 0% of the time, Pallas kernels for 18%

profile of v5, /device:TPU:0, one launch (start us, length us, event | category | flops | bytes accessed | tf_op | source)
XLA Modules:
  0.0 53.1 jit_solution(18138972979214595713)
XLA Ops:
  1.3 2.7 %products_other.1 = (f32[4,296,128]{2,1,0:T(8,128)S(1)}, bf16[256,1152]{1,0:T(8,128)(2,1)S(1)}, f32[2,136,128]{2,1,0:T(8,128)S(1)}, f32[384,512]{1,0:T(8,128)S(1)}) custom-call(s32[1]{0:T(128)} %bitcast.place_ref, s32[1]{0:T(128)S(6)} %copy.8.live_ref, f32[384,256]{1,0:T(8,128)} %panel_ref.3, f32[384,1024]{1,0:T(8,128)} %trail_ref.5), custom_call_target="tpu_custom_call" | custom-call | flops 301989888 | bytes 786432 | tf_op jit(solution)/shard_map/products_other/pallas_call | solution.py:161
  4.0 0.5 collective-permute-start
  4.5 0.6 %products_own.1 = f32[4,296,128]{2,1,0:T(8,128)S(1)} custom-call(s32[1]{0:T(128)} %bitcast.place_ref, s32[1]{0:T(128)S(6)} %copy.8.live_ref, bf16[256,1152]{1,0:T(8,128)(2,1)S(1)} %get-tuple-element.19.left_ref, f32[2,136,128]{2,1,0:T(8,128)S(1)} %get-tuple-element.20.gram_ref, f32[384,512]{1,0:T(8,128)S(1)} %get-tuple-element.21.half_ref), custom_call_target="tpu_custom_call" | custom-call | flops 301989888 | bytes 786432 | tf_op jit(solution)/shard_map/products_own/pallas_call | solution.py:181
  5.1 1.1 %collective-permute-done = f32[4,296,128]{2,1,0:T(8,128)S(1)} collective-permute-done((f32[4,296,128]{2,1,0:T(8,128)S(1)}, f32[4,296,128]{2,1,0:T(8,128)S(1)}, u32[]{:S(2)}, u32[]{:S(2)}) %collective-permute-start) | collective-permute-done | bytes 606240 | tf_op jit(solution)/shard_map/ppermute | solution.py:405
  6.3 3.9 %collective-permute-start.3 = (f32[296,128]{1,0:T(8,128)S(1)}, f32[296,128]{1,0:T(8,128)S(1)}, u32[]{:S(2)}, u32[]{:S(2)}) collective-permute-start(f32[296,128]{1,0:T(8,128)S(1)} %get-tuple-element.35), channel_id=1, source_target_pairs={{0,6},{2,4},{4,2},{6,0},{1,7},{3,5},{5,3},{7,1},{8,14},{10,12},{12... | collective-permute-start | bytes 454664 | tf_op jit(solution)/shard_map/ppermute | solution.py:409
  10.8 4.1 %collective-permute-done.3 = f32[296,128]{1,0:T(8,128)S(1)} collective-permute-done((f32[296,128]{1,0:T(8,128)S(1)}, f32[296,128]{1,0:T(8,128)S(1)}, u32[]{:S(2)}, u32[]{:S(2)}) %collective-permute-start.3) | collective-permute-done | bytes 151584 | tf_op jit(solution)/shard_map/ppermute | solution.py:409
  14.9 2.8 %collective-permute-done.2 = f32[296,128]{1,0:T(8,128)S(1)} collective-permute-done((f32[296,128]{1,0:T(8,128)S(1)}, f32[296,128]{1,0:T(8,128)S(1)}, u32[]{:S(2)}, u32[]{:S(2)}) %collective-permute-start.2) | collective-permute-done | bytes 151584 | tf_op jit(solution)/shard_map/ppermute | solution.py:409
  18.0 3.7 %collective-permute-start.6 = (f32[104,128]{1,0:T(8,128)S(1)}, f32[104,128]{1,0:T(8,128)S(1)}, u32[]{:S(2)}, u32[]{:S(2)}) collective-permute-start(f32[104,128]{1,0:T(8,128)S(1)} %get-tuple-element.43), channel_id=1, source_target_pairs={{0,24},{8,16},{16,8},{24,0},{1,25},{9,17},{17,9},{25,1},{2,26},{10... | collective-permute-start | bytes 159752 | tf_op jit(solution)/shard_map/ppermute | solution.py:409
  21.7 0.8 %collective-permute-start.4 = (f32[104,128]{1,0:T(8,128)S(1)}, f32[104,128]{1,0:T(8,128)S(1)}, u32[]{:S(2)}, u32[]{:S(2)}) collective-permute-start(f32[104,128]{1,0:T(8,128)S(1)} %get-tuple-element.45), channel_id=1, source_target_pairs={{0,8},{8,0},{16,24},{24,16},{1,9},{9,1},{17,25},{25,17},{2,10},{10... | collective-permute-start | bytes 159752 | tf_op jit(solution)/shard_map/ppermute | solution.py:409
  22.5 1.9 %collective-permute-done.6 = f32[104,128]{1,0:T(8,128)S(1)} collective-permute-done((f32[104,128]{1,0:T(8,128)S(1)}, f32[104,128]{1,0:T(8,128)S(1)}, u32[]{:S(2)}, u32[]{:S(2)}) %collective-permute-start.6) | collective-permute-done | bytes 53280 | tf_op jit(solution)/shard_map/ppermute | solution.py:409
  24.4 2.3 %collective-permute-done.5 = f32[104,128]{1,0:T(8,128)S(1)} collective-permute-done((f32[104,128]{1,0:T(8,128)S(1)}, f32[104,128]{1,0:T(8,128)S(1)}, u32[]{:S(2)}, u32[]{:S(2)}) %collective-permute-start.5) | collective-permute-done | bytes 53280 | tf_op jit(solution)/shard_map/ppermute | solution.py:409
  26.8 1.5 %collective-permute-start.8 = (f32[40,128]{1,0:T(8,128)S(1)}, f32[40,128]{1,0:T(8,128)S(1)}, u32[]{:S(2)}, u32[]{:S(2)}) collective-permute-start(f32[40,128]{1,0:T(8,128)S(1)} %get-tuple-element.42), channel_id=1, source_target_pairs={{0,4},{2,6},{4,0},{6,2},{1,5},{3,7},{5,1},{7,3},{8,12},{10,14},{12... | collective-permute-start | bytes 61448 | tf_op jit(solution)/shard_map/ppermute | solution.py:409
  28.3 0.8 %collective-permute-start.7 = (f32[40,128]{1,0:T(8,128)S(1)}, f32[40,128]{1,0:T(8,128)S(1)}, u32[]{:S(2)}, u32[]{:S(2)}) collective-permute-start(f32[40,128]{1,0:T(8,128)S(1)} %get-tuple-element.42), channel_id=1, source_target_pairs={{0,2},{2,0},{4,6},{6,4},{1,3},{3,1},{5,7},{7,5},{8,10},{10,8},{12,... | collective-permute-start | bytes 61448 | tf_op jit(solution)/shard_map/ppermute | solution.py:409
  29.1 1.3 %collective-permute-start.9 = (f32[40,128]{1,0:T(8,128)S(1)}, f32[40,128]{1,0:T(8,128)S(1)}, u32[]{:S(2)}, u32[]{:S(2)}) collective-permute-start(f32[40,128]{1,0:T(8,128)S(1)} %get-tuple-element.42), channel_id=1, source_target_pairs={{0,6},{2,4},{4,2},{6,0},{1,7},{3,5},{5,3},{7,1},{8,14},{10,12},{12... | collective-permute-start | bytes 61448 | tf_op jit(solution)/shard_map/ppermute | solution.py:409
  30.3 2.4 %collective-permute-start.13 = (f32[64,128]{1,0:T(8,128)S(1)}, f32[64,128]{1,0:T(8,128)S(1)}, u32[]{:S(2)}, u32[]{:S(2)}) collective-permute-start(f32[64,128]{1,0:T(8,128)S(1)} %slice.51), channel_id=1, source_target_pairs={{0,24},{8,16},{16,8},{24,0},{1,25},{9,17},{17,9},{25,1},{2,26},{10... | collective-permute-start | bytes 98312 | tf_op jit(solution)/shard_map/ppermute | solution.py:409
  32.8 2.0 %collective-permute-start.11 = (f32[64,128]{1,0:T(8,128)S(1)}, f32[64,128]{1,0:T(8,128)S(1)}, u32[]{:S(2)}, u32[]{:S(2)}) collective-permute-start(f32[64,128]{1,0:T(8,128)S(1)} %slice.51), channel_id=1, source_target_pairs={{0,8},{8,0},{16,24},{24,16},{1,9},{9,1},{17,25},{25,17},{2,10},{10... | collective-permute-start | bytes 98312 | tf_op jit(solution)/shard_map/ppermute | solution.py:409
  34.8 1.2 %collective-permute-done.13 = f32[64,128]{1,0:T(8,128)S(1)} collective-permute-done((f32[64,128]{1,0:T(8,128)S(1)}, f32[64,128]{1,0:T(8,128)S(1)}, u32[]{:S(2)}, u32[]{:S(2)}) %collective-permute-start.13) | collective-permute-done | bytes 32800 | tf_op jit(solution)/shard_map/ppermute | solution.py:409
  36.1 1.5 %collective-permute-done.12 = f32[64,128]{1,0:T(8,128)S(1)} collective-permute-done((f32[64,128]{1,0:T(8,128)S(1)}, f32[64,128]{1,0:T(8,128)S(1)}, u32[]{:S(2)}, u32[]{:S(2)}) %collective-permute-start.12) | collective-permute-done | bytes 32800 | tf_op jit(solution)/shard_map/ppermute | solution.py:409
  37.6 1.5 %collective-permute-start.16 = (f32[256,128]{1,0:T(8,128)S(1)}, f32[256,128]{1,0:T(8,128)S(1)}, u32[]{:S(2)}, u32[]{:S(2)}) collective-permute-start(f32[256,128]{1,0:T(8,128)S(1)} %pad_maximum_fusion.1), channel_id=1, source_target_pairs={{0,6},{2,4},{4,2},{6,0},{1,7},{3,5},{5,3},{7,1},{8,14},{10,12},{12... | collective-permute-start | bytes 393224 | tf_op jit(solution)/shard_map/ppermute | solution.py:409
  39.1 1.5 %collective-permute-start.15 = (f32[256,128]{1,0:T(8,128)S(1)}, f32[256,128]{1,0:T(8,128)S(1)}, u32[]{:S(2)}, u32[]{:S(2)}) collective-permute-start(f32[256,128]{1,0:T(8,128)S(1)} %pad_maximum_fusion.1), channel_id=1, source_target_pairs={{0,4},{2,6},{4,0},{6,2},{1,5},{3,7},{5,1},{7,3},{8,12},{10,14},{12... | collective-permute-start | bytes 393224 | tf_op jit(solution)/shard_map/ppermute | solution.py:409
  40.6 0.5 %collective-permute-start.14 = (f32[256,128]{1,0:T(8,128)S(1)}, f32[256,128]{1,0:T(8,128)S(1)}, u32[]{:S(2)}, u32[]{:S(2)}) collective-permute-start(f32[256,128]{1,0:T(8,128)S(1)} %pad_maximum_fusion.1), channel_id=1, source_target_pairs={{0,2},{2,0},{4,6},{6,4},{1,3},{3,1},{5,7},{7,5},{8,10},{10,8},{12,... | collective-permute-start | bytes 393224 | tf_op jit(solution)/shard_map/ppermute | solution.py:409
  41.2 7.4 %factor.1 = (bf16[256,768]{1,0:T(8,128)(2,1)S(1)}, bf16[384,768]{1,0:T(8,128)(2,1)S(1)}, f32[384,256]{1,0:T(8,128)}) custom-call(s32[1]{0:T(128)} %bitcast.place_ref, s32[1]{0:T(128)S(6)} %copy.8.live_ref, f32[4,40,128]{2,1,0:T(8,128)S(1)} %pad_maximum_fusion.2.own_ref, f32[4,40,128]{2,1,0:T(8,128)S(1)} %collective-permute-done.10.other_ref, ...), custom_call_target="tpu_custom_call" | custom-call | flops 6000000000 | bytes 393216 | tf_op jit(solution)/shard_map/factor/pallas_call | solution.py:324
  48.7 1.8 %rest_own.1 = (f32[256,256]{1,0:T(8,128)S(1)}, f32[384,1024]{1,0:T(8,128)}) custom-call(s32[1]{0:T(128)} %bitcast.place_ref, s32[1]{0:T(128)S(6)} %copy.8.live_ref, bf16[256,768]{1,0:T(8,128)(2,1)S(1)} %get-tuple-element.25.inverse_ref, bf16[384,768]{1,0:T(8,128)(2,1)S(1)} %get-tuple-element.26.unit_ref, f32[4,256,128]{2,1,0:T(8,128)S(1)} %pad_maximum_fusion.cross_ref, ...), custom_call_target="tpu_custom_call" | custom-call | flops 1006632960 | bytes 1572864 | tf_op jit(solution)/shard_map/rest_own/pallas_call | solution.py:386
  50.6 2.5 %rest_other.1 = (f32[256,256]{1,0:T(8,128)}, f32[384,1024]{1,0:T(8,128)}) custom-call(s32[1]{0:T(128)} %bitcast.place_ref, s32[1]{0:T(128)S(6)} %copy.8.live_ref, bf16[256,768]{1,0:T(8,128)(2,1)S(1)} %get-tuple-element.25.inverse_ref, bf16[384,768]{1,0:T(8,128)(2,1)S(1)} %get-tuple-element.26.unit_ref, ...), custom_call_target="tpu_custom_call", output_to_operand_aliasing={{1}: (7, {})} | custom-call | flops 1006632960 | bytes 1572864 | tf_op jit(solution)/shard_map/rest_other/pallas_call | solution.py:386
  (33 shorter events, 1.4 us)
Async XLA Ops:
  4.0 2.2 %collective-permute-start = (f32[4,296,128]{2,1,0:T(8,128)S(1)}, f32[4,296,128]{2,1,0:T(8,128)S(1)}, u32[]{:S(2)}, u32[]{:S(2)}) collective-permute-start(f32[4,296,128]{2,1,0:T(8,128)S(1)} %get-tuple-element.22), channel_id=1, source_target_pairs={{0,1},{1,0},{2,3},{3,2},{4,5},{5,4},{6,7},{7,6},{8,9},{9,8},{10,11... | collective-permute-start | bytes 1818632 | tf_op jit(solution)/shard_map/ppermute | solution.py:405
  6.2 34.9 %copy-start.1 = (f32[384,256]{1,0:T(8,128)S(1)}, f32[384,256]{1,0:T(8,128)}, u32[]{:S(2)}) copy-start(f32[384,256]{1,0:T(8,128)} %panel_ref.3) | copy-start | bytes 1179652
  6.3 8.6 %collective-permute-start.3 = (f32[296,128]{1,0:T(8,128)S(1)}, f32[296,128]{1,0:T(8,128)S(1)}, u32[]{:S(2)}, u32[]{:S(2)}) collective-permute-start(f32[296,128]{1,0:T(8,128)S(1)} %get-tuple-element.35), channel_id=1, source_target_pairs={{0,6},{2,4},{4,2},{6,0},{1,7},{3,5},{5,3},{7,1},{8,14},{10,12},{12... | collective-permute-start | bytes 454664 | tf_op jit(solution)/shard_map/ppermute | solution.py:409
  10.2 7.5 %collective-permute-start.2 = (f32[296,128]{1,0:T(8,128)S(1)}, f32[296,128]{1,0:T(8,128)S(1)}, u32[]{:S(2)}, u32[]{:S(2)}) collective-permute-start(f32[296,128]{1,0:T(8,128)S(1)} %get-tuple-element.36), channel_id=1, source_target_pairs={{0,4},{2,6},{4,0},{6,2},{1,5},{3,7},{5,1},{7,3},{8,12},{10,14},{12... | collective-permute-start | bytes 454664 | tf_op jit(solution)/shard_map/ppermute | solution.py:409
  10.7 7.3 %collective-permute-start.1 = (f32[296,128]{1,0:T(8,128)S(1)}, f32[296,128]{1,0:T(8,128)S(1)}, u32[]{:S(2)}, u32[]{:S(2)}) collective-permute-start(f32[296,128]{1,0:T(8,128)S(1)} %get-tuple-element.37), channel_id=1, source_target_pairs={{0,2},{2,0},{4,6},{6,4},{1,3},{3,1},{5,7},{7,5},{8,10},{10,8},{12,... | collective-permute-start | bytes 454664 | tf_op jit(solution)/shard_map/ppermute | solution.py:409
  18.0 6.4 %collective-permute-start.6 = (f32[104,128]{1,0:T(8,128)S(1)}, f32[104,128]{1,0:T(8,128)S(1)}, u32[]{:S(2)}, u32[]{:S(2)}) collective-permute-start(f32[104,128]{1,0:T(8,128)S(1)} %get-tuple-element.43), channel_id=1, source_target_pairs={{0,24},{8,16},{16,8},{24,0},{1,25},{9,17},{17,9},{25,1},{2,26},{10... | collective-permute-start | bytes 159752 | tf_op jit(solution)/shard_map/ppermute | solution.py:409
  21.7 5.0 %collective-permute-start.5 = (f32[104,128]{1,0:T(8,128)S(1)}, f32[104,128]{1,0:T(8,128)S(1)}, u32[]{:S(2)}, u32[]{:S(2)}) collective-permute-start(f32[104,128]{1,0:T(8,128)S(1)} %get-tuple-element.44), channel_id=1, source_target_pairs={{0,16},{8,24},{16,0},{24,8},{1,17},{9,25},{17,1},{25,9},{2,18},{10... | collective-permute-start | bytes 159752 | tf_op jit(solution)/shard_map/ppermute | solution.py:409
  21.7 5.0 %collective-permute-start.4 = (f32[104,128]{1,0:T(8,128)S(1)}, f32[104,128]{1,0:T(8,128)S(1)}, u32[]{:S(2)}, u32[]{:S(2)}) collective-permute-start(f32[104,128]{1,0:T(8,128)S(1)} %get-tuple-element.45), channel_id=1, source_target_pairs={{0,8},{8,0},{16,24},{24,16},{1,9},{9,1},{17,25},{25,17},{2,10},{10... | collective-permute-start | bytes 159752 | tf_op jit(solution)/shard_map/ppermute | solution.py:409
  26.8 6.0 %collective-permute-start.8 = (f32[40,128]{1,0:T(8,128)S(1)}, f32[40,128]{1,0:T(8,128)S(1)}, u32[]{:S(2)}, u32[]{:S(2)}) collective-permute-start(f32[40,128]{1,0:T(8,128)S(1)} %get-tuple-element.42), channel_id=1, source_target_pairs={{0,4},{2,6},{4,0},{6,2},{1,5},{3,7},{5,1},{7,3},{8,12},{10,14},{12... | collective-permute-start | bytes 61448 | tf_op jit(solution)/shard_map/ppermute | solution.py:409
  28.3 6.5 %collective-permute-start.7 = (f32[40,128]{1,0:T(8,128)S(1)}, f32[40,128]{1,0:T(8,128)S(1)}, u32[]{:S(2)}, u32[]{:S(2)}) collective-permute-start(f32[40,128]{1,0:T(8,128)S(1)} %get-tuple-element.42), channel_id=1, source_target_pairs={{0,2},{2,0},{4,6},{6,4},{1,3},{3,1},{5,7},{7,5},{8,10},{10,8},{12,... | collective-permute-start | bytes 61448 | tf_op jit(solution)/shard_map/ppermute | solution.py:409
  29.1 5.7 %collective-permute-start.9 = (f32[40,128]{1,0:T(8,128)S(1)}, f32[40,128]{1,0:T(8,128)S(1)}, u32[]{:S(2)}, u32[]{:S(2)}) collective-permute-start(f32[40,128]{1,0:T(8,128)S(1)} %get-tuple-element.42), channel_id=1, source_target_pairs={{0,6},{2,4},{4,2},{6,0},{1,7},{3,5},{5,3},{7,1},{8,14},{10,12},{12... | collective-permute-start | bytes 61448 | tf_op jit(solution)/shard_map/ppermute | solution.py:409
  30.3 5.7 %collective-permute-start.13 = (f32[64,128]{1,0:T(8,128)S(1)}, f32[64,128]{1,0:T(8,128)S(1)}, u32[]{:S(2)}, u32[]{:S(2)}) collective-permute-start(f32[64,128]{1,0:T(8,128)S(1)} %slice.51), channel_id=1, source_target_pairs={{0,24},{8,16},{16,8},{24,0},{1,25},{9,17},{17,9},{25,1},{2,26},{10... | collective-permute-start | bytes 98312 | tf_op jit(solution)/shard_map/ppermute | solution.py:409
  32.8 4.8 %collective-permute-start.12 = (f32[64,128]{1,0:T(8,128)S(1)}, f32[64,128]{1,0:T(8,128)S(1)}, u32[]{:S(2)}, u32[]{:S(2)}) collective-permute-start(f32[64,128]{1,0:T(8,128)S(1)} %slice.51), channel_id=1, source_target_pairs={{0,16},{8,24},{16,0},{24,8},{1,17},{9,25},{17,1},{25,9},{2,18},{10... | collective-permute-start | bytes 98312 | tf_op jit(solution)/shard_map/ppermute | solution.py:409
  32.8 4.8 %collective-permute-start.11 = (f32[64,128]{1,0:T(8,128)S(1)}, f32[64,128]{1,0:T(8,128)S(1)}, u32[]{:S(2)}, u32[]{:S(2)}) collective-permute-start(f32[64,128]{1,0:T(8,128)S(1)} %slice.51), channel_id=1, source_target_pairs={{0,8},{8,0},{16,24},{24,16},{1,9},{9,1},{17,25},{25,17},{2,10},{10... | collective-permute-start | bytes 98312 | tf_op jit(solution)/shard_map/ppermute | solution.py:409
  34.7 6.4 %collective-permute-start.10 = (f32[4,40,128]{2,1,0:T(8,128)S(1)}, f32[4,40,128]{2,1,0:T(8,128)S(1)}, u32[]{:S(2)}, u32[]{:S(2)}) collective-permute-start(f32[4,40,128]{2,1,0:T(8,128)S(1)} %pad_maximum_fusion.2.own_ref), channel_id=1, source_target_pairs={{0,1},{1,0},{2,3},{3,2},{4,5},{5,4},{6,7},{7,6},{8,9},{9,8},{10,11... | collective-permute-start | bytes 245768 | tf_op jit(solution)/shard_map/ppermute | solution.py:405
  37.6 11.1 %copy-start = (f32[384,1024]{1,0:T(8,128)S(1)}, f32[384,1024]{1,0:T(8,128)}, u32[]{:S(2)}) copy-start(f32[384,1024]{1,0:T(8,128)} %trail_ref.5) | copy-start | bytes 4718596
  37.6 10.9 %collective-permute-start.16 = (f32[256,128]{1,0:T(8,128)S(1)}, f32[256,128]{1,0:T(8,128)S(1)}, u32[]{:S(2)}, u32[]{:S(2)}) collective-permute-start(f32[256,128]{1,0:T(8,128)S(1)} %pad_maximum_fusion.1), channel_id=1, source_target_pairs={{0,6},{2,4},{4,2},{6,0},{1,7},{3,5},{5,3},{7,1},{8,14},{10,12},{12... | collective-permute-start | bytes 393224 | tf_op jit(solution)/shard_map/ppermute | solution.py:409
  39.1 9.4 %collective-permute-start.15 = (f32[256,128]{1,0:T(8,128)S(1)}, f32[256,128]{1,0:T(8,128)S(1)}, u32[]{:S(2)}, u32[]{:S(2)}) collective-permute-start(f32[256,128]{1,0:T(8,128)S(1)} %pad_maximum_fusion.1), channel_id=1, source_target_pairs={{0,4},{2,6},{4,0},{6,2},{1,5},{3,7},{5,1},{7,3},{8,12},{10,14},{12... | collective-permute-start | bytes 393224 | tf_op jit(solution)/shard_map/ppermute | solution.py:409
  40.6 7.9 %collective-permute-start.14 = (f32[256,128]{1,0:T(8,128)S(1)}, f32[256,128]{1,0:T(8,128)S(1)}, u32[]{:S(2)}, u32[]{:S(2)}) collective-permute-start(f32[256,128]{1,0:T(8,128)S(1)} %pad_maximum_fusion.1), channel_id=1, source_target_pairs={{0,2},{2,0},{4,6},{6,4},{1,3},{3,1},{5,7},{7,5},{8,10},{10,8},{12,... | collective-permute-start | bytes 393224 | tf_op jit(solution)/shard_map/ppermute | solution.py:409
  48.6 2.0 %collective-permute-start.17 = (f32[4,256,128]{2,1,0:T(8,128)S(1)}, f32[4,256,128]{2,1,0:T(8,128)S(1)}, u32[]{:S(2)}, u32[]{:S(2)}) collective-permute-start(f32[4,256,128]{2,1,0:T(8,128)S(1)} %pad_maximum_fusion.cross_ref), channel_id=1, source_target_pairs={{0,1},{1,0},{2,3},{3,2},{4,5},{5,4},{6,7},{7,6},{8,9},{9,8},{10,11... | collective-permute-start | bytes 1572872 | tf_op jit(solution)/shard_map/ppermute | solution.py:405

commit v6 on v5

--- a/solution.py
+++ b/solution.py
@@ -16,7 +16,6 @@
 LANES = 128
 BLOCK = 32
 BATCH = 16
-STRIP = 512
 EXTRA = 8
 SMEM = pl.BlockSpec(memory_space=pltpu.SMEM)
 VMEM = pl.BlockSpec(memory_space=pltpu.VMEM)
@@ -118,8 +117,8 @@
 
 
 def other_kernel(
-    place_ref, live_ref, panel_ref, trail_ref, out_ref, left_ref, gram_ref, half_ref,
-    cross_scr, panel_scr, trail_scr, panel_sem, trail_sem, half_sem,
+    place_ref, live_ref, panel_ref, trail_ref, out_ref, left_ref, gram_ref, half_ref, panel_scr,
+    cross_scr, trail_scr, panel_sem, trail_sem, half_sem,
 ):
     columns = trail_ref.shape[1]
     core = place_of(place_ref)[0]
@@ -146,10 +145,13 @@
     copy_half.wait()
 
 
-def own_kernel(place_ref, live_ref, left_ref, gram_ref, half_ref, out_ref, cross_scr):
+def own_kernel(
+    place_ref, live_ref, left_ref, gram_ref, half_ref, panel_ref, out_ref, rows_ref, cross_scr
+):
     cross = dot(left_ref[...], right_of(masked(half_ref, live_ref)))
     core = place_of(place_ref)[0]
     place_products(place_ref, gram_ref.at[core], cross, out_ref, cross_scr)
+    rows_ref[...] = left_of(masked(panel_ref, live_ref), 1)
 
 
 def products_of(place, live, panel, trail):
@@ -165,30 +167,27 @@
             jax.ShapeDtypeStruct((width, 3 * rows), BF16),
             struct(2, LANES + EXTRA, LANES),
             struct(rows, columns // 2),
+            struct(rows, width),
         ),
         in_specs=[SMEM, SMEM, HBM, HBM],
-        out_specs=(VMEM,) * 4,
-        scratch_shapes=[
-            cross_scr,
-            pltpu.VMEM((rows, width), F32),
-            pltpu.VMEM((rows, columns // 2), F32),
-        ]
+        out_specs=(VMEM,) * 5,
+        scratch_shapes=[cross_scr, pltpu.VMEM((rows, columns // 2), F32)]
         + [pltpu.SemaphoreType.DMA] * 3,
         cost_estimate=work,
         compiler_params=PARAMS,
         name="products_other",
     )(place, live, in_hbm(panel), in_hbm(trail))
-    ours = pl.pallas_call(
+    ours, panel_rows = pl.pallas_call(
         own_kernel,
-        out_shape=out,
-        in_specs=[SMEM, SMEM] + [VMEM] * 3,
-        out_specs=VMEM,
+        out_shape=(out, jax.ShapeDtypeStruct((rows, 3 * width), BF16)),
+        in_specs=[SMEM, SMEM] + [VMEM] * 4,
+        out_specs=(VMEM,) * 2,
         scratch_shapes=[cross_scr],
         cost_estimate=work,
         compiler_params=PARAMS,
         name="products_own",
     )(place, live, *handed)
-    return theirs, ours
+    return theirs, ours, panel_rows
 
 
 def across(x, lane):
@@ -202,6 +201,7 @@
 def eliminate(rows, first):
     groups = len(rows)
     index = lax.broadcasted_iota(jnp.int32, (8, LANES), 0)
+    lanes = lax.broadcasted_iota(jnp.int32, (8, LANES), 1)
     pivots = [jnp.ones((8, LANES), F32) for _ in range(groups)]
     for start in range(0, BLOCK, BATCH):
         columns = {
@@ -209,6 +209,10 @@
             for j in range(start, start + BATCH)
             for group in range(j // 8, groups)
         }
+        for group in range(groups):
+            taken = (lanes >= first + start) & (lanes < first + start + BATCH)
+            unit = jnp.where(lanes == index + (first + 8 * group), 1.0, 0.0)
+            rows[group][0] = jnp.where(taken, unit, rows[group][0])
         for j in range(start, start + BATCH, 2):
             home, place = divmod(j, 8)
             a = down(columns[home, j], place)
@@ -249,11 +253,8 @@
     return pivots
 
 
-def factor_inverse(gram_ref, inverse_ref):
+def factor_inverse(gram_ref):
     size = gram_ref.shape[0]
-    row = lax.broadcasted_iota(jnp.int32, (size, size), 0)
-    column = lax.broadcasted_iota(jnp.int32, (size, size), 1)
-    inverse_ref[...] = jnp.where(row == column, 1.0, 0.0)
     tiles = size // LANES
     groups = BLOCK // 8
 
@@ -263,40 +264,42 @@
     for start in range(0, size, BLOCK):
         stop = start + BLOCK
         here = start // LANES
-        rows = []
-        for group in range(groups):
-            at = slice(start + 8 * group, start + 8 * group + 8)
-            rows.append(
-                [gram_ref[at, tile_of(t)] for t in range(here, tiles)]
-                + [inverse_ref[at, tile_of(t)] for t in range(here + 1)]
-            )
+        order = [here] + [t for t in range(tiles) if t != here]
+        rows = [
+            [gram_ref[start + 8 * group : start + 8 * group + 8, tile_of(t)] for t in order]
+            for group in range(groups)
+        ]
         pivots = eliminate(rows, start % LANES)
+        scaled = {t: [] for t in order}
         for group in range(groups):
             scale = lax.rsqrt(pivots[group])
-            rows[group] = [value * scale for value in rows[group]]
-            at = slice(start + 8 * group, start + 8 * group + 8)
-            for t in range(here + 1):
-                inverse_ref[at, tile_of(t)] = rows[group][tiles - here + t]
+            for t, value in zip(order, rows[group]):
+                scaled[t].append(value * scale)
+        stacked = [jnp.concatenate(scaled[t], axis=0) for t in range(tiles)]
+        lanes = lax.broadcasted_iota(jnp.int32, (BLOCK, LANES), 1)
+        done = jnp.where(lanes < stop - here * LANES, stacked[here], 0.0)
+        for t in range(tiles):
+            gram_ref[start:stop, tile_of(t)] = (
+                stacked[t] if t < here else done if t == here else jnp.zeros_like(done)
+            )
         if stop == size:
             break
         base = stop // LANES
-        stacked = [
-            jnp.concatenate([rows[group][i] for group in range(groups)], axis=0)
-            for i in range(base - here, len(rows[0]))
-        ]
-        left = jnp.concatenate(stacked[: tiles - base], axis=1)
+        left = jnp.concatenate(stacked[base:], axis=1)
         product = dot(
             left_of(left, 0, 6), right_of(jnp.concatenate(stacked, axis=1), 6), ((0,), (0,))
         )[stop - base * LANES :]
-        for i, t in enumerate(range(base, tiles)):
-            gram_ref[stop:, tile_of(t)] -= product[:, tile_of(i)]
-        for t in range(here + 1):
-            inverse_ref[stop:, tile_of(t)] -= product[:, tile_of(tiles - base + t)]
+        for t in range(tiles):
+            before = gram_ref[stop:, tile_of(t)]
+            if t == here:
+                lanes = lax.broadcasted_iota(jnp.int32, before.shape, 1) + here * LANES
+                before = jnp.where((lanes >= start) & (lanes < stop), 0.0, before)
+            gram_ref[stop:, tile_of(t)] = before - product[:, tile_of(t)]
 
 
 def factor_kernel(
-    place_ref, live_ref, own_ref, other_ref, panel_ref, left_ref, unit_ref, basis_ref,
-    gram_ref, inverse_ref, packed_ref,
+    place_ref, own_ref, other_ref, rows_ref, left_ref, split_ref, unit_ref, root_ref,
+    inverse_ref, packed_ref,
 ):
     core, chip, _ = place_of(place_ref)
     tall = LANES // SLOTS
@@ -310,45 +313,55 @@
             def _(side=side, ref=ref, slot=slot):
                 packed_ref[side, LANES:, :] = ref[slot, tall:, :]
 
-    root = jnp.sqrt(unpack_gram(packed_ref, gram_ref))
-    factor_inverse(gram_ref, inverse_ref)
+    root = jnp.sqrt(unpack_gram(packed_ref, inverse_ref))
+    root_ref[...] = jnp.broadcast_to(root, root_ref.shape)
+    factor_inverse(inverse_ref)
     inverse = inverse_ref[...]
     left_ref[...] = left_of(inverse, 1)
-    unit = dot(left_of(masked(panel_ref, live_ref), 1), right_of(inverse, axis=1), ((1,), (1,)))
-    unit_ref[...] = left_of(unit, 1)
-    basis_ref[...] = unit * root
-
-
-def factor_of(place, live, own, other, panel):
-    rows, width = panel.shape
+    unit = dot(rows_ref[...], right_of(inverse, axis=1), ((1,), (1,)))
+    split_ref[...] = left_of(unit, 1)
+    unit_ref[...] = unit
+
+
+def factor_of(place, own, other, panel_rows):
+    rows = panel_rows.shape[0]
+    width = panel_rows.shape[1] // 3
     return pl.pallas_call(
         factor_kernel,
         out_shape=(
             jax.ShapeDtypeStruct((width, 3 * width), BF16),
             jax.ShapeDtypeStruct((rows, 3 * width), BF16),
             struct(rows, width),
+            struct(8, LANES),
         ),
-        in_specs=[SMEM, SMEM, VMEM, VMEM, VMEM],
-        out_specs=(VMEM,) * 3,
-        scratch_shapes=[pltpu.VMEM((width, width), F32)] * 2
-        + [pltpu.VMEM((2, LANES + EXTRA, LANES), F32)],
+        in_specs=[SMEM, VMEM, VMEM, VMEM],
+        out_specs=(VMEM,) * 4,
+        scratch_shapes=[
+            pltpu.VMEM((width, width), F32),
+            pltpu.VMEM((2, LANES + EXTRA, LANES), F32),
+        ],
         cost_estimate=cost(6 * 10**9, 4 * rows * width),
         compiler_params=PARAMS,
         name="factor",
-    )(place, live, own, other, panel)
-
-
-def rest_kernel(other, place_ref, live_ref, inverse_ref, unit_ref, cross_ref, trail_ref, *refs):
+    )(place, own, other, panel_rows)
+
+
+def rest_kernel(other, place_ref, live_ref, inverse_ref, split_ref, cross_ref, trail_ref, *refs):
     width = inverse_ref.shape[0]
     columns = trail_ref.shape[1]
     half = columns // 2
     core, chip, depth = place_of(place_ref)
     if other:
-        top_before_ref, _, top_ref, rest_ref, top_scr, cross_scr, rest_scr, sem = refs
+        *_, top_ref, rest_ref, top_scr, cross_scr, rest_scr, top_sem, rest_sem = refs
         side = 1 - core
     else:
-        top_ref, rest_ref, top_scr, cross_scr, rest_scr, sem = refs
+        unit_ref, root_ref, *refs = refs
+        top_ref, rest_ref, basis_ref, top_scr, cross_scr, rest_scr, top_sem, rest_sem, *refs = refs
+        basis_scr, basis_sem = refs
         side = core
+        basis_scr[...] = unit_ref[...] * root_ref[0:1, 0:1]
+        copy_basis = pltpu.make_async_copy(basis_scr, basis_ref, basis_sem)
+        copy_basis.start()
     start = pl.multiple_of(side * half, half)
     part = width // PARTS
     for slot in range(SLOTS):
@@ -358,47 +371,57 @@
             cross_scr[pl.ds(row, part), pl.ds(lane, LANES)] = cross_ref[
                 slot, piece * part : (piece + 1) * part, :
             ]
-    pieces = half // STRIP
-    copies = []
-    for piece in range(pieces):
-        at = slice(piece * STRIP, (piece + 1) * STRIP)
-        to = pl.ds(start + piece * STRIP, STRIP)
-        top = dot(inverse_ref[...], right_of(cross_scr[:, at]))
-        top_scr[:, at] = top
-        rest_scr[:, at] = masked(trail_ref, live_ref, to) - dot(unit_ref[...], right_of(top))
-        copies.append(pltpu.make_async_copy(rest_scr.at[:, at], rest_ref.at[:, to], sem.at[piece]))
-        copies[piece].start()
+    top = dot(inverse_ref[...], right_of(cross_scr[...]))
+    top_scr[...] = top
     wide = top_ref.shape[1]
     begin = place_ref[0] % (columns // wide) * wide
-    mine = top_scr[:, pl.ds(pl.multiple_of(begin % half, LANES), wide)]
-    if other:
-        top_ref[...] = jnp.where(begin // half == side, mine, top_before_ref[...])
-    else:
-        top_ref[...] = mine
-    for copy in copies:
-        copy.wait()
-
-
-def rest_of(other, place, live, inverse, unit, cross, trail, wide, before):
+    mine = begin // half == side
+    copy_top = pltpu.make_async_copy(
+        top_scr.at[:, pl.ds(pl.multiple_of(begin % half, LANES), wide)], top_ref, top_sem
+    )
+
+    @pl.when(mine)
+    def _():
+        copy_top.start()
+
+    rest_scr[...] = masked(trail_ref, live_ref, pl.ds(start, half)) - dot(
+        split_ref[...], right_of(top)
+    )
+    copy_rest = pltpu.make_async_copy(rest_scr, rest_ref.at[:, pl.ds(start, half)], rest_sem)
+    copy_rest.start()
+    copy_rest.wait()
+
+    @pl.when(mine)
+    def _():
+        copy_top.wait()
+
+    if not other:
+        copy_basis.wait()
+
+
+def rest_of(other, place, live, inverse, split, cross, trail, wide, more):
     rows, columns = trail.shape
     width = inverse.shape[0]
     half = columns // 2
+    basis = [] if other else [struct(rows, width)]
     return pl.pallas_call(
         functools.partial(rest_kernel, other),
-        out_shape=(struct(width, wide), struct(rows, columns)),
-        in_specs=[SMEM] * 2 + [VMEM] * 4 + ([VMEM, ANY] if other else []),
-        out_specs=(VMEM, ANY),
+        out_shape=[struct(width, wide), struct(rows, columns)] + basis,
+        in_specs=[SMEM] * 2 + [VMEM] * 4 + [ANY if other else VMEM] * 2,
+        out_specs=[ANY] * (2 + len(basis)),
         scratch_shapes=[
             pltpu.VMEM((width, half), F32),
             pltpu.VMEM((width, half), F32),
             pltpu.VMEM((rows, half), F32),
-            pltpu.SemaphoreType.DMA((half // STRIP,)),
-        ],
-        input_output_aliases={7: 1} if other else {},
-        cost_estimate=cost(12 * (rows + width) * width * half, 8 * rows * half),
+            pltpu.SemaphoreType.DMA,
+            pltpu.SemaphoreType.DMA,
+        ]
+        + ([] if other else [pltpu.VMEM((rows, width), F32), pltpu.SemaphoreType.DMA]),
+        input_output_aliases={6: 0, 7: 1} if other else {},
+        cost_estimate=cost(6 * (rows + width) * width * half, 8 * rows * half),
         compiler_params=PARAMS,
         name="rest_other" if other else "rest_own",
-    )(place, live, inverse, unit, cross, trail, *before)
+    )(place, live, inverse, split, cross, trail, *more)
 
 
 def swap(x):
@@ -420,7 +443,7 @@
     place = lax.axis_index(AXES)[None]
     tall, part = LANES // SLOTS + EXTRA, width // PARTS
 
-    theirs, ours = products_of(place, live_rows, panel, trailing)
+    theirs, ours, panel_rows = products_of(place, live_rows, panel, trailing)
     pair = ours + swap(theirs)
     slots = [pair[0]] + [send(pair[k], flat, SLOTS, k) for k in range(1, SLOTS)]
     summed = tree(slots)
@@ -437,13 +460,13 @@
     gram_own = jnp.stack([gram] + [send(gram, flat, SLOTS, k) for k in range(1, SLOTS)])
     cross = jnp.concatenate([cross] + [send(cross, deep, PARTS, j) for j in range(1, PARTS)])
     cross_own = [cross] + [send(cross, flat, SLOTS, k) for k in range(1, SLOTS)]
-    inverse, unit, basis = factor_of(place, live_rows, gram_own, swap(gram_own), panel)
+    inverse, split, unit, root = factor_of(place, gram_own, swap(gram_own), panel_rows)
     *cross_own, inverse = lax.optimization_barrier((*cross_own, inverse))
     cross_own = jnp.stack(cross_own)
     cross_other = swap(cross_own)
-    args = (place, live_rows, inverse, unit)
-    before = rest_of(False, *args, cross_own, trailing, wide, ())
-    top, rest = rest_of(True, *args, cross_other, trailing, wide, before)
+    args = (place, live_rows, inverse, split)
+    top, rest, basis = rest_of(False, *args, cross_own, trailing, wide, (unit, root))
+    top, rest = rest_of(True, *args, cross_other, trailing, wide, (top, rest))
     return basis, top, rest
 
 

time: 53.2 us -> 51.7 us (0.972)
  Pallas kernels: 15 us -> 13.5 us
    pallas_call x1, Pallas kernels: 7.36 us -> 6.37 us  [factor_of(): pl.pallas_call(factor_kernel, out_shape=(jax.ShapeDtypeStruct((width, 3 *...]
  transfers between devices with their start and end apart: 18 -> 18, of which waited for: 9 -> 8; matrix products, arithmetic and copies ran while one was open for 0% -> 0% of each run, Pallas kernels for 18% -> 17%
where the time goes in v6:
time: 51.7 us; the launch traced here: 51.5 us
  starting transfers between devices  21.1 us (41%)
  waiting for transfers between devices  15.2 us (29%)
  Pallas kernels  13.5 us (26%)
  between operations  1.45 us (3%)
    ppermute x15, starting transfers between devices, send(): return lax.ppermute(x, axes, [(i, i ^ shift) for i in range(size)])  20.5 us
    ppermute x15, waiting for transfers between devices, send(): return lax.ppermute(x, axes, [(i, i ^ shift) for i in range(size)])  14.1 us
    pallas_call x1, Pallas kernels, factor_of(): pl.pallas_call(factor_kernel, out_shape=(jax.ShapeDtypeStruct((width, 3 *...  6.37 us
    pallas_call x2, Pallas kernels, rest_of(): pl.pallas_call(functools.partial(rest_kernel, other), out_shape=[struct(w...  3.82 us
    pallas_call x1, Pallas kernels, products_of(): pl.pallas_call(other_kernel, out_shape=(out, jax.ShapeDtypeStruct((width,...  2.71 us
    ppermute x3, waiting for transfers between devices, swap(): return lax.ppermute(x, 'core', [(0, 1), (1, 0)])  1.04 us
  transfers between devices with their start and end apart: 18, of which 8 were waited for; matrix products, arithmetic and copies ran while one was open for 0% of the time, Pallas kernels for 17%

profile of v6, /device:TPU:0, one launch (start us, length us, event | category | flops | bytes accessed | tf_op | source)
XLA Modules:
  0.0 51.5 jit_solution(4553976221042767139)
XLA Ops:
  1.3 2.7 %products_other.1 = (f32[4,296,128]{2,1,0:T(8,128)S(1)}, bf16[256,1152]{1,0:T(8,128)(2,1)S(1)}, f32[2,136,128]{2,1,0:T(8,128)S(1)}, f32[384,512]{1,0:T(8,128)S(1)}, f32[384,256]{1,0:T(8,128)S(1)}) custom-call(s32[1]{0:T(128)} %bitcast.place_ref, s32[1]{0:T(128)S(6)} %copy.10.live_ref, f32[384,256]{1,0:T(8,128)} %panel_ref.1, f32[384,1024]{1,0:T(8,128)} %trail_ref.5), custom_call_target="tpu_custom_call" | custom-call | flops 301989888 | bytes 786432 | tf_op jit(solution)/shard_map/products_other/pallas_call | solution.py:163
  4.0 0.5 %collective-permute-start = (f32[4,296,128]{2,1,0:T(8,128)S(1)}, f32[4,296,128]{2,1,0:T(8,128)S(1)}, u32[]{:S(2)}, u32[]{:S(2)}) collective-permute-start(f32[4,296,128]{2,1,0:T(8,128)S(1)} %get-tuple-element.29), channel_id=1, source_target_pairs={{0,1},{1,0},{2,3},{3,2},{4,5},{5,4},{6,7},{7,6},{8,9},{9,8},{10,11... | collective-permute-start | bytes 1818632 | tf_op jit(solution)/shard_map/ppermute | solution.py:428
  4.5 0.6 %products_own.1 = (f32[4,296,128]{2,1,0:T(8,128)S(1)}, bf16[384,768]{1,0:T(8,128)(2,1)S(1)}) custom-call(s32[1]{0:T(128)} %bitcast.place_ref, s32[1]{0:T(128)S(6)} %copy.10.live_ref, bf16[256,1152]{1,0:T(8,128)(2,1)S(1)} %get-tuple-element.24.left_ref, f32[2,136,128]{2,1,0:T(8,128)S(1)} %get-tuple-element.25.gram_ref, ...), custom_call_target="tpu_custom_call" | custom-call | flops 301989888 | bytes 786432 | tf_op jit(solution)/shard_map/products_own/pallas_call | solution.py:180
  5.1 1.0 %collective-permute-done = f32[4,296,128]{2,1,0:T(8,128)S(1)} collective-permute-done((f32[4,296,128]{2,1,0:T(8,128)S(1)}, f32[4,296,128]{2,1,0:T(8,128)S(1)}, u32[]{:S(2)}, u32[]{:S(2)}) %collective-permute-start) | collective-permute-done | bytes 606240 | tf_op jit(solution)/shard_map/ppermute | solution.py:428
  6.3 3.9 %collective-permute-start.3 = (f32[296,128]{1,0:T(8,128)S(1)}, f32[296,128]{1,0:T(8,128)S(1)}, u32[]{:S(2)}, u32[]{:S(2)}) collective-permute-start(f32[296,128]{1,0:T(8,128)S(1)} %get-tuple-element.45), channel_id=1, source_target_pairs={{0,6},{2,4},{4,2},{6,0},{1,7},{3,5},{5,3},{7,1},{8,14},{10,12},{12... | collective-permute-start | bytes 454664 | tf_op jit(solution)/shard_map/ppermute | solution.py:432
  10.8 4.1 %collective-permute-done.3 = f32[296,128]{1,0:T(8,128)S(1)} collective-permute-done((f32[296,128]{1,0:T(8,128)S(1)}, f32[296,128]{1,0:T(8,128)S(1)}, u32[]{:S(2)}, u32[]{:S(2)}) %collective-permute-start.3) | collective-permute-done | bytes 151584 | tf_op jit(solution)/shard_map/ppermute | solution.py:432
  14.9 2.8 %collective-permute-done.2 = f32[296,128]{1,0:T(8,128)S(1)} collective-permute-done((f32[296,128]{1,0:T(8,128)S(1)}, f32[296,128]{1,0:T(8,128)S(1)}, u32[]{:S(2)}, u32[]{:S(2)}) %collective-permute-start.2) | collective-permute-done | bytes 151584 | tf_op jit(solution)/shard_map/ppermute | solution.py:432
  18.0 3.7 %collective-permute-start.6 = (f32[104,128]{1,0:T(8,128)S(1)}, f32[104,128]{1,0:T(8,128)S(1)}, u32[]{:S(2)}, u32[]{:S(2)}) collective-permute-start(f32[104,128]{1,0:T(8,128)S(1)} %get-tuple-element.53), channel_id=1, source_target_pairs={{0,24},{8,16},{16,8},{24,0},{1,25},{9,17},{17,9},{25,1},{2,26},{10... | collective-permute-start | bytes 159752 | tf_op jit(solution)/shard_map/ppermute | solution.py:432
  21.7 0.8 %collective-permute-start.4 = (f32[104,128]{1,0:T(8,128)S(1)}, f32[104,128]{1,0:T(8,128)S(1)}, u32[]{:S(2)}, u32[]{:S(2)}) collective-permute-start(f32[104,128]{1,0:T(8,128)S(1)} %get-tuple-element.55), channel_id=1, source_target_pairs={{0,8},{8,0},{16,24},{24,16},{1,9},{9,1},{17,25},{25,17},{2,10},{10... | collective-permute-start | bytes 159752 | tf_op jit(solution)/shard_map/ppermute | solution.py:432
  22.5 1.9 %collective-permute-done.6 = f32[104,128]{1,0:T(8,128)S(1)} collective-permute-done((f32[104,128]{1,0:T(8,128)S(1)}, f32[104,128]{1,0:T(8,128)S(1)}, u32[]{:S(2)}, u32[]{:S(2)}) %collective-permute-start.6) | collective-permute-done | bytes 53280 | tf_op jit(solution)/shard_map/ppermute | solution.py:432
  24.4 2.3 %collective-permute-done.5 = f32[104,128]{1,0:T(8,128)S(1)} collective-permute-done((f32[104,128]{1,0:T(8,128)S(1)}, f32[104,128]{1,0:T(8,128)S(1)}, u32[]{:S(2)}, u32[]{:S(2)}) %collective-permute-start.5) | collective-permute-done | bytes 53280 | tf_op jit(solution)/shard_map/ppermute | solution.py:432
  26.8 1.5 %collective-permute-start.14 = (f32[40,128]{1,0:T(8,128)S(1)}, f32[40,128]{1,0:T(8,128)S(1)}, u32[]{:S(2)}, u32[]{:S(2)}) collective-permute-start(f32[40,128]{1,0:T(8,128)S(1)} %get-tuple-element.52), channel_id=1, source_target_pairs={{0,4},{2,6},{4,0},{6,2},{1,5},{3,7},{5,1},{7,3},{8,12},{10,14},{12... | collective-permute-start | bytes 61448 | tf_op jit(solution)/shard_map/ppermute | solution.py:432
  28.3 0.8 %collective-permute-start.13 = (f32[40,128]{1,0:T(8,128)S(1)}, f32[40,128]{1,0:T(8,128)S(1)}, u32[]{:S(2)}, u32[]{:S(2)}) collective-permute-start(f32[40,128]{1,0:T(8,128)S(1)} %get-tuple-element.52), channel_id=1, source_target_pairs={{0,2},{2,0},{4,6},{6,4},{1,3},{3,1},{5,7},{7,5},{8,10},{10,8},{12,... | collective-permute-start | bytes 61448 | tf_op jit(solution)/shard_map/ppermute | solution.py:432
  29.0 1.3 %collective-permute-start.15 = (f32[40,128]{1,0:T(8,128)S(1)}, f32[40,128]{1,0:T(8,128)S(1)}, u32[]{:S(2)}, u32[]{:S(2)}) collective-permute-start(f32[40,128]{1,0:T(8,128)S(1)} %get-tuple-element.52), channel_id=1, source_target_pairs={{0,6},{2,4},{4,2},{6,0},{1,7},{3,5},{5,3},{7,1},{8,14},{10,12},{12... | collective-permute-start | bytes 61448 | tf_op jit(solution)/shard_map/ppermute | solution.py:432
  30.3 2.4 %collective-permute-start.9 = (f32[64,128]{1,0:T(8,128)S(1)}, f32[64,128]{1,0:T(8,128)S(1)}, u32[]{:S(2)}, u32[]{:S(2)}) collective-permute-start(f32[64,128]{1,0:T(8,128)S(1)} %slice.50), channel_id=1, source_target_pairs={{0,24},{8,16},{16,8},{24,0},{1,25},{9,17},{17,9},{25,1},{2,26},{10... | collective-permute-start | bytes 98312 | tf_op jit(solution)/shard_map/ppermute | solution.py:432
  32.7 2.0 %collective-permute-start.7 = (f32[64,128]{1,0:T(8,128)S(1)}, f32[64,128]{1,0:T(8,128)S(1)}, u32[]{:S(2)}, u32[]{:S(2)}) collective-permute-start(f32[64,128]{1,0:T(8,128)S(1)} %slice.50), channel_id=1, source_target_pairs={{0,8},{8,0},{16,24},{24,16},{1,9},{9,1},{17,25},{25,17},{2,10},{10... | collective-permute-start | bytes 98312 | tf_op jit(solution)/shard_map/ppermute | solution.py:432
  34.8 1.2 %collective-permute-done.9 = f32[64,128]{1,0:T(8,128)S(1)} collective-permute-done((f32[64,128]{1,0:T(8,128)S(1)}, f32[64,128]{1,0:T(8,128)S(1)}, u32[]{:S(2)}, u32[]{:S(2)}) %collective-permute-start.9) | collective-permute-done | bytes 32800 | tf_op jit(solution)/shard_map/ppermute | solution.py:432
  36.0 1.5 %collective-permute-done.8 = f32[64,128]{1,0:T(8,128)S(1)} collective-permute-done((f32[64,128]{1,0:T(8,128)S(1)}, f32[64,128]{1,0:T(8,128)S(1)}, u32[]{:S(2)}, u32[]{:S(2)}) %collective-permute-start.8) | collective-permute-done | bytes 32800 | tf_op jit(solution)/shard_map/ppermute | solution.py:432
  37.6 1.5 %collective-permute-start.12 = (f32[256,128]{1,0:T(8,128)S(1)}, f32[256,128]{1,0:T(8,128)S(1)}, u32[]{:S(2)}, u32[]{:S(2)}) collective-permute-start(f32[256,128]{1,0:T(8,128)S(1)} %pad_maximum_fusion.1), channel_id=1, source_target_pairs={{0,6},{2,4},{4,2},{6,0},{1,7},{3,5},{5,3},{7,1},{8,14},{10,12},{12... | collective-permute-start | bytes 393224 | tf_op jit(solution)/shard_map/ppermute | solution.py:432
  39.1 1.5 %collective-permute-start.11 = (f32[256,128]{1,0:T(8,128)S(1)}, f32[256,128]{1,0:T(8,128)S(1)}, u32[]{:S(2)}, u32[]{:S(2)}) collective-permute-start(f32[256,128]{1,0:T(8,128)S(1)} %pad_maximum_fusion.1), channel_id=1, source_target_pairs={{0,4},{2,6},{4,0},{6,2},{1,5},{3,7},{5,1},{7,3},{8,12},{10,14},{12... | collective-permute-start | bytes 393224 | tf_op jit(solution)/shard_map/ppermute | solution.py:432
  40.6 0.5 %collective-permute-start.10 = (f32[256,128]{1,0:T(8,128)S(1)}, f32[256,128]{1,0:T(8,128)S(1)}, u32[]{:S(2)}, u32[]{:S(2)}) collective-permute-start(f32[256,128]{1,0:T(8,128)S(1)} %pad_maximum_fusion.1), channel_id=1, source_target_pairs={{0,2},{2,0},{4,6},{6,4},{1,3},{3,1},{5,7},{7,5},{8,10},{10,8},{12,... | collective-permute-start | bytes 393224 | tf_op jit(solution)/shard_map/ppermute | solution.py:432
  41.1 6.4 %factor.1 = (bf16[256,768]{1,0:T(8,128)(2,1)S(1)}, bf16[384,768]{1,0:T(8,128)(2,1)S(1)}, f32[384,256]{1,0:T(8,128)S(1)}, f32[8,128]{1,0:T(8,128)S(1)}) custom-call(s32[1]{0:T(128)} %bitcast.place_ref, f32[4,40,128]{2,1,0:T(8,128)S(1)} %pad_maximum_fusion.2.own_ref, f32[4,40,128]{2,1,0:T(8,128)S(1)} %collective-permute-done.16.other_ref, ...), custom_call_target="tpu_custom_call" | custom-call | flops 6000000000 | bytes 393216 | tf_op jit(solution)/shard_map/factor/pallas_call | solution.py:329
  47.7 2.0 %rest_own.1 = (f32[256,256]{1,0:T(8,128)}, f32[384,1024]{1,0:T(8,128)}, f32[384,256]{1,0:T(8,128)}) custom-call(s32[1]{0:T(128)} %bitcast.place_ref, s32[1]{0:T(128)S(6)} %copy.10.live_ref, bf16[256,768]{1,0:T(8,128)(2,1)S(1)} %get-tuple-element.32.inverse_ref, bf16[384,768]{1,0:T(8,128)(2,1)S(1)} %get-tuple-element.33.split_ref, ...), custom_call_target="tpu_custom_call" | custom-call | flops 503316480 | bytes 1572864 | tf_op jit(solution)/shard_map/rest_own/pallas_call | solution.py:407
  49.7 1.8 %rest_other.1 = (f32[256,256]{1,0:T(8,128)}, f32[384,1024]{1,0:T(8,128)}) custom-call(s32[1]{0:T(128)} %bitcast.place_ref, s32[1]{0:T(128)S(6)} %copy.10.live_ref, bf16[256,768]{1,0:T(8,128)(2,1)S(1)} %get-tuple-element.32.inverse_ref, bf16[384,768]{1,0:T(8,128)(2,1)S(1)} %get-tuple-element.33.split_ref, ...), custom_call_target="tpu_custom_call", output_to_operand_aliasing={{0}: (6, {}), {1}: (7, {})} | custom-call | flops 503316480 | bytes 1572864 | tf_op jit(solution)/shard_map/rest_other/pallas_call | solution.py:407
  (31 shorter events, 1.3 us)
Async XLA Ops:
  4.0 2.2 %collective-permute-start = (f32[4,296,128]{2,1,0:T(8,128)S(1)}, f32[4,296,128]{2,1,0:T(8,128)S(1)}, u32[]{:S(2)}, u32[]{:S(2)}) collective-permute-start(f32[4,296,128]{2,1,0:T(8,128)S(1)} %get-tuple-element.29), channel_id=1, source_target_pairs={{0,1},{1,0},{2,3},{3,2},{4,5},{5,4},{6,7},{7,6},{8,9},{9,8},{10,11... | collective-permute-start | bytes 1818632 | tf_op jit(solution)/shard_map/ppermute | solution.py:428
  6.3 8.6 %collective-permute-start.3 = (f32[296,128]{1,0:T(8,128)S(1)}, f32[296,128]{1,0:T(8,128)S(1)}, u32[]{:S(2)}, u32[]{:S(2)}) collective-permute-start(f32[296,128]{1,0:T(8,128)S(1)} %get-tuple-element.45), channel_id=1, source_target_pairs={{0,6},{2,4},{4,2},{6,0},{1,7},{3,5},{5,3},{7,1},{8,14},{10,12},{12... | collective-permute-start | bytes 454664 | tf_op jit(solution)/shard_map/ppermute | solution.py:432
  10.2 7.5 %collective-permute-start.2 = (f32[296,128]{1,0:T(8,128)S(1)}, f32[296,128]{1,0:T(8,128)S(1)}, u32[]{:S(2)}, u32[]{:S(2)}) collective-permute-start(f32[296,128]{1,0:T(8,128)S(1)} %get-tuple-element.46), channel_id=1, source_target_pairs={{0,4},{2,6},{4,0},{6,2},{1,5},{3,7},{5,1},{7,3},{8,12},{10,14},{12... | collective-permute-start | bytes 454664 | tf_op jit(solution)/shard_map/ppermute | solution.py:432
  10.7 7.3 %collective-permute-start.1 = (f32[296,128]{1,0:T(8,128)S(1)}, f32[296,128]{1,0:T(8,128)S(1)}, u32[]{:S(2)}, u32[]{:S(2)}) collective-permute-start(f32[296,128]{1,0:T(8,128)S(1)} %get-tuple-element.47), channel_id=1, source_target_pairs={{0,2},{2,0},{4,6},{6,4},{1,3},{3,1},{5,7},{7,5},{8,10},{10,8},{12,... | collective-permute-start | bytes 454664 | tf_op jit(solution)/shard_map/ppermute | solution.py:432
  18.0 6.4 %collective-permute-start.6 = (f32[104,128]{1,0:T(8,128)S(1)}, f32[104,128]{1,0:T(8,128)S(1)}, u32[]{:S(2)}, u32[]{:S(2)}) collective-permute-start(f32[104,128]{1,0:T(8,128)S(1)} %get-tuple-element.53), channel_id=1, source_target_pairs={{0,24},{8,16},{16,8},{24,0},{1,25},{9,17},{17,9},{25,1},{2,26},{10... | collective-permute-start | bytes 159752 | tf_op jit(solution)/shard_map/ppermute | solution.py:432
  21.7 5.0 %collective-permute-start.5 = (f32[104,128]{1,0:T(8,128)S(1)}, f32[104,128]{1,0:T(8,128)S(1)}, u32[]{:S(2)}, u32[]{:S(2)}) collective-permute-start(f32[104,128]{1,0:T(8,128)S(1)} %get-tuple-element.54), channel_id=1, source_target_pairs={{0,16},{8,24},{16,0},{24,8},{1,17},{9,25},{17,1},{25,9},{2,18},{10... | collective-permute-start | bytes 159752 | tf_op jit(solution)/shard_map/ppermute | solution.py:432
  21.7 5.0 %collective-permute-start.4 = (f32[104,128]{1,0:T(8,128)S(1)}, f32[104,128]{1,0:T(8,128)S(1)}, u32[]{:S(2)}, u32[]{:S(2)}) collective-permute-start(f32[104,128]{1,0:T(8,128)S(1)} %get-tuple-element.55), channel_id=1, source_target_pairs={{0,8},{8,0},{16,24},{24,16},{1,9},{9,1},{17,25},{25,17},{2,10},{10... | collective-permute-start | bytes 159752 | tf_op jit(solution)/shard_map/ppermute | solution.py:432
  26.8 6.0 %collective-permute-start.14 = (f32[40,128]{1,0:T(8,128)S(1)}, f32[40,128]{1,0:T(8,128)S(1)}, u32[]{:S(2)}, u32[]{:S(2)}) collective-permute-start(f32[40,128]{1,0:T(8,128)S(1)} %get-tuple-element.52), channel_id=1, source_target_pairs={{0,4},{2,6},{4,0},{6,2},{1,5},{3,7},{5,1},{7,3},{8,12},{10,14},{12... | collective-permute-start | bytes 61448 | tf_op jit(solution)/shard_map/ppermute | solution.py:432
  28.3 6.5 %collective-permute-start.13 = (f32[40,128]{1,0:T(8,128)S(1)}, f32[40,128]{1,0:T(8,128)S(1)}, u32[]{:S(2)}, u32[]{:S(2)}) collective-permute-start(f32[40,128]{1,0:T(8,128)S(1)} %get-tuple-element.52), channel_id=1, source_target_pairs={{0,2},{2,0},{4,6},{6,4},{1,3},{3,1},{5,7},{7,5},{8,10},{10,8},{12,... | collective-permute-start | bytes 61448 | tf_op jit(solution)/shard_map/ppermute | solution.py:432
  29.0 5.7 %collective-permute-start.15 = (f32[40,128]{1,0:T(8,128)S(1)}, f32[40,128]{1,0:T(8,128)S(1)}, u32[]{:S(2)}, u32[]{:S(2)}) collective-permute-start(f32[40,128]{1,0:T(8,128)S(1)} %get-tuple-element.52), channel_id=1, source_target_pairs={{0,6},{2,4},{4,2},{6,0},{1,7},{3,5},{5,3},{7,1},{8,14},{10,12},{12... | collective-permute-start | bytes 61448 | tf_op jit(solution)/shard_map/ppermute | solution.py:432
  30.3 5.7 %collective-permute-start.9 = (f32[64,128]{1,0:T(8,128)S(1)}, f32[64,128]{1,0:T(8,128)S(1)}, u32[]{:S(2)}, u32[]{:S(2)}) collective-permute-start(f32[64,128]{1,0:T(8,128)S(1)} %slice.50), channel_id=1, source_target_pairs={{0,24},{8,16},{16,8},{24,0},{1,25},{9,17},{17,9},{25,1},{2,26},{10... | collective-permute-start | bytes 98312 | tf_op jit(solution)/shard_map/ppermute | solution.py:432
  32.7 4.8 %collective-permute-start.8 = (f32[64,128]{1,0:T(8,128)S(1)}, f32[64,128]{1,0:T(8,128)S(1)}, u32[]{:S(2)}, u32[]{:S(2)}) collective-permute-start(f32[64,128]{1,0:T(8,128)S(1)} %slice.50), channel_id=1, source_target_pairs={{0,16},{8,24},{16,0},{24,8},{1,17},{9,25},{17,1},{25,9},{2,18},{10... | collective-permute-start | bytes 98312 | tf_op jit(solution)/shard_map/ppermute | solution.py:432
  32.7 4.8 %collective-permute-start.7 = (f32[64,128]{1,0:T(8,128)S(1)}, f32[64,128]{1,0:T(8,128)S(1)}, u32[]{:S(2)}, u32[]{:S(2)}) collective-permute-start(f32[64,128]{1,0:T(8,128)S(1)} %slice.50), channel_id=1, source_target_pairs={{0,8},{8,0},{16,24},{24,16},{1,9},{9,1},{17,25},{25,17},{2,10},{10... | collective-permute-start | bytes 98312 | tf_op jit(solution)/shard_map/ppermute | solution.py:432
  34.7 6.4 %collective-permute-start.16 = (f32[4,40,128]{2,1,0:T(8,128)S(1)}, f32[4,40,128]{2,1,0:T(8,128)S(1)}, u32[]{:S(2)}, u32[]{:S(2)}) collective-permute-start(f32[4,40,128]{2,1,0:T(8,128)S(1)} %pad_maximum_fusion.2.own_ref), channel_id=1, source_target_pairs={{0,1},{1,0},{2,3},{3,2},{4,5},{5,4},{6,7},{7,6},{8,9},{9,8},{10,11... | collective-permute-start | bytes 245768 | tf_op jit(solution)/shard_map/ppermute | solution.py:428
  37.6 9.9 %collective-permute-start.12 = (f32[256,128]{1,0:T(8,128)S(1)}, f32[256,128]{1,0:T(8,128)S(1)}, u32[]{:S(2)}, u32[]{:S(2)}) collective-permute-start(f32[256,128]{1,0:T(8,128)S(1)} %pad_maximum_fusion.1), channel_id=1, source_target_pairs={{0,6},{2,4},{4,2},{6,0},{1,7},{3,5},{5,3},{7,1},{8,14},{10,12},{12... | collective-permute-start | bytes 393224 | tf_op jit(solution)/shard_map/ppermute | solution.py:432
  39.1 8.5 %collective-permute-start.11 = (f32[256,128]{1,0:T(8,128)S(1)}, f32[256,128]{1,0:T(8,128)S(1)}, u32[]{:S(2)}, u32[]{:S(2)}) collective-permute-start(f32[256,128]{1,0:T(8,128)S(1)} %pad_maximum_fusion.1), channel_id=1, source_target_pairs={{0,4},{2,6},{4,0},{6,2},{1,5},{3,7},{5,1},{7,3},{8,12},{10,14},{12... | collective-permute-start | bytes 393224 | tf_op jit(solution)/shard_map/ppermute | solution.py:432
  40.6 6.9 %collective-permute-start.10 = (f32[256,128]{1,0:T(8,128)S(1)}, f32[256,128]{1,0:T(8,128)S(1)}, u32[]{:S(2)}, u32[]{:S(2)}) collective-permute-start(f32[256,128]{1,0:T(8,128)S(1)} %pad_maximum_fusion.1), channel_id=1, source_target_pairs={{0,2},{2,0},{4,6},{6,4},{1,3},{3,1},{5,7},{7,5},{8,10},{10,8},{12,... | collective-permute-start | bytes 393224 | tf_op jit(solution)/shard_map/ppermute | solution.py:432
  41.1 6.5 %copy-start = (f32[384,1024]{1,0:T(8,128)S(1)}, f32[384,1024]{1,0:T(8,128)}, u32[]{:S(2)}) copy-start(f32[384,1024]{1,0:T(8,128)} %trail_ref.5) | copy-start | bytes 4718596
  47.6 2.1 %collective-permute-start.17 = (f32[4,256,128]{2,1,0:T(8,128)S(1)}, f32[4,256,128]{2,1,0:T(8,128)S(1)}, u32[]{:S(2)}, u32[]{:S(2)}) collective-permute-start(f32[4,256,128]{2,1,0:T(8,128)S(1)} %pad_maximum_fusion.cross_ref), channel_id=1, source_target_pairs={{0,1},{1,0},{2,3},{3,2},{4,5},{5,4},{6,7},{7,6},{8,9},{9,8},{10,11... | collective-permute-start | bytes 1572872 | tf_op jit(solution)/shard_map/ppermute | solution.py:428

commit v7 on v6

--- a/solution.py
+++ b/solution.py
@@ -68,7 +68,7 @@
     return pl.CostEstimate(flops=flops, bytes_accessed=transferred, transcendentals=0)
 
 
-def place_products(place_ref, gram, cross, out_ref, cross_scr):
+def place_products(place_ref, gram, cross, out_refs, cross_scr):
     width = cross.shape[0]
     _, chip, depth = place_of(place_ref)
     tall = LANES // SLOTS
@@ -77,12 +77,13 @@
         cross_scr[tile] = cross[:, tile * LANES : (tile + 1) * LANES]
     for slot in range(SLOTS):
         chunk = jnp.bitwise_xor(chip, slot)
-        out_ref[slot, :tall, :] = gram[pl.ds(pl.multiple_of(chunk * tall, 8), tall), :]
-        out_ref[slot, tall : tall + EXTRA, :] = gram[LANES:, :]
+        out_ref = out_refs[slot]
+        out_ref[:tall, :] = gram[pl.ds(pl.multiple_of(chunk * tall, 8), tall), :]
+        out_ref[tall : tall + EXTRA, :] = gram[LANES:, :]
         for piece in range(PARTS):
             at = pl.multiple_of(jnp.bitwise_xor(depth, piece) * part, 8)
             to = tall + EXTRA + piece * part
-            out_ref[slot, to : to + part, :] = cross_scr[chunk, pl.ds(at, part), :]
+            out_ref[to : to + part, :] = cross_scr[chunk, pl.ds(at, part), :]
 
 
 def triangle():
@@ -117,9 +118,11 @@
 
 
 def other_kernel(
-    place_ref, live_ref, panel_ref, trail_ref, out_ref, left_ref, gram_ref, half_ref, panel_scr,
-    cross_scr, trail_scr, panel_sem, trail_sem, half_sem,
+    place_ref, live_ref, panel_ref, trail_ref, *refs
 ):
+    out_refs = refs[:SLOTS]
+    left_ref, gram_ref, half_ref, panel_scr, cross_scr, trail_scr, *sems = refs[SLOTS:]
+    panel_sem, trail_sem, half_sem = sems
     columns = trail_ref.shape[1]
     core = place_of(place_ref)[0]
     wide = columns // 2
@@ -136,52 +139,57 @@
     copy_panel.wait()
     rows = panel_scr.shape[0]
     panel = masked(panel_scr, live_ref)
-    left = left_of(panel.T, 1, 6)
-    left_ref[...] = left[:, : 3 * rows]
-    pack_gram(dot(left, right_of(panel, 6)), live_ref[0], gram_ref)
+    left = left_of(panel.T, 1)
+    left_ref[...] = left
+    high, middle, low = parts_of(panel)
+    mixed = dot(left[:, : 2 * rows], jnp.concatenate([middle, low], axis=0))
+    gram = dot(left[:, rows:], jnp.concatenate([high, middle], axis=0)) + (mixed + mixed.T)
+    pack_gram(gram, live_ref[0], gram_ref)
     copy_trail.wait()
-    cross = dot(left[:, : 3 * rows], right_of(masked(trail_scr, live_ref)))
-    place_products(place_ref, gram_ref.at[1 - core], cross, out_ref, cross_scr)
+    cross = dot(left, right_of(masked(trail_scr, live_ref)))
+    place_products(place_ref, gram_ref.at[1 - core], cross, out_refs, cross_scr)
     copy_half.wait()
 
 
 def own_kernel(
-    place_ref, live_ref, left_ref, gram_ref, half_ref, panel_ref, out_ref, rows_ref, cross_scr
+    place_ref, live_ref, left_ref, gram_ref, half_ref, panel_ref, *refs
 ):
+    *out_refs, rows_ref, cross_scr = refs
     cross = dot(left_ref[...], right_of(masked(half_ref, live_ref)))
     core = place_of(place_ref)[0]
-    place_products(place_ref, gram_ref.at[core], cross, out_ref, cross_scr)
+    place_products(place_ref, gram_ref.at[core], cross, out_refs, cross_scr)
     rows_ref[...] = left_of(masked(panel_ref, live_ref), 1)
 
 
 def products_of(place, live, panel, trail):
     rows, width = panel.shape
     columns = trail.shape[1]
-    out = struct(SLOTS, LANES // SLOTS + EXTRA + width, LANES)
+    out = (struct(LANES // SLOTS + EXTRA + width, LANES),) * SLOTS
     work = cost(6 * rows * width * columns // 2, 2 * rows * columns)
     cross_scr = pltpu.VMEM((SLOTS, width, LANES), F32)
-    theirs, *handed = pl.pallas_call(
+    outs = pl.pallas_call(
         other_kernel,
         out_shape=(
-            out,
+            *out,
             jax.ShapeDtypeStruct((width, 3 * rows), BF16),
             struct(2, LANES + EXTRA, LANES),
             struct(rows, columns // 2),
             struct(rows, width),
         ),
         in_specs=[SMEM, SMEM, HBM, HBM],
-        out_specs=(VMEM,) * 5,
+        out_specs=(VMEM,) * (SLOTS + 4),
         scratch_shapes=[cross_scr, pltpu.VMEM((rows, columns // 2), F32)]
         + [pltpu.SemaphoreType.DMA] * 3,
         cost_estimate=work,
         compiler_params=PARAMS,
         name="products_other",
     )(place, live, in_hbm(panel), in_hbm(trail))
-    ours, panel_rows = pl.pallas_call(
+    theirs, handed = outs[:SLOTS], outs[SLOTS:]
+    *ours, panel_rows = pl.pallas_call(
         own_kernel,
-        out_shape=(out, jax.ShapeDtypeStruct((rows, 3 * width), BF16)),
+        out_shape=(*out, jax.ShapeDtypeStruct((rows, 3 * width), BF16)),
         in_specs=[SMEM, SMEM] + [VMEM] * 4,
-        out_specs=(VMEM,) * 2,
+        out_specs=(VMEM,) * (SLOTS + 1),
         scratch_shapes=[cross_scr],
         cost_estimate=work,
         compiler_params=PARAMS,
@@ -444,7 +452,9 @@
     tall, part = LANES // SLOTS + EXTRA, width // PARTS
 
     theirs, ours, panel_rows = products_of(place, live_rows, panel, trailing)
-    pair = ours + swap(theirs)
+    order = [3, 1, 2, 0]
+    arrived = {k: swap(theirs[k]) for k in order}
+    pair = {k: ours[k] + arrived[k] for k in order}
     slots = [pair[0]] + [send(pair[k], flat, SLOTS, k) for k in range(1, SLOTS)]
     summed = tree(slots)
     gram = summed[:tall]

time: 51.7 us -> 50.4 us (0.975)
  waiting for transfers between devices: 15.2 us -> 13.7 us
  starting transfers between devices: 21.1 us -> 21.8 us
  Pallas kernels: 13.5 us -> 12.9 us
    ppermute x3 -> x6, waiting for transfers between devices: 1.04 us -> 0.02 us  [swap(): return lax.ppermute(x, 'core', [(0, 1), (1, 0)])]
    ppermute x3 -> x6, starting transfers between devices: 0.66 us -> 1.25 us  [swap(): return lax.ppermute(x, 'core', [(0, 1), (1, 0)])]
    pallas_call x2, Pallas kernels: 3.32 us -> 2.75 us  [the longest x1 2.14 us: products_of(): pl.pallas_call(other_kernel, out_shape=(*out, jax.ShapeDtypeStruct((width...]
  transfers between devices with their start and end apart: 18 -> 21, of which waited for: 8 -> 6; matrix products, arithmetic and copies ran while one was open for 0% -> 0% of each run, Pallas kernels for 17% -> 18%
where the time goes in v7:
time: 50.4 us; the launch traced here: 50.2 us
  starting transfers between devices  21.8 us (43%)
  waiting for transfers between devices  13.7 us (27%)
  Pallas kernels  12.9 us (26%)
  between operations  1.47 us (3%)
    ppermute x15, starting transfers between devices, send(): return lax.ppermute(x, axes, [(i, i ^ shift) for i in range(size)])  20.6 us
    ppermute x15, waiting for transfers between devices, send(): return lax.ppermute(x, axes, [(i, i ^ shift) for i in range(size)])  13.7 us
    pallas_call x1, Pallas kernels, factor_of(): pl.pallas_call(factor_kernel, out_shape=(jax.ShapeDtypeStruct((width, 3 *...  6.37 us
    pallas_call x2, Pallas kernels, rest_of(): pl.pallas_call(functools.partial(rest_kernel, other), out_shape=[struct(w...  3.82 us
    pallas_call x1, Pallas kernels, products_of(): pl.pallas_call(other_kernel, out_shape=(*out, jax.ShapeDtypeStruct((width...  2.14 us
    ppermute x6, starting transfers between devices, swap(): return lax.ppermute(x, 'core', [(0, 1), (1, 0)])  1.25 us
  transfers between devices with their start and end apart: 21, of which 6 were waited for; matrix products, arithmetic and copies ran while one was open for 0% of the time, Pallas kernels for 18%

profile of v7, /device:TPU:0, one launch (start us, length us, event | category | flops | bytes accessed | tf_op | source)
XLA Modules:
  0.0 50.2 jit_solution(1581064706096471615)
XLA Ops:
  1.3 2.1 %products_other.1 = (f32[296,128]{1,0:T(8,128)S(1)}, f32[296,128]{1,0:T(8,128)S(1)}, f32[296,128]{1,0:T(8,128)S(1)}, f32[296,128]{1,0:T(8,128)S(1)}, bf16[256,11...) custom-call(s32[1]{0:T(128)} %bitcast.place_ref, ...), custom_call_target="tpu_custom_call" | custom-call | flops 301989888 | bytes 786432 | tf_op jit(solution)/shard_map/products_other/pallas_call | solution.py:170
  3.4 0.5 %collective-permute-start.1 = (f32[296,128]{1,0:T(8,128)S(1)}, f32[296,128]{1,0:T(8,128)S(1)}, u32[]{:S(2)}, u32[]{:S(2)}) collective-permute-start(f32[296,128]{1,0:T(8,128)S(1)} %get-tuple-element.37), channel_id=1, source_target_pairs={{0,1},{1,0},{2,3},{3,2},{4,5},{5,4},{6,7},{7,6},{8,9},{9,8},{10,11... | collective-permute-start | bytes 454664 | tf_op jit(solution)/shard_map/ppermute | solution.py:436
  4.5 0.6 %products_own.1 = (f32[296,128]{1,0:T(8,128)S(1)}, f32[296,128]{1,0:T(8,128)S(1)}, f32[296,128]{1,0:T(8,128)S(1)}, f32[296,128]{1,0:T(8,128)S(1)}, bf16[384,768]{1,0:T(8,128)(2,1)S(1)}) custom-call(s32[1]{0:T(128)} %bitcast.place_ref, s32[1]{0:T(128)S(6)} %copy.10.live_ref, bf16[256,1152]{1,0:T(8,128)(2,1)S(1)} %get-tuple-element.30.left_ref, ...), custom_call_target="tpu_custom_call" | custom-call | flops 301989888 | bytes 786432 | tf_op jit(solution)/shard_map/products_own/pallas_call | solution.py:188
  5.2 3.0 %collective-permute-start.2 = (f32[296,128]{1,0:T(8,128)S(1)}, f32[296,128]{1,0:T(8,128)S(1)}, u32[]{:S(2)}, u32[]{:S(2)}) collective-permute-start(f32[296,128]{1,0:T(8,128)S(1)} %add.44), channel_id=1, source_target_pairs={{0,2},{2,0},{4,6},{6,4},{1,3},{3,1},{5,7},{7,5},{8,10},{10,8},{12,... | collective-permute-start | bytes 454664 | tf_op jit(solution)/shard_map/ppermute | solution.py:440
  8.2 1.6 %collective-permute-start.4 = (f32[296,128]{1,0:T(8,128)S(1)}, f32[296,128]{1,0:T(8,128)S(1)}, u32[]{:S(2)}, u32[]{:S(2)}) collective-permute-start(f32[296,128]{1,0:T(8,128)S(1)} %add.46), channel_id=1, source_target_pairs={{0,4},{2,6},{4,0},{6,2},{1,5},{3,7},{5,1},{7,3},{8,12},{10,14},{12... | collective-permute-start | bytes 454664 | tf_op jit(solution)/shard_map/ppermute | solution.py:440
  9.9 2.8 %collective-permute-done.2 = f32[296,128]{1,0:T(8,128)S(1)} collective-permute-done((f32[296,128]{1,0:T(8,128)S(1)}, f32[296,128]{1,0:T(8,128)S(1)}, u32[]{:S(2)}, u32[]{:S(2)}) %collective-permute-start.2) | collective-permute-done | bytes 151584 | tf_op jit(solution)/shard_map/ppermute | solution.py:440
  12.7 4.4 %collective-permute-done.4 = f32[296,128]{1,0:T(8,128)S(1)} collective-permute-done((f32[296,128]{1,0:T(8,128)S(1)}, f32[296,128]{1,0:T(8,128)S(1)}, u32[]{:S(2)}, u32[]{:S(2)}) %collective-permute-start.4) | collective-permute-done | bytes 151584 | tf_op jit(solution)/shard_map/ppermute | solution.py:440
  17.3 3.7 %collective-permute-start.9 = (f32[104,128]{1,0:T(8,128)S(1)}, f32[104,128]{1,0:T(8,128)S(1)}, u32[]{:S(2)}, u32[]{:S(2)}) collective-permute-start(f32[104,128]{1,0:T(8,128)S(1)} %get-tuple-element.62), channel_id=1, source_target_pairs={{0,24},{8,16},{16,8},{24,0},{1,25},{9,17},{17,9},{25,1},{2,26},{10... | collective-permute-start | bytes 159752 | tf_op jit(solution)/shard_map/ppermute | solution.py:440
  20.9 0.8 %collective-permute-start.7 = (f32[104,128]{1,0:T(8,128)S(1)}, f32[104,128]{1,0:T(8,128)S(1)}, u32[]{:S(2)}, u32[]{:S(2)}) collective-permute-start(f32[104,128]{1,0:T(8,128)S(1)} %get-tuple-element.64), channel_id=1, source_target_pairs={{0,8},{8,0},{16,24},{24,16},{1,9},{9,1},{17,25},{25,17},{2,10},{10... | collective-permute-start | bytes 159752 | tf_op jit(solution)/shard_map/ppermute | solution.py:440
  21.7 1.6 %collective-permute-done.9 = f32[104,128]{1,0:T(8,128)S(1)} collective-permute-done((f32[104,128]{1,0:T(8,128)S(1)}, f32[104,128]{1,0:T(8,128)S(1)}, u32[]{:S(2)}, u32[]{:S(2)}) %collective-permute-start.9) | collective-permute-done | bytes 53280 | tf_op jit(solution)/shard_map/ppermute | solution.py:440
  23.4 2.6 %collective-permute-done.8 = f32[104,128]{1,0:T(8,128)S(1)} collective-permute-done((f32[104,128]{1,0:T(8,128)S(1)}, f32[104,128]{1,0:T(8,128)S(1)}, u32[]{:S(2)}, u32[]{:S(2)}) %collective-permute-start.8) | collective-permute-done | bytes 53280 | tf_op jit(solution)/shard_map/ppermute | solution.py:440
  26.0 1.5 %collective-permute-start.17 = (f32[40,128]{1,0:T(8,128)S(1)}, f32[40,128]{1,0:T(8,128)S(1)}, u32[]{:S(2)}, u32[]{:S(2)}) collective-permute-start(f32[40,128]{1,0:T(8,128)S(1)} %get-tuple-element.61), channel_id=1, source_target_pairs={{0,4},{2,6},{4,0},{6,2},{1,5},{3,7},{5,1},{7,3},{8,12},{10,14},{12... | collective-permute-start | bytes 61448 | tf_op jit(solution)/shard_map/ppermute | solution.py:440
  27.6 0.5 %collective-permute-start.16 = (f32[40,128]{1,0:T(8,128)S(1)}, f32[40,128]{1,0:T(8,128)S(1)}, u32[]{:S(2)}, u32[]{:S(2)}) collective-permute-start(f32[40,128]{1,0:T(8,128)S(1)} %get-tuple-element.61), channel_id=1, source_target_pairs={{0,2},{2,0},{4,6},{6,4},{1,3},{3,1},{5,7},{7,5},{8,10},{10,8},{12,... | collective-permute-start | bytes 61448 | tf_op jit(solution)/shard_map/ppermute | solution.py:440
  28.1 1.5 %collective-permute-start.18 = (f32[40,128]{1,0:T(8,128)S(1)}, f32[40,128]{1,0:T(8,128)S(1)}, u32[]{:S(2)}, u32[]{:S(2)}) collective-permute-start(f32[40,128]{1,0:T(8,128)S(1)} %get-tuple-element.61), channel_id=1, source_target_pairs={{0,6},{2,4},{4,2},{6,0},{1,7},{3,5},{5,3},{7,1},{8,14},{10,12},{12... | collective-permute-start | bytes 61448 | tf_op jit(solution)/shard_map/ppermute | solution.py:440
  29.6 1.7 %collective-permute-start.12 = (f32[64,128]{1,0:T(8,128)S(1)}, f32[64,128]{1,0:T(8,128)S(1)}, u32[]{:S(2)}, u32[]{:S(2)}) collective-permute-start(f32[64,128]{1,0:T(8,128)S(1)} %slice.30), channel_id=1, source_target_pairs={{0,24},{8,16},{16,8},{24,0},{1,25},{9,17},{17,9},{25,1},{2,26},{10... | collective-permute-start | bytes 98312 | tf_op jit(solution)/shard_map/ppermute | solution.py:440
  31.6 2.4 %collective-permute-start.10 = (f32[64,128]{1,0:T(8,128)S(1)}, f32[64,128]{1,0:T(8,128)S(1)}, u32[]{:S(2)}, u32[]{:S(2)}) collective-permute-start(f32[64,128]{1,0:T(8,128)S(1)} %slice.30), channel_id=1, source_target_pairs={{0,8},{8,0},{16,24},{24,16},{1,9},{9,1},{17,25},{25,17},{2,10},{10... | collective-permute-start | bytes 98312 | tf_op jit(solution)/shard_map/ppermute | solution.py:440
  34.1 1.2 %collective-permute-done.12 = f32[64,128]{1,0:T(8,128)S(1)} collective-permute-done((f32[64,128]{1,0:T(8,128)S(1)}, f32[64,128]{1,0:T(8,128)S(1)}, u32[]{:S(2)}, u32[]{:S(2)}) %collective-permute-start.12) | collective-permute-done | bytes 32800 | tf_op jit(solution)/shard_map/ppermute | solution.py:440
  35.3 0.9 %collective-permute-done.11 = f32[64,128]{1,0:T(8,128)S(1)} collective-permute-done((f32[64,128]{1,0:T(8,128)S(1)}, f32[64,128]{1,0:T(8,128)S(1)}, u32[]{:S(2)}, u32[]{:S(2)}) %collective-permute-start.11) | collective-permute-done | bytes 32800 | tf_op jit(solution)/shard_map/ppermute | solution.py:440
  36.3 1.5 %collective-permute-start.15 = (f32[256,128]{1,0:T(8,128)S(1)}, f32[256,128]{1,0:T(8,128)S(1)}, u32[]{:S(2)}, u32[]{:S(2)}) collective-permute-start(f32[256,128]{1,0:T(8,128)S(1)} %pad_maximum_fusion.1), channel_id=1, source_target_pairs={{0,6},{2,4},{4,2},{6,0},{1,7},{3,5},{5,3},{7,1},{8,14},{10,12},{12... | collective-permute-start | bytes 393224 | tf_op jit(solution)/shard_map/ppermute | solution.py:440
  37.8 1.5 %collective-permute-start.14 = (f32[256,128]{1,0:T(8,128)S(1)}, f32[256,128]{1,0:T(8,128)S(1)}, u32[]{:S(2)}, u32[]{:S(2)}) collective-permute-start(f32[256,128]{1,0:T(8,128)S(1)} %pad_maximum_fusion.1), channel_id=1, source_target_pairs={{0,4},{2,6},{4,0},{6,2},{1,5},{3,7},{5,1},{7,3},{8,12},{10,14},{12... | collective-permute-start | bytes 393224 | tf_op jit(solution)/shard_map/ppermute | solution.py:440
  39.3 0.6 %collective-permute-start.13 = (f32[256,128]{1,0:T(8,128)S(1)}, f32[256,128]{1,0:T(8,128)S(1)}, u32[]{:S(2)}, u32[]{:S(2)}) collective-permute-start(f32[256,128]{1,0:T(8,128)S(1)} %pad_maximum_fusion.1), channel_id=1, source_target_pairs={{0,2},{2,0},{4,6},{6,4},{1,3},{3,1},{5,7},{7,5},{8,10},{10,8},{12,... | collective-permute-start | bytes 393224 | tf_op jit(solution)/shard_map/ppermute | solution.py:440
  39.8 6.4 %factor.1 = (bf16[256,768]{1,0:T(8,128)(2,1)S(1)}, bf16[384,768]{1,0:T(8,128)(2,1)S(1)}, f32[384,256]{1,0:T(8,128)S(1)}, f32[8,128]{1,0:T(8,128)S(1)}) custom-call(s32[1]{0:T(128)} %bitcast.place_ref, f32[4,40,128]{2,1,0:T(8,128)S(1)} %pad_maximum_fusion.2.own_ref, f32[4,40,128]{2,1,0:T(8,128)S(1)} %collective-permute-done.19.other_ref, ...), custom_call_target="tpu_custom_call" | custom-call | flops 6000000000 | bytes 393216 | tf_op jit(solution)/shard_map/factor/pallas_call | solution.py:337
  46.4 2.0 %rest_own.1 = (f32[256,256]{1,0:T(8,128)}, f32[384,1024]{1,0:T(8,128)}, f32[384,256]{1,0:T(8,128)}) custom-call(s32[1]{0:T(128)} %bitcast.place_ref, s32[1]{0:T(128)S(6)} %copy.10.live_ref, bf16[256,768]{1,0:T(8,128)(2,1)S(1)} %get-tuple-element.44.inverse_ref, bf16[384,768]{1,0:T(8,128)(2,1)S(1)} %get-tuple-element.45.split_ref, ...), custom_call_target="tpu_custom_call" | custom-call | flops 503316480 | bytes 1572864 | tf_op jit(solution)/shard_map/rest_own/pallas_call | solution.py:415
  48.4 1.8 %rest_other.1 = (f32[256,256]{1,0:T(8,128)}, f32[384,1024]{1,0:T(8,128)}) custom-call(s32[1]{0:T(128)} %bitcast.place_ref, s32[1]{0:T(128)S(6)} %copy.10.live_ref, bf16[256,768]{1,0:T(8,128)(2,1)S(1)} %get-tuple-element.44.inverse_ref, bf16[384,768]{1,0:T(8,128)(2,1)S(1)} %get-tuple-element.45.split_ref, ...), custom_call_target="tpu_custom_call", output_to_operand_aliasing={{0}: (6, {}), {1}: (7, {})} | custom-call | flops 503316480 | bytes 1572864 | tf_op jit(solution)/shard_map/rest_other/pallas_call | solution.py:415
  (38 shorter events, 1.3 us)
Async XLA Ops:
  3.4 1.7 %collective-permute-start.1 = (f32[296,128]{1,0:T(8,128)S(1)}, f32[296,128]{1,0:T(8,128)S(1)}, u32[]{:S(2)}, u32[]{:S(2)}) collective-permute-start(f32[296,128]{1,0:T(8,128)S(1)} %get-tuple-element.37), channel_id=1, source_target_pairs={{0,1},{1,0},{2,3},{3,2},{4,5},{5,4},{6,7},{7,6},{8,9},{9,8},{10,11... | collective-permute-start | bytes 454664 | tf_op jit(solution)/shard_map/ppermute | solution.py:436
  4.0 4.2 %collective-permute-start.3 = (f32[296,128]{1,0:T(8,128)S(1)}, f32[296,128]{1,0:T(8,128)S(1)}, u32[]{:S(2)}, u32[]{:S(2)}) collective-permute-start(f32[296,128]{1,0:T(8,128)S(1)} %get-tuple-element.39), channel_id=1, source_target_pairs={{0,1},{1,0},{2,3},{3,2},{4,5},{5,4},{6,7},{7,6},{8,9},{9,8},{10,11... | collective-permute-start | bytes 454664 | tf_op jit(solution)/shard_map/ppermute | solution.py:436
  4.0 5.8 %collective-permute-start.5 = (f32[296,128]{1,0:T(8,128)S(1)}, f32[296,128]{1,0:T(8,128)S(1)}, u32[]{:S(2)}, u32[]{:S(2)}) collective-permute-start(f32[296,128]{1,0:T(8,128)S(1)} %get-tuple-element.41), channel_id=1, source_target_pairs={{0,1},{1,0},{2,3},{3,2},{4,5},{5,4},{6,7},{7,6},{8,9},{9,8},{10,11... | collective-permute-start | bytes 454664 | tf_op jit(solution)/shard_map/ppermute | solution.py:436
  4.5 5.4 %collective-permute-start = (f32[296,128]{1,0:T(8,128)S(1)}, f32[296,128]{1,0:T(8,128)S(1)}, u32[]{:S(2)}, u32[]{:S(2)}) collective-permute-start(f32[296,128]{1,0:T(8,128)S(1)} %get-tuple-element.35), channel_id=1, source_target_pairs={{0,1},{1,0},{2,3},{3,2},{4,5},{5,4},{6,7},{7,6},{8,9},{9,8},{10,11... | collective-permute-start | bytes 454664 | tf_op jit(solution)/shard_map/ppermute | solution.py:436
  5.2 7.5 %collective-permute-start.2 = (f32[296,128]{1,0:T(8,128)S(1)}, f32[296,128]{1,0:T(8,128)S(1)}, u32[]{:S(2)}, u32[]{:S(2)}) collective-permute-start(f32[296,128]{1,0:T(8,128)S(1)} %add.44), channel_id=1, source_target_pairs={{0,2},{2,0},{4,6},{6,4},{1,3},{3,1},{5,7},{7,5},{8,10},{10,8},{12,... | collective-permute-start | bytes 454664 | tf_op jit(solution)/shard_map/ppermute | solution.py:440
  8.2 9.0 %collective-permute-start.4 = (f32[296,128]{1,0:T(8,128)S(1)}, f32[296,128]{1,0:T(8,128)S(1)}, u32[]{:S(2)}, u32[]{:S(2)}) collective-permute-start(f32[296,128]{1,0:T(8,128)S(1)} %add.46), channel_id=1, source_target_pairs={{0,4},{2,6},{4,0},{6,2},{1,5},{3,7},{5,1},{7,3},{8,12},{10,14},{12... | collective-permute-start | bytes 454664 | tf_op jit(solution)/shard_map/ppermute | solution.py:440
  9.8 7.3 %collective-permute-start.6 = (f32[296,128]{1,0:T(8,128)S(1)}, f32[296,128]{1,0:T(8,128)S(1)}, u32[]{:S(2)}, u32[]{:S(2)}) collective-permute-start(f32[296,128]{1,0:T(8,128)S(1)} %add.47), channel_id=1, source_target_pairs={{0,6},{2,4},{4,2},{6,0},{1,7},{3,5},{5,3},{7,1},{8,14},{10,12},{12... | collective-permute-start | bytes 454664 | tf_op jit(solution)/shard_map/ppermute | solution.py:440
  17.3 6.1 %collective-permute-start.9 = (f32[104,128]{1,0:T(8,128)S(1)}, f32[104,128]{1,0:T(8,128)S(1)}, u32[]{:S(2)}, u32[]{:S(2)}) collective-permute-start(f32[104,128]{1,0:T(8,128)S(1)} %get-tuple-element.62), channel_id=1, source_target_pairs={{0,24},{8,16},{16,8},{24,0},{1,25},{9,17},{17,9},{25,1},{2,26},{10... | collective-permute-start | bytes 159752 | tf_op jit(solution)/shard_map/ppermute | solution.py:440
  20.9 5.1 %collective-permute-start.8 = (f32[104,128]{1,0:T(8,128)S(1)}, f32[104,128]{1,0:T(8,128)S(1)}, u32[]{:S(2)}, u32[]{:S(2)}) collective-permute-start(f32[104,128]{1,0:T(8,128)S(1)} %get-tuple-element.63), channel_id=1, source_target_pairs={{0,16},{8,24},{16,0},{24,8},{1,17},{9,25},{17,1},{25,9},{2,18},{10... | collective-permute-start | bytes 159752 | tf_op jit(solution)/shard_map/ppermute | solution.py:440
  20.9 5.1 %collective-permute-start.7 = (f32[104,128]{1,0:T(8,128)S(1)}, f32[104,128]{1,0:T(8,128)S(1)}, u32[]{:S(2)}, u32[]{:S(2)}) collective-permute-start(f32[104,128]{1,0:T(8,128)S(1)} %get-tuple-element.64), channel_id=1, source_target_pairs={{0,8},{8,0},{16,24},{24,16},{1,9},{9,1},{17,25},{25,17},{2,10},{10... | collective-permute-start | bytes 159752 | tf_op jit(solution)/shard_map/ppermute | solution.py:440
  26.0 5.5 %collective-permute-start.17 = (f32[40,128]{1,0:T(8,128)S(1)}, f32[40,128]{1,0:T(8,128)S(1)}, u32[]{:S(2)}, u32[]{:S(2)}) collective-permute-start(f32[40,128]{1,0:T(8,128)S(1)} %get-tuple-element.61), channel_id=1, source_target_pairs={{0,4},{2,6},{4,0},{6,2},{1,5},{3,7},{5,1},{7,3},{8,12},{10,14},{12... | collective-permute-start | bytes 61448 | tf_op jit(solution)/shard_map/ppermute | solution.py:440
  27.6 6.4 %collective-permute-start.16 = (f32[40,128]{1,0:T(8,128)S(1)}, f32[40,128]{1,0:T(8,128)S(1)}, u32[]{:S(2)}, u32[]{:S(2)}) collective-permute-start(f32[40,128]{1,0:T(8,128)S(1)} %get-tuple-element.61), channel_id=1, source_target_pairs={{0,2},{2,0},{4,6},{6,4},{1,3},{3,1},{5,7},{7,5},{8,10},{10,8},{12,... | collective-permute-start | bytes 61448 | tf_op jit(solution)/shard_map/ppermute | solution.py:440
  28.1 5.9 %collective-permute-start.18 = (f32[40,128]{1,0:T(8,128)S(1)}, f32[40,128]{1,0:T(8,128)S(1)}, u32[]{:S(2)}, u32[]{:S(2)}) collective-permute-start(f32[40,128]{1,0:T(8,128)S(1)} %get-tuple-element.61), channel_id=1, source_target_pairs={{0,6},{2,4},{4,2},{6,0},{1,7},{3,5},{5,3},{7,1},{8,14},{10,12},{12... | collective-permute-start | bytes 61448 | tf_op jit(solution)/shard_map/ppermute | solution.py:440
  29.6 5.7 %collective-permute-start.12 = (f32[64,128]{1,0:T(8,128)S(1)}, f32[64,128]{1,0:T(8,128)S(1)}, u32[]{:S(2)}, u32[]{:S(2)}) collective-permute-start(f32[64,128]{1,0:T(8,128)S(1)} %slice.30), channel_id=1, source_target_pairs={{0,24},{8,16},{16,8},{24,0},{1,25},{9,17},{17,9},{25,1},{2,26},{10... | collective-permute-start | bytes 98312 | tf_op jit(solution)/shard_map/ppermute | solution.py:440
  31.3 4.9 %collective-permute-start.11 = (f32[64,128]{1,0:T(8,128)S(1)}, f32[64,128]{1,0:T(8,128)S(1)}, u32[]{:S(2)}, u32[]{:S(2)}) collective-permute-start(f32[64,128]{1,0:T(8,128)S(1)} %slice.30), channel_id=1, source_target_pairs={{0,16},{8,24},{16,0},{24,8},{1,17},{9,25},{17,1},{25,9},{2,18},{10... | collective-permute-start | bytes 98312 | tf_op jit(solution)/shard_map/ppermute | solution.py:440
  31.6 4.6 %collective-permute-start.10 = (f32[64,128]{1,0:T(8,128)S(1)}, f32[64,128]{1,0:T(8,128)S(1)}, u32[]{:S(2)}, u32[]{:S(2)}) collective-permute-start(f32[64,128]{1,0:T(8,128)S(1)} %slice.30), channel_id=1, source_target_pairs={{0,8},{8,0},{16,24},{24,16},{1,9},{9,1},{17,25},{25,17},{2,10},{10... | collective-permute-start | bytes 98312 | tf_op jit(solution)/shard_map/ppermute | solution.py:440
  34.0 5.8 %collective-permute-start.19 = (f32[4,40,128]{2,1,0:T(8,128)S(1)}, f32[4,40,128]{2,1,0:T(8,128)S(1)}, u32[]{:S(2)}, u32[]{:S(2)}) collective-permute-start(f32[4,40,128]{2,1,0:T(8,128)S(1)} %pad_maximum_fusion.2.own_ref), channel_id=1, source_target_pairs={{0,1},{1,0},{2,3},{3,2},{4,5},{5,4},{6,7},{7,6},{8,9},{9,8},{10,11... | collective-permute-start | bytes 245768 | tf_op jit(solution)/shard_map/ppermute | solution.py:436
  36.3 9.9 %collective-permute-start.15 = (f32[256,128]{1,0:T(8,128)S(1)}, f32[256,128]{1,0:T(8,128)S(1)}, u32[]{:S(2)}, u32[]{:S(2)}) collective-permute-start(f32[256,128]{1,0:T(8,128)S(1)} %pad_maximum_fusion.1), channel_id=1, source_target_pairs={{0,6},{2,4},{4,2},{6,0},{1,7},{3,5},{5,3},{7,1},{8,14},{10,12},{12... | collective-permute-start | bytes 393224 | tf_op jit(solution)/shard_map/ppermute | solution.py:440
  37.8 8.4 %collective-permute-start.14 = (f32[256,128]{1,0:T(8,128)S(1)}, f32[256,128]{1,0:T(8,128)S(1)}, u32[]{:S(2)}, u32[]{:S(2)}) collective-permute-start(f32[256,128]{1,0:T(8,128)S(1)} %pad_maximum_fusion.1), channel_id=1, source_target_pairs={{0,4},{2,6},{4,0},{6,2},{1,5},{3,7},{5,1},{7,3},{8,12},{10,14},{12... | collective-permute-start | bytes 393224 | tf_op jit(solution)/shard_map/ppermute | solution.py:440
  39.3 7.0 %collective-permute-start.13 = (f32[256,128]{1,0:T(8,128)S(1)}, f32[256,128]{1,0:T(8,128)S(1)}, u32[]{:S(2)}, u32[]{:S(2)}) collective-permute-start(f32[256,128]{1,0:T(8,128)S(1)} %pad_maximum_fusion.1), channel_id=1, source_target_pairs={{0,2},{2,0},{4,6},{6,4},{1,3},{3,1},{5,7},{7,5},{8,10},{10,8},{12,... | collective-permute-start | bytes 393224 | tf_op jit(solution)/shard_map/ppermute | solution.py:440
  39.8 6.5 %copy-start = (f32[384,1024]{1,0:T(8,128)S(1)}, f32[384,1024]{1,0:T(8,128)}, u32[]{:S(2)}) copy-start(f32[384,1024]{1,0:T(8,128)} %trail_ref.5) | copy-start | bytes 4718596
  46.3 2.1 %collective-permute-start.20 = (f32[4,256,128]{2,1,0:T(8,128)S(1)}, f32[4,256,128]{2,1,0:T(8,128)S(1)}, u32[]{:S(2)}, u32[]{:S(2)}) collective-permute-start(f32[4,256,128]{2,1,0:T(8,128)S(1)} %pad_maximum_fusion.cross_ref), channel_id=1, source_target_pairs={{0,1},{1,0},{2,3},{3,2},{4,5},{5,4},{6,7},{7,6},{8,9},{9,8},{10,11... | collective-permute-start | bytes 1572872 | tf_op jit(solution)/shard_map/ppermute | solution.py:436

commit v8 on v7

--- a/solution.py
+++ b/solution.py
@@ -468,7 +468,8 @@
         summed = lax.psum(summed, "far")
     gram, cross = summed[:tall], summed[tall:]
     gram_own = jnp.stack([gram] + [send(gram, flat, SLOTS, k) for k in range(1, SLOTS)])
-    cross = jnp.concatenate([cross] + [send(cross, deep, PARTS, j) for j in range(1, PARTS)])
+    cross = jnp.concatenate([cross, send(cross, deep, PARTS, 1)])
+    cross = jnp.concatenate([cross, send(cross, deep, PARTS, 2)])
     cross_own = [cross] + [send(cross, flat, SLOTS, k) for k in range(1, SLOTS)]
     inverse, split, unit, root = factor_of(place, gram_own, swap(gram_own), panel_rows)
     *cross_own, inverse = lax.optimization_barrier((*cross_own, inverse))

time: 50.4 us -> 49.3 us (0.978)
  starting transfers between devices: 21.8 us -> 19.7 us
  waiting for transfers between devices: 13.7 us -> 14.8 us
    ppermute x15 -> x14, starting transfers between devices: 20.6 us -> 18.4 us  [send(): return lax.ppermute(x, axes, [(i, i ^ shift) for i in range(size)])]
    ppermute x15 -> x14, waiting for transfers between devices: 13.7 us -> 14.8 us  [send(): return lax.ppermute(x, axes, [(i, i ^ shift) for i in range(size)])]
  transfers between devices with their start and end apart: 21 -> 20, of which waited for: 6 -> 7; matrix products, arithmetic and copies ran while one was open for 0% -> 0% of each run, Pallas kernels for 18% -> 18%
where the time goes in v8:
time: 49.3 us; the launch traced here: 49.2 us
  starting transfers between devices  19.7 us (40%)
  waiting for transfers between devices  14.8 us (30%)
  Pallas kernels  12.9 us (26%)
  between operations  1.47 us (3%)
    ppermute x14, starting transfers between devices, send(): return lax.ppermute(x, axes, [(i, i ^ shift) for i in range(size)])  18.4 us
    ppermute x14, waiting for transfers between devices, send(): return lax.ppermute(x, axes, [(i, i ^ shift) for i in range(size)])  14.8 us
    pallas_call x1, Pallas kernels, factor_of(): pl.pallas_call(factor_kernel, out_shape=(jax.ShapeDtypeStruct((width, 3 *...  6.37 us
    pallas_call x2, Pallas kernels, rest_of(): pl.pallas_call(functools.partial(rest_kernel, other), out_shape=[struct(w...  3.82 us
    pallas_call x1, Pallas kernels, products_of(): pl.pallas_call(other_kernel, out_shape=(*out, jax.ShapeDtypeStruct((width...  2.14 us
    ppermute x6, starting transfers between devices, swap(): return lax.ppermute(x, 'core', [(0, 1), (1, 0)])  1.24 us
  transfers between devices with their start and end apart: 20, of which 7 were waited for; matrix products, arithmetic and copies ran while one was open for 0% of the time, Pallas kernels for 18%

profile of v8, /device:TPU:0, one launch (start us, length us, event | category | flops | bytes accessed | tf_op | source)
XLA Modules:
  0.0 49.2 jit_solution(8241939415809793067)
XLA Ops:
  1.3 2.1 %products_other.1 = (f32[296,128]{1,0:T(8,128)S(1)}, f32[296,128]{1,0:T(8,128)S(1)}, f32[296,128]{1,0:T(8,128)S(1)}, f32[296,128]{1,0:T(8,128)S(1)}, bf16[256,11...) custom-call(s32[1]{0:T(128)} %bitcast.place_ref, ...), custom_call_target="tpu_custom_call" | custom-call | flops 301989888 | bytes 786432 | tf_op jit(solution)/shard_map/products_other/pallas_call | solution.py:170
  3.4 0.5 %collective-permute-start.1 = (f32[296,128]{1,0:T(8,128)S(1)}, f32[296,128]{1,0:T(8,128)S(1)}, u32[]{:S(2)}, u32[]{:S(2)}) collective-permute-start(f32[296,128]{1,0:T(8,128)S(1)} %get-tuple-element.37), channel_id=1, source_target_pairs={{0,1},{1,0},{2,3},{3,2},{4,5},{5,4},{6,7},{7,6},{8,9},{9,8},{10,11... | collective-permute-start | bytes 454664 | tf_op jit(solution)/shard_map/ppermute | solution.py:436
  4.0 0.4 collective-permute-start.5
  4.5 0.6 %products_own.1 = (f32[296,128]{1,0:T(8,128)S(1)}, f32[296,128]{1,0:T(8,128)S(1)}, f32[296,128]{1,0:T(8,128)S(1)}, f32[296,128]{1,0:T(8,128)S(1)}, bf16[384,768]{1,0:T(8,128)(2,1)S(1)}) custom-call(s32[1]{0:T(128)} %bitcast.place_ref, s32[1]{0:T(128)S(6)} %copy.10.live_ref, bf16[256,1152]{1,0:T(8,128)(2,1)S(1)} %get-tuple-element.30.left_ref, ...), custom_call_target="tpu_custom_call" | custom-call | flops 301989888 | bytes 786432 | tf_op jit(solution)/shard_map/products_own/pallas_call | solution.py:188
  5.2 3.0 %collective-permute-start.2 = (f32[296,128]{1,0:T(8,128)S(1)}, f32[296,128]{1,0:T(8,128)S(1)}, u32[]{:S(2)}, u32[]{:S(2)}) collective-permute-start(f32[296,128]{1,0:T(8,128)S(1)} %add.44), channel_id=1, source_target_pairs={{0,2},{2,0},{4,6},{6,4},{1,3},{3,1},{5,7},{7,5},{8,10},{10,8},{12,... | collective-permute-start | bytes 454664 | tf_op jit(solution)/shard_map/ppermute | solution.py:440
  8.2 1.6 %collective-permute-start.4 = (f32[296,128]{1,0:T(8,128)S(1)}, f32[296,128]{1,0:T(8,128)S(1)}, u32[]{:S(2)}, u32[]{:S(2)}) collective-permute-start(f32[296,128]{1,0:T(8,128)S(1)} %add.46), channel_id=1, source_target_pairs={{0,4},{2,6},{4,0},{6,2},{1,5},{3,7},{5,1},{7,3},{8,12},{10,14},{12... | collective-permute-start | bytes 454664 | tf_op jit(solution)/shard_map/ppermute | solution.py:440
  9.9 2.8 %collective-permute-done.2 = f32[296,128]{1,0:T(8,128)S(1)} collective-permute-done((f32[296,128]{1,0:T(8,128)S(1)}, f32[296,128]{1,0:T(8,128)S(1)}, u32[]{:S(2)}, u32[]{:S(2)}) %collective-permute-start.2) | collective-permute-done | bytes 151584 | tf_op jit(solution)/shard_map/ppermute | solution.py:440
  12.7 4.4 %collective-permute-done.4 = f32[296,128]{1,0:T(8,128)S(1)} collective-permute-done((f32[296,128]{1,0:T(8,128)S(1)}, f32[296,128]{1,0:T(8,128)S(1)}, u32[]{:S(2)}, u32[]{:S(2)}) %collective-permute-start.4) | collective-permute-done | bytes 151584 | tf_op jit(solution)/shard_map/ppermute | solution.py:440
  17.3 3.7 %collective-permute-start.9 = (f32[104,128]{1,0:T(8,128)S(1)}, f32[104,128]{1,0:T(8,128)S(1)}, u32[]{:S(2)}, u32[]{:S(2)}) collective-permute-start(f32[104,128]{1,0:T(8,128)S(1)} %get-tuple-element.62), channel_id=1, source_target_pairs={{0,24},{8,16},{16,8},{24,0},{1,25},{9,17},{17,9},{25,1},{2,26},{10... | collective-permute-start | bytes 159752 | tf_op jit(solution)/shard_map/ppermute | solution.py:440
  20.9 0.8 %collective-permute-start.7 = (f32[104,128]{1,0:T(8,128)S(1)}, f32[104,128]{1,0:T(8,128)S(1)}, u32[]{:S(2)}, u32[]{:S(2)}) collective-permute-start(f32[104,128]{1,0:T(8,128)S(1)} %get-tuple-element.64), channel_id=1, source_target_pairs={{0,8},{8,0},{16,24},{24,16},{1,9},{9,1},{17,25},{25,17},{2,10},{10... | collective-permute-start | bytes 159752 | tf_op jit(solution)/shard_map/ppermute | solution.py:440
  21.7 1.6 %collective-permute-done.9 = f32[104,128]{1,0:T(8,128)S(1)} collective-permute-done((f32[104,128]{1,0:T(8,128)S(1)}, f32[104,128]{1,0:T(8,128)S(1)}, u32[]{:S(2)}, u32[]{:S(2)}) %collective-permute-start.9) | collective-permute-done | bytes 53280 | tf_op jit(solution)/shard_map/ppermute | solution.py:440
  23.4 2.6 %collective-permute-done.8 = f32[104,128]{1,0:T(8,128)S(1)} collective-permute-done((f32[104,128]{1,0:T(8,128)S(1)}, f32[104,128]{1,0:T(8,128)S(1)}, u32[]{:S(2)}, u32[]{:S(2)}) %collective-permute-start.8) | collective-permute-done | bytes 53280 | tf_op jit(solution)/shard_map/ppermute | solution.py:440
  26.4 1.5 %collective-permute-start.16 = (f32[40,128]{1,0:T(8,128)S(1)}, f32[40,128]{1,0:T(8,128)S(1)}, u32[]{:S(2)}, u32[]{:S(2)}) collective-permute-start(f32[40,128]{1,0:T(8,128)S(1)} %get-tuple-element.61), channel_id=1, source_target_pairs={{0,4},{2,6},{4,0},{6,2},{1,5},{3,7},{5,1},{7,3},{8,12},{10,14},{12... | collective-permute-start | bytes 61448 | tf_op jit(solution)/shard_map/ppermute | solution.py:440
  27.9 0.5 %collective-permute-start.15 = (f32[40,128]{1,0:T(8,128)S(1)}, f32[40,128]{1,0:T(8,128)S(1)}, u32[]{:S(2)}, u32[]{:S(2)}) collective-permute-start(f32[40,128]{1,0:T(8,128)S(1)} %get-tuple-element.61), channel_id=1, source_target_pairs={{0,2},{2,0},{4,6},{6,4},{1,3},{3,1},{5,7},{7,5},{8,10},{10,8},{12,... | collective-permute-start | bytes 61448 | tf_op jit(solution)/shard_map/ppermute | solution.py:440
  28.4 1.4 %collective-permute-start.17 = (f32[40,128]{1,0:T(8,128)S(1)}, f32[40,128]{1,0:T(8,128)S(1)}, u32[]{:S(2)}, u32[]{:S(2)}) collective-permute-start(f32[40,128]{1,0:T(8,128)S(1)} %get-tuple-element.61), channel_id=1, source_target_pairs={{0,6},{2,4},{4,2},{6,0},{1,7},{3,5},{5,3},{7,1},{8,14},{10,12},{12... | collective-permute-start | bytes 61448 | tf_op jit(solution)/shard_map/ppermute | solution.py:440
  30.0 2.0 %collective-permute-start.11 = (f32[128,128]{1,0:T(8,128)S(1)}, f32[128,128]{1,0:T(8,128)S(1)}, u32[]{:S(2)}, u32[]{:S(2)}) collective-permute-start(f32[128,128]{1,0:T(8,128)S(1)} %pad_maximum_fusion.6), channel_id=1, source_target_pairs={{0,16},{8,24},{16,0},{24,8},{1,17},{9,25},{17,1},{25,9},{2,18},{10... | collective-permute-start | bytes 196616 | tf_op jit(solution)/shard_map/ppermute | solution.py:440
  32.0 1.1 %collective-permute-done.17 = f32[40,128]{1,0:T(8,128)S(1)} collective-permute-done((f32[40,128]{1,0:T(8,128)S(1)}, f32[40,128]{1,0:T(8,128)S(1)}, u32[]{:S(2)}, u32[]{:S(2)}) %collective-permute-start.17) | collective-permute-done | bytes 20512 | tf_op jit(solution)/shard_map/ppermute | solution.py:440
  33.2 2.0 %collective-permute-done.11 = f32[128,128]{1,0:T(8,128)S(1)} collective-permute-done((f32[128,128]{1,0:T(8,128)S(1)}, f32[128,128]{1,0:T(8,128)S(1)}, u32[]{:S(2)}, u32[]{:S(2)}) %collective-permute-start.11) | collective-permute-done | bytes 65568 | tf_op jit(solution)/shard_map/ppermute | solution.py:440
  35.2 1.5 %collective-permute-start.14 = (f32[256,128]{1,0:T(8,128)S(1)}, f32[256,128]{1,0:T(8,128)S(1)}, u32[]{:S(2)}, u32[]{:S(2)}) collective-permute-start(f32[256,128]{1,0:T(8,128)S(1)} %pad_maximum_fusion.1), channel_id=1, source_target_pairs={{0,6},{2,4},{4,2},{6,0},{1,7},{3,5},{5,3},{7,1},{8,14},{10,12},{12... | collective-permute-start | bytes 393224 | tf_op jit(solution)/shard_map/ppermute | solution.py:440
  36.7 1.1 %collective-permute-start.13 = (f32[256,128]{1,0:T(8,128)S(1)}, f32[256,128]{1,0:T(8,128)S(1)}, u32[]{:S(2)}, u32[]{:S(2)}) collective-permute-start(f32[256,128]{1,0:T(8,128)S(1)} %pad_maximum_fusion.1), channel_id=1, source_target_pairs={{0,4},{2,6},{4,0},{6,2},{1,5},{3,7},{5,1},{7,3},{8,12},{10,14},{12... | collective-permute-start | bytes 393224 | tf_op jit(solution)/shard_map/ppermute | solution.py:440
  37.8 0.9 %collective-permute-start.12 = (f32[256,128]{1,0:T(8,128)S(1)}, f32[256,128]{1,0:T(8,128)S(1)}, u32[]{:S(2)}, u32[]{:S(2)}) collective-permute-start(f32[256,128]{1,0:T(8,128)S(1)} %pad_maximum_fusion.1), channel_id=1, source_target_pairs={{0,2},{2,0},{4,6},{6,4},{1,3},{3,1},{5,7},{7,5},{8,10},{10,8},{12,... | collective-permute-start | bytes 393224 | tf_op jit(solution)/shard_map/ppermute | solution.py:440
  38.8 6.4 %factor.1 = (bf16[256,768]{1,0:T(8,128)(2,1)S(1)}, bf16[384,768]{1,0:T(8,128)(2,1)S(1)}, f32[384,256]{1,0:T(8,128)S(1)}, f32[8,128]{1,0:T(8,128)S(1)}) custom-call(s32[1]{0:T(128)} %bitcast.place_ref, f32[4,40,128]{2,1,0:T(8,128)S(1)} %pad_maximum_fusion.2.own_ref, f32[4,40,128]{2,1,0:T(8,128)S(1)} %collective-permute-done.18.other_ref, ...), custom_call_target="tpu_custom_call" | custom-call | flops 6000000000 | bytes 393216 | tf_op jit(solution)/shard_map/factor/pallas_call | solution.py:337
  45.3 2.0 %rest_own.1 = (f32[256,256]{1,0:T(8,128)}, f32[384,1024]{1,0:T(8,128)}, f32[384,256]{1,0:T(8,128)}) custom-call(s32[1]{0:T(128)} %bitcast.place_ref, s32[1]{0:T(128)S(6)} %copy.10.live_ref, bf16[256,768]{1,0:T(8,128)(2,1)S(1)} %get-tuple-element.44.inverse_ref, bf16[384,768]{1,0:T(8,128)(2,1)S(1)} %get-tuple-element.45.split_ref, ...), custom_call_target="tpu_custom_call" | custom-call | flops 503316480 | bytes 1572864 | tf_op jit(solution)/shard_map/rest_own/pallas_call | solution.py:415
  47.3 1.8 %rest_other.1 = (f32[256,256]{1,0:T(8,128)}, f32[384,1024]{1,0:T(8,128)}) custom-call(s32[1]{0:T(128)} %bitcast.place_ref, s32[1]{0:T(128)S(6)} %copy.10.live_ref, bf16[256,768]{1,0:T(8,128)(2,1)S(1)} %get-tuple-element.44.inverse_ref, bf16[384,768]{1,0:T(8,128)(2,1)S(1)} %get-tuple-element.45.split_ref, ...), custom_call_target="tpu_custom_call", output_to_operand_aliasing={{0}: (6, {}), {1}: (7, {})} | custom-call | flops 503316480 | bytes 1572864 | tf_op jit(solution)/shard_map/rest_other/pallas_call | solution.py:415
  (37 shorter events, 1.1 us)
Async XLA Ops:
  3.4 1.7 %collective-permute-start.1 = (f32[296,128]{1,0:T(8,128)S(1)}, f32[296,128]{1,0:T(8,128)S(1)}, u32[]{:S(2)}, u32[]{:S(2)}) collective-permute-start(f32[296,128]{1,0:T(8,128)S(1)} %get-tuple-element.37), channel_id=1, source_target_pairs={{0,1},{1,0},{2,3},{3,2},{4,5},{5,4},{6,7},{7,6},{8,9},{9,8},{10,11... | collective-permute-start | bytes 454664 | tf_op jit(solution)/shard_map/ppermute | solution.py:436
  4.0 4.2 %collective-permute-start.3 = (f32[296,128]{1,0:T(8,128)S(1)}, f32[296,128]{1,0:T(8,128)S(1)}, u32[]{:S(2)}, u32[]{:S(2)}) collective-permute-start(f32[296,128]{1,0:T(8,128)S(1)} %get-tuple-element.39), channel_id=1, source_target_pairs={{0,1},{1,0},{2,3},{3,2},{4,5},{5,4},{6,7},{7,6},{8,9},{9,8},{10,11... | collective-permute-start | bytes 454664 | tf_op jit(solution)/shard_map/ppermute | solution.py:436
  4.0 5.8 %collective-permute-start.5 = (f32[296,128]{1,0:T(8,128)S(1)}, f32[296,128]{1,0:T(8,128)S(1)}, u32[]{:S(2)}, u32[]{:S(2)}) collective-permute-start(f32[296,128]{1,0:T(8,128)S(1)} %get-tuple-element.41), channel_id=1, source_target_pairs={{0,1},{1,0},{2,3},{3,2},{4,5},{5,4},{6,7},{7,6},{8,9},{9,8},{10,11... | collective-permute-start | bytes 454664 | tf_op jit(solution)/shard_map/ppermute | solution.py:436
  4.5 5.4 %collective-permute-start = (f32[296,128]{1,0:T(8,128)S(1)}, f32[296,128]{1,0:T(8,128)S(1)}, u32[]{:S(2)}, u32[]{:S(2)}) collective-permute-start(f32[296,128]{1,0:T(8,128)S(1)} %get-tuple-element.35), channel_id=1, source_target_pairs={{0,1},{1,0},{2,3},{3,2},{4,5},{5,4},{6,7},{7,6},{8,9},{9,8},{10,11... | collective-permute-start | bytes 454664 | tf_op jit(solution)/shard_map/ppermute | solution.py:436
  5.2 7.5 %collective-permute-start.2 = (f32[296,128]{1,0:T(8,128)S(1)}, f32[296,128]{1,0:T(8,128)S(1)}, u32[]{:S(2)}, u32[]{:S(2)}) collective-permute-start(f32[296,128]{1,0:T(8,128)S(1)} %add.44), channel_id=1, source_target_pairs={{0,2},{2,0},{4,6},{6,4},{1,3},{3,1},{5,7},{7,5},{8,10},{10,8},{12,... | collective-permute-start | bytes 454664 | tf_op jit(solution)/shard_map/ppermute | solution.py:440
  8.2 9.0 %collective-permute-start.4 = (f32[296,128]{1,0:T(8,128)S(1)}, f32[296,128]{1,0:T(8,128)S(1)}, u32[]{:S(2)}, u32[]{:S(2)}) collective-permute-start(f32[296,128]{1,0:T(8,128)S(1)} %add.46), channel_id=1, source_target_pairs={{0,4},{2,6},{4,0},{6,2},{1,5},{3,7},{5,1},{7,3},{8,12},{10,14},{12... | collective-permute-start | bytes 454664 | tf_op jit(solution)/shard_map/ppermute | solution.py:440
  9.8 7.3 %collective-permute-start.6 = (f32[296,128]{1,0:T(8,128)S(1)}, f32[296,128]{1,0:T(8,128)S(1)}, u32[]{:S(2)}, u32[]{:S(2)}) collective-permute-start(f32[296,128]{1,0:T(8,128)S(1)} %add.47), channel_id=1, source_target_pairs={{0,6},{2,4},{4,2},{6,0},{1,7},{3,5},{5,3},{7,1},{8,14},{10,12},{12... | collective-permute-start | bytes 454664 | tf_op jit(solution)/shard_map/ppermute | solution.py:440
  17.3 6.1 %collective-permute-start.9 = (f32[104,128]{1,0:T(8,128)S(1)}, f32[104,128]{1,0:T(8,128)S(1)}, u32[]{:S(2)}, u32[]{:S(2)}) collective-permute-start(f32[104,128]{1,0:T(8,128)S(1)} %get-tuple-element.62), channel_id=1, source_target_pairs={{0,24},{8,16},{16,8},{24,0},{1,25},{9,17},{17,9},{25,1},{2,26},{10... | collective-permute-start | bytes 159752 | tf_op jit(solution)/shard_map/ppermute | solution.py:440
  20.9 5.1 %collective-permute-start.8 = (f32[104,128]{1,0:T(8,128)S(1)}, f32[104,128]{1,0:T(8,128)S(1)}, u32[]{:S(2)}, u32[]{:S(2)}) collective-permute-start(f32[104,128]{1,0:T(8,128)S(1)} %get-tuple-element.63), channel_id=1, source_target_pairs={{0,16},{8,24},{16,0},{24,8},{1,17},{9,25},{17,1},{25,9},{2,18},{10... | collective-permute-start | bytes 159752 | tf_op jit(solution)/shard_map/ppermute | solution.py:440
  20.9 5.1 %collective-permute-start.7 = (f32[104,128]{1,0:T(8,128)S(1)}, f32[104,128]{1,0:T(8,128)S(1)}, u32[]{:S(2)}, u32[]{:S(2)}) collective-permute-start(f32[104,128]{1,0:T(8,128)S(1)} %get-tuple-element.64), channel_id=1, source_target_pairs={{0,8},{8,0},{16,24},{24,16},{1,9},{9,1},{17,25},{25,17},{2,10},{10... | collective-permute-start | bytes 159752 | tf_op jit(solution)/shard_map/ppermute | solution.py:440
  26.0 4.0 %collective-permute-start.10 = (f32[64,128]{1,0:T(8,128)S(1)}, f32[64,128]{1,0:T(8,128)S(1)}, u32[]{:S(2)}, u32[]{:S(2)}) collective-permute-start(f32[64,128]{1,0:T(8,128)S(1)} %slice.30), channel_id=1, source_target_pairs={{0,8},{8,0},{16,24},{24,16},{1,9},{9,1},{17,25},{25,17},{2,10},{10... | collective-permute-start | bytes 98312 | tf_op jit(solution)/shard_map/ppermute | solution.py:440
  26.4 5.7 %collective-permute-start.16 = (f32[40,128]{1,0:T(8,128)S(1)}, f32[40,128]{1,0:T(8,128)S(1)}, u32[]{:S(2)}, u32[]{:S(2)}) collective-permute-start(f32[40,128]{1,0:T(8,128)S(1)} %get-tuple-element.61), channel_id=1, source_target_pairs={{0,4},{2,6},{4,0},{6,2},{1,5},{3,7},{5,1},{7,3},{8,12},{10,14},{12... | collective-permute-start | bytes 61448 | tf_op jit(solution)/shard_map/ppermute | solution.py:440
  27.9 4.1 %collective-permute-start.15 = (f32[40,128]{1,0:T(8,128)S(1)}, f32[40,128]{1,0:T(8,128)S(1)}, u32[]{:S(2)}, u32[]{:S(2)}) collective-permute-start(f32[40,128]{1,0:T(8,128)S(1)} %get-tuple-element.61), channel_id=1, source_target_pairs={{0,2},{2,0},{4,6},{6,4},{1,3},{3,1},{5,7},{7,5},{8,10},{10,8},{12,... | collective-permute-start | bytes 61448 | tf_op jit(solution)/shard_map/ppermute | solution.py:440
  28.4 4.7 %collective-permute-start.17 = (f32[40,128]{1,0:T(8,128)S(1)}, f32[40,128]{1,0:T(8,128)S(1)}, u32[]{:S(2)}, u32[]{:S(2)}) collective-permute-start(f32[40,128]{1,0:T(8,128)S(1)} %get-tuple-element.61), channel_id=1, source_target_pairs={{0,6},{2,4},{4,2},{6,0},{1,7},{3,5},{5,3},{7,1},{8,14},{10,12},{12... | collective-permute-start | bytes 61448 | tf_op jit(solution)/shard_map/ppermute | solution.py:440
  30.0 5.2 %collective-permute-start.11 = (f32[128,128]{1,0:T(8,128)S(1)}, f32[128,128]{1,0:T(8,128)S(1)}, u32[]{:S(2)}, u32[]{:S(2)}) collective-permute-start(f32[128,128]{1,0:T(8,128)S(1)} %pad_maximum_fusion.6), channel_id=1, source_target_pairs={{0,16},{8,24},{16,0},{24,8},{1,17},{9,25},{17,1},{25,9},{2,18},{10... | collective-permute-start | bytes 196616 | tf_op jit(solution)/shard_map/ppermute | solution.py:440
  33.1 5.7 %collective-permute-start.18 = (f32[4,40,128]{2,1,0:T(8,128)S(1)}, f32[4,40,128]{2,1,0:T(8,128)S(1)}, u32[]{:S(2)}, u32[]{:S(2)}) collective-permute-start(f32[4,40,128]{2,1,0:T(8,128)S(1)} %pad_maximum_fusion.2.own_ref), channel_id=1, source_target_pairs={{0,1},{1,0},{2,3},{3,2},{4,5},{5,4},{6,7},{7,6},{8,9},{9,8},{10,11... | collective-permute-start | bytes 245768 | tf_op jit(solution)/shard_map/ppermute | solution.py:436
  35.2 9.9 %collective-permute-start.14 = (f32[256,128]{1,0:T(8,128)S(1)}, f32[256,128]{1,0:T(8,128)S(1)}, u32[]{:S(2)}, u32[]{:S(2)}) collective-permute-start(f32[256,128]{1,0:T(8,128)S(1)} %pad_maximum_fusion.1), channel_id=1, source_target_pairs={{0,6},{2,4},{4,2},{6,0},{1,7},{3,5},{5,3},{7,1},{8,14},{10,12},{12... | collective-permute-start | bytes 393224 | tf_op jit(solution)/shard_map/ppermute | solution.py:440
  36.7 8.4 %collective-permute-start.13 = (f32[256,128]{1,0:T(8,128)S(1)}, f32[256,128]{1,0:T(8,128)S(1)}, u32[]{:S(2)}, u32[]{:S(2)}) collective-permute-start(f32[256,128]{1,0:T(8,128)S(1)} %pad_maximum_fusion.1), channel_id=1, source_target_pairs={{0,4},{2,6},{4,0},{6,2},{1,5},{3,7},{5,1},{7,3},{8,12},{10,14},{12... | collective-permute-start | bytes 393224 | tf_op jit(solution)/shard_map/ppermute | solution.py:440
  37.8 7.3 %collective-permute-start.12 = (f32[256,128]{1,0:T(8,128)S(1)}, f32[256,128]{1,0:T(8,128)S(1)}, u32[]{:S(2)}, u32[]{:S(2)}) collective-permute-start(f32[256,128]{1,0:T(8,128)S(1)} %pad_maximum_fusion.1), channel_id=1, source_target_pairs={{0,2},{2,0},{4,6},{6,4},{1,3},{3,1},{5,7},{7,5},{8,10},{10,8},{12,... | collective-permute-start | bytes 393224 | tf_op jit(solution)/shard_map/ppermute | solution.py:440
  38.8 6.5 %copy-start = (f32[384,1024]{1,0:T(8,128)S(1)}, f32[384,1024]{1,0:T(8,128)}, u32[]{:S(2)}) copy-start(f32[384,1024]{1,0:T(8,128)} %trail_ref.5) | copy-start | bytes 4718596
  45.2 2.1 %collective-permute-start.19 = (f32[4,256,128]{2,1,0:T(8,128)S(1)}, f32[4,256,128]{2,1,0:T(8,128)S(1)}, u32[]{:S(2)}, u32[]{:S(2)}) collective-permute-start(f32[4,256,128]{2,1,0:T(8,128)S(1)} %pad_maximum_fusion.cross_ref), channel_id=1, source_target_pairs={{0,1},{1,0},{2,3},{3,2},{4,5},{5,4},{6,7},{7,6},{8,9},{9,8},{10,11... | collective-permute-start | bytes 1572872 | tf_op jit(solution)/shard_map/ppermute | solution.py:436

commit v9 on v8

--- a/solution.py
+++ b/solution.py
@@ -16,6 +16,7 @@
 LANES = 128
 BLOCK = 32
 BATCH = 16
+STRIPS = 2
 EXTRA = 8
 SMEM = pl.BlockSpec(memory_space=pltpu.SMEM)
 VMEM = pl.BlockSpec(memory_space=pltpu.VMEM)
@@ -392,12 +393,21 @@
     def _():
         copy_top.start()
 
-    rest_scr[...] = masked(trail_ref, live_ref, pl.ds(start, half)) - dot(
-        split_ref[...], right_of(top)
-    )
-    copy_rest = pltpu.make_async_copy(rest_scr, rest_ref.at[:, pl.ds(start, half)], rest_sem)
-    copy_rest.start()
-    copy_rest.wait()
+    right = right_of(top)
+    trail = masked(trail_ref, live_ref, pl.ds(start, half))
+    height = rest_scr.shape[0] // STRIPS
+    copies = []
+    for k in range(STRIPS):
+        at = slice(k * height, (k + 1) * height)
+        rest_scr[at, :] = trail[at] - dot(split_ref[at, :], right)
+        copies.append(
+            pltpu.make_async_copy(
+                rest_scr.at[at, :], rest_ref.at[at, pl.ds(start, half)], rest_sem.at[k]
+            )
+        )
+        copies[k].start()
+    for copy in copies:
+        copy.wait()
 
     @pl.when(mine)
     def _():
@@ -422,7 +432,7 @@
             pltpu.VMEM((width, half), F32),
             pltpu.VMEM((rows, half), F32),
             pltpu.SemaphoreType.DMA,
-            pltpu.SemaphoreType.DMA,
+            pltpu.SemaphoreType.DMA((STRIPS,)),
         ]
         + ([] if other else [pltpu.VMEM((rows, width), F32), pltpu.SemaphoreType.DMA]),
         input_output_aliases={6: 0, 7: 1} if other else {},

time: 49.3 us -> 49.1 us (level)
  no operation moved by 1% of the time
where the time goes in v9:
time: 49.1 us; the launch traced here: 48.9 us
  starting transfers between devices  19.7 us (40%)
  waiting for transfers between devices  14.8 us (30%)
  Pallas kernels  12.7 us (26%)
  between operations  1.47 us (3%)
    ppermute x14, starting transfers between devices, send(): return lax.ppermute(x, axes, [(i, i ^ shift) for i in range(size)])  18.4 us
    ppermute x14, waiting for transfers between devices, send(): return lax.ppermute(x, axes, [(i, i ^ shift) for i in range(size)])  14.8 us
    pallas_call x1, Pallas kernels, factor_of(): pl.pallas_call(factor_kernel, out_shape=(jax.ShapeDtypeStruct((width, 3 *...  6.37 us
    pallas_call x2, Pallas kernels, rest_of(): pl.pallas_call(functools.partial(rest_kernel, other), out_shape=[struct(w...  3.6 us
    pallas_call x1, Pallas kernels, products_of(): pl.pallas_call(other_kernel, out_shape=(*out, jax.ShapeDtypeStruct((width...  2.14 us
    ppermute x6, starting transfers between devices, swap(): return lax.ppermute(x, 'core', [(0, 1), (1, 0)])  1.24 us
  transfers between devices with their start and end apart: 20, of which 7 were waited for; matrix products, arithmetic and copies ran while one was open for 0% of the time, Pallas kernels for 18%

profile of v9, /device:TPU:0, one launch (start us, length us, event | category | flops | bytes accessed | tf_op | source)
XLA Modules:
  0.0 48.9 jit_solution(17179131552005661275)
XLA Ops:
  1.3 2.1 %products_other.1 = (f32[296,128]{1,0:T(8,128)S(1)}, f32[296,128]{1,0:T(8,128)S(1)}, f32[296,128]{1,0:T(8,128)S(1)}, f32[296,128]{1,0:T(8,128)S(1)}, bf16[256,11...) custom-call(s32[1]{0:T(128)} %bitcast.place_ref, ...), custom_call_target="tpu_custom_call" | custom-call | flops 301989888 | bytes 786432 | tf_op jit(solution)/shard_map/products_other/pallas_call | solution.py:171
  3.4 0.5 %collective-permute-start.1 = (f32[296,128]{1,0:T(8,128)S(1)}, f32[296,128]{1,0:T(8,128)S(1)}, u32[]{:S(2)}, u32[]{:S(2)}) collective-permute-start(f32[296,128]{1,0:T(8,128)S(1)} %get-tuple-element.37), channel_id=1, source_target_pairs={{0,1},{1,0},{2,3},{3,2},{4,5},{5,4},{6,7},{7,6},{8,9},{9,8},{10,11... | collective-permute-start | bytes 454664 | tf_op jit(solution)/shard_map/ppermute | solution.py:446
  4.0 0.4 collective-permute-start.5
  4.5 0.6 %products_own.1 = (f32[296,128]{1,0:T(8,128)S(1)}, f32[296,128]{1,0:T(8,128)S(1)}, f32[296,128]{1,0:T(8,128)S(1)}, f32[296,128]{1,0:T(8,128)S(1)}, bf16[384,768]{1,0:T(8,128)(2,1)S(1)}) custom-call(s32[1]{0:T(128)} %bitcast.place_ref, s32[1]{0:T(128)S(6)} %copy.10.live_ref, bf16[256,1152]{1,0:T(8,128)(2,1)S(1)} %get-tuple-element.30.left_ref, ...), custom_call_target="tpu_custom_call" | custom-call | flops 301989888 | bytes 786432 | tf_op jit(solution)/shard_map/products_own/pallas_call | solution.py:189
  5.2 3.0 %collective-permute-start.2 = (f32[296,128]{1,0:T(8,128)S(1)}, f32[296,128]{1,0:T(8,128)S(1)}, u32[]{:S(2)}, u32[]{:S(2)}) collective-permute-start(f32[296,128]{1,0:T(8,128)S(1)} %add.44), channel_id=1, source_target_pairs={{0,2},{2,0},{4,6},{6,4},{1,3},{3,1},{5,7},{7,5},{8,10},{10,8},{12,... | collective-permute-start | bytes 454664 | tf_op jit(solution)/shard_map/ppermute | solution.py:450
  8.2 1.6 %collective-permute-start.4 = (f32[296,128]{1,0:T(8,128)S(1)}, f32[296,128]{1,0:T(8,128)S(1)}, u32[]{:S(2)}, u32[]{:S(2)}) collective-permute-start(f32[296,128]{1,0:T(8,128)S(1)} %add.46), channel_id=1, source_target_pairs={{0,4},{2,6},{4,0},{6,2},{1,5},{3,7},{5,1},{7,3},{8,12},{10,14},{12... | collective-permute-start | bytes 454664 | tf_op jit(solution)/shard_map/ppermute | solution.py:450
  9.9 2.8 %collective-permute-done.2 = f32[296,128]{1,0:T(8,128)S(1)} collective-permute-done((f32[296,128]{1,0:T(8,128)S(1)}, f32[296,128]{1,0:T(8,128)S(1)}, u32[]{:S(2)}, u32[]{:S(2)}) %collective-permute-start.2) | collective-permute-done | bytes 151584 | tf_op jit(solution)/shard_map/ppermute | solution.py:450
  12.7 4.4 %collective-permute-done.4 = f32[296,128]{1,0:T(8,128)S(1)} collective-permute-done((f32[296,128]{1,0:T(8,128)S(1)}, f32[296,128]{1,0:T(8,128)S(1)}, u32[]{:S(2)}, u32[]{:S(2)}) %collective-permute-start.4) | collective-permute-done | bytes 151584 | tf_op jit(solution)/shard_map/ppermute | solution.py:450
  17.3 3.7 %collective-permute-start.9 = (f32[104,128]{1,0:T(8,128)S(1)}, f32[104,128]{1,0:T(8,128)S(1)}, u32[]{:S(2)}, u32[]{:S(2)}) collective-permute-start(f32[104,128]{1,0:T(8,128)S(1)} %get-tuple-element.62), channel_id=1, source_target_pairs={{0,24},{8,16},{16,8},{24,0},{1,25},{9,17},{17,9},{25,1},{2,26},{10... | collective-permute-start | bytes 159752 | tf_op jit(solution)/shard_map/ppermute | solution.py:450
  20.9 0.8 %collective-permute-start.7 = (f32[104,128]{1,0:T(8,128)S(1)}, f32[104,128]{1,0:T(8,128)S(1)}, u32[]{:S(2)}, u32[]{:S(2)}) collective-permute-start(f32[104,128]{1,0:T(8,128)S(1)} %get-tuple-element.64), channel_id=1, source_target_pairs={{0,8},{8,0},{16,24},{24,16},{1,9},{9,1},{17,25},{25,17},{2,10},{10... | collective-permute-start | bytes 159752 | tf_op jit(solution)/shard_map/ppermute | solution.py:450
  21.7 1.6 %collective-permute-done.9 = f32[104,128]{1,0:T(8,128)S(1)} collective-permute-done((f32[104,128]{1,0:T(8,128)S(1)}, f32[104,128]{1,0:T(8,128)S(1)}, u32[]{:S(2)}, u32[]{:S(2)}) %collective-permute-start.9) | collective-permute-done | bytes 53280 | tf_op jit(solution)/shard_map/ppermute | solution.py:450
  23.4 2.6 %collective-permute-done.8 = f32[104,128]{1,0:T(8,128)S(1)} collective-permute-done((f32[104,128]{1,0:T(8,128)S(1)}, f32[104,128]{1,0:T(8,128)S(1)}, u32[]{:S(2)}, u32[]{:S(2)}) %collective-permute-start.8) | collective-permute-done | bytes 53280 | tf_op jit(solution)/shard_map/ppermute | solution.py:450
  26.4 1.5 %collective-permute-start.16 = (f32[40,128]{1,0:T(8,128)S(1)}, f32[40,128]{1,0:T(8,128)S(1)}, u32[]{:S(2)}, u32[]{:S(2)}) collective-permute-start(f32[40,128]{1,0:T(8,128)S(1)} %get-tuple-element.61), channel_id=1, source_target_pairs={{0,4},{2,6},{4,0},{6,2},{1,5},{3,7},{5,1},{7,3},{8,12},{10,14},{12... | collective-permute-start | bytes 61448 | tf_op jit(solution)/shard_map/ppermute | solution.py:450
  27.9 0.5 %collective-permute-start.15 = (f32[40,128]{1,0:T(8,128)S(1)}, f32[40,128]{1,0:T(8,128)S(1)}, u32[]{:S(2)}, u32[]{:S(2)}) collective-permute-start(f32[40,128]{1,0:T(8,128)S(1)} %get-tuple-element.61), channel_id=1, source_target_pairs={{0,2},{2,0},{4,6},{6,4},{1,3},{3,1},{5,7},{7,5},{8,10},{10,8},{12,... | collective-permute-start | bytes 61448 | tf_op jit(solution)/shard_map/ppermute | solution.py:450
  28.4 1.4 %collective-permute-start.17 = (f32[40,128]{1,0:T(8,128)S(1)}, f32[40,128]{1,0:T(8,128)S(1)}, u32[]{:S(2)}, u32[]{:S(2)}) collective-permute-start(f32[40,128]{1,0:T(8,128)S(1)} %get-tuple-element.61), channel_id=1, source_target_pairs={{0,6},{2,4},{4,2},{6,0},{1,7},{3,5},{5,3},{7,1},{8,14},{10,12},{12... | collective-permute-start | bytes 61448 | tf_op jit(solution)/shard_map/ppermute | solution.py:450
  30.0 2.0 %collective-permute-start.11 = (f32[128,128]{1,0:T(8,128)S(1)}, f32[128,128]{1,0:T(8,128)S(1)}, u32[]{:S(2)}, u32[]{:S(2)}) collective-permute-start(f32[128,128]{1,0:T(8,128)S(1)} %pad_maximum_fusion.6), channel_id=1, source_target_pairs={{0,16},{8,24},{16,0},{24,8},{1,17},{9,25},{17,1},{25,9},{2,18},{10... | collective-permute-start | bytes 196616 | tf_op jit(solution)/shard_map/ppermute | solution.py:450
  32.0 1.1 %collective-permute-done.17 = f32[40,128]{1,0:T(8,128)S(1)} collective-permute-done((f32[40,128]{1,0:T(8,128)S(1)}, f32[40,128]{1,0:T(8,128)S(1)}, u32[]{:S(2)}, u32[]{:S(2)}) %collective-permute-start.17) | collective-permute-done | bytes 20512 | tf_op jit(solution)/shard_map/ppermute | solution.py:450
  33.2 2.0 %collective-permute-done.11 = f32[128,128]{1,0:T(8,128)S(1)} collective-permute-done((f32[128,128]{1,0:T(8,128)S(1)}, f32[128,128]{1,0:T(8,128)S(1)}, u32[]{:S(2)}, u32[]{:S(2)}) %collective-permute-start.11) | collective-permute-done | bytes 65568 | tf_op jit(solution)/shard_map/ppermute | solution.py:450
  35.2 1.5 %collective-permute-start.14 = (f32[256,128]{1,0:T(8,128)S(1)}, f32[256,128]{1,0:T(8,128)S(1)}, u32[]{:S(2)}, u32[]{:S(2)}) collective-permute-start(f32[256,128]{1,0:T(8,128)S(1)} %pad_maximum_fusion.1), channel_id=1, source_target_pairs={{0,6},{2,4},{4,2},{6,0},{1,7},{3,5},{5,3},{7,1},{8,14},{10,12},{12... | collective-permute-start | bytes 393224 | tf_op jit(solution)/shard_map/ppermute | solution.py:450
  36.7 1.1 %collective-permute-start.13 = (f32[256,128]{1,0:T(8,128)S(1)}, f32[256,128]{1,0:T(8,128)S(1)}, u32[]{:S(2)}, u32[]{:S(2)}) collective-permute-start(f32[256,128]{1,0:T(8,128)S(1)} %pad_maximum_fusion.1), channel_id=1, source_target_pairs={{0,4},{2,6},{4,0},{6,2},{1,5},{3,7},{5,1},{7,3},{8,12},{10,14},{12... | collective-permute-start | bytes 393224 | tf_op jit(solution)/shard_map/ppermute | solution.py:450
  37.8 0.9 %collective-permute-start.12 = (f32[256,128]{1,0:T(8,128)S(1)}, f32[256,128]{1,0:T(8,128)S(1)}, u32[]{:S(2)}, u32[]{:S(2)}) collective-permute-start(f32[256,128]{1,0:T(8,128)S(1)} %pad_maximum_fusion.1), channel_id=1, source_target_pairs={{0,2},{2,0},{4,6},{6,4},{1,3},{3,1},{5,7},{7,5},{8,10},{10,8},{12,... | collective-permute-start | bytes 393224 | tf_op jit(solution)/shard_map/ppermute | solution.py:450
  38.8 6.4 %factor.1 = (bf16[256,768]{1,0:T(8,128)(2,1)S(1)}, bf16[384,768]{1,0:T(8,128)(2,1)S(1)}, f32[384,256]{1,0:T(8,128)S(1)}, f32[8,128]{1,0:T(8,128)S(1)}) custom-call(s32[1]{0:T(128)} %bitcast.place_ref, f32[4,40,128]{2,1,0:T(8,128)S(1)} %pad_maximum_fusion.2.own_ref, f32[4,40,128]{2,1,0:T(8,128)S(1)} %collective-permute-done.18.other_ref, ...), custom_call_target="tpu_custom_call" | custom-call | flops 6000000000 | bytes 393216 | tf_op jit(solution)/shard_map/factor/pallas_call | solution.py:338
  45.3 1.9 %rest_own.1 = (f32[256,256]{1,0:T(8,128)}, f32[384,1024]{1,0:T(8,128)}, f32[384,256]{1,0:T(8,128)}) custom-call(s32[1]{0:T(128)} %bitcast.place_ref, s32[1]{0:T(128)S(6)} %copy.10.live_ref, bf16[256,768]{1,0:T(8,128)(2,1)S(1)} %get-tuple-element.44.inverse_ref, bf16[384,768]{1,0:T(8,128)(2,1)S(1)} %get-tuple-element.45.split_ref, ...), custom_call_target="tpu_custom_call" | custom-call | flops 503316480 | bytes 1572864 | tf_op jit(solution)/shard_map/rest_own/pallas_call | solution.py:425
  47.2 1.7 %rest_other.1 = (f32[256,256]{1,0:T(8,128)}, f32[384,1024]{1,0:T(8,128)}) custom-call(s32[1]{0:T(128)} %bitcast.place_ref, s32[1]{0:T(128)S(6)} %copy.10.live_ref, bf16[256,768]{1,0:T(8,128)(2,1)S(1)} %get-tuple-element.44.inverse_ref, bf16[384,768]{1,0:T(8,128)(2,1)S(1)} %get-tuple-element.45.split_ref, ...), custom_call_target="tpu_custom_call", output_to_operand_aliasing={{0}: (6, {}), {1}: (7, {})} | custom-call | flops 503316480 | bytes 1572864 | tf_op jit(solution)/shard_map/rest_other/pallas_call | solution.py:425
  (37 shorter events, 1.1 us)
Async XLA Ops:
  3.4 1.7 %collective-permute-start.1 = (f32[296,128]{1,0:T(8,128)S(1)}, f32[296,128]{1,0:T(8,128)S(1)}, u32[]{:S(2)}, u32[]{:S(2)}) collective-permute-start(f32[296,128]{1,0:T(8,128)S(1)} %get-tuple-element.37), channel_id=1, source_target_pairs={{0,1},{1,0},{2,3},{3,2},{4,5},{5,4},{6,7},{7,6},{8,9},{9,8},{10,11... | collective-permute-start | bytes 454664 | tf_op jit(solution)/shard_map/ppermute | solution.py:446
  4.0 4.2 %collective-permute-start.3 = (f32[296,128]{1,0:T(8,128)S(1)}, f32[296,128]{1,0:T(8,128)S(1)}, u32[]{:S(2)}, u32[]{:S(2)}) collective-permute-start(f32[296,128]{1,0:T(8,128)S(1)} %get-tuple-element.39), channel_id=1, source_target_pairs={{0,1},{1,0},{2,3},{3,2},{4,5},{5,4},{6,7},{7,6},{8,9},{9,8},{10,11... | collective-permute-start | bytes 454664 | tf_op jit(solution)/shard_map/ppermute | solution.py:446
  4.0 5.8 %collective-permute-start.5 = (f32[296,128]{1,0:T(8,128)S(1)}, f32[296,128]{1,0:T(8,128)S(1)}, u32[]{:S(2)}, u32[]{:S(2)}) collective-permute-start(f32[296,128]{1,0:T(8,128)S(1)} %get-tuple-element.41), channel_id=1, source_target_pairs={{0,1},{1,0},{2,3},{3,2},{4,5},{5,4},{6,7},{7,6},{8,9},{9,8},{10,11... | collective-permute-start | bytes 454664 | tf_op jit(solution)/shard_map/ppermute | solution.py:446
  4.5 5.4 %collective-permute-start = (f32[296,128]{1,0:T(8,128)S(1)}, f32[296,128]{1,0:T(8,128)S(1)}, u32[]{:S(2)}, u32[]{:S(2)}) collective-permute-start(f32[296,128]{1,0:T(8,128)S(1)} %get-tuple-element.35), channel_id=1, source_target_pairs={{0,1},{1,0},{2,3},{3,2},{4,5},{5,4},{6,7},{7,6},{8,9},{9,8},{10,11... | collective-permute-start | bytes 454664 | tf_op jit(solution)/shard_map/ppermute | solution.py:446
  5.2 7.5 %collective-permute-start.2 = (f32[296,128]{1,0:T(8,128)S(1)}, f32[296,128]{1,0:T(8,128)S(1)}, u32[]{:S(2)}, u32[]{:S(2)}) collective-permute-start(f32[296,128]{1,0:T(8,128)S(1)} %add.44), channel_id=1, source_target_pairs={{0,2},{2,0},{4,6},{6,4},{1,3},{3,1},{5,7},{7,5},{8,10},{10,8},{12,... | collective-permute-start | bytes 454664 | tf_op jit(solution)/shard_map/ppermute | solution.py:450
  8.2 9.0 %collective-permute-start.4 = (f32[296,128]{1,0:T(8,128)S(1)}, f32[296,128]{1,0:T(8,128)S(1)}, u32[]{:S(2)}, u32[]{:S(2)}) collective-permute-start(f32[296,128]{1,0:T(8,128)S(1)} %add.46), channel_id=1, source_target_pairs={{0,4},{2,6},{4,0},{6,2},{1,5},{3,7},{5,1},{7,3},{8,12},{10,14},{12... | collective-permute-start | bytes 454664 | tf_op jit(solution)/shard_map/ppermute | solution.py:450
  9.8 7.3 %collective-permute-start.6 = (f32[296,128]{1,0:T(8,128)S(1)}, f32[296,128]{1,0:T(8,128)S(1)}, u32[]{:S(2)}, u32[]{:S(2)}) collective-permute-start(f32[296,128]{1,0:T(8,128)S(1)} %add.47), channel_id=1, source_target_pairs={{0,6},{2,4},{4,2},{6,0},{1,7},{3,5},{5,3},{7,1},{8,14},{10,12},{12... | collective-permute-start | bytes 454664 | tf_op jit(solution)/shard_map/ppermute | solution.py:450
  17.3 6.1 %collective-permute-start.9 = (f32[104,128]{1,0:T(8,128)S(1)}, f32[104,128]{1,0:T(8,128)S(1)}, u32[]{:S(2)}, u32[]{:S(2)}) collective-permute-start(f32[104,128]{1,0:T(8,128)S(1)} %get-tuple-element.62), channel_id=1, source_target_pairs={{0,24},{8,16},{16,8},{24,0},{1,25},{9,17},{17,9},{25,1},{2,26},{10... | collective-permute-start | bytes 159752 | tf_op jit(solution)/shard_map/ppermute | solution.py:450
  20.9 5.1 %collective-permute-start.8 = (f32[104,128]{1,0:T(8,128)S(1)}, f32[104,128]{1,0:T(8,128)S(1)}, u32[]{:S(2)}, u32[]{:S(2)}) collective-permute-start(f32[104,128]{1,0:T(8,128)S(1)} %get-tuple-element.63), channel_id=1, source_target_pairs={{0,16},{8,24},{16,0},{24,8},{1,17},{9,25},{17,1},{25,9},{2,18},{10... | collective-permute-start | bytes 159752 | tf_op jit(solution)/shard_map/ppermute | solution.py:450
  20.9 5.1 %collective-permute-start.7 = (f32[104,128]{1,0:T(8,128)S(1)}, f32[104,128]{1,0:T(8,128)S(1)}, u32[]{:S(2)}, u32[]{:S(2)}) collective-permute-start(f32[104,128]{1,0:T(8,128)S(1)} %get-tuple-element.64), channel_id=1, source_target_pairs={{0,8},{8,0},{16,24},{24,16},{1,9},{9,1},{17,25},{25,17},{2,10},{10... | collective-permute-start | bytes 159752 | tf_op jit(solution)/shard_map/ppermute | solution.py:450
  26.0 4.0 %collective-permute-start.10 = (f32[64,128]{1,0:T(8,128)S(1)}, f32[64,128]{1,0:T(8,128)S(1)}, u32[]{:S(2)}, u32[]{:S(2)}) collective-permute-start(f32[64,128]{1,0:T(8,128)S(1)} %slice.30), channel_id=1, source_target_pairs={{0,8},{8,0},{16,24},{24,16},{1,9},{9,1},{17,25},{25,17},{2,10},{10... | collective-permute-start | bytes 98312 | tf_op jit(solution)/shard_map/ppermute | solution.py:450
  26.4 5.7 %collective-permute-start.16 = (f32[40,128]{1,0:T(8,128)S(1)}, f32[40,128]{1,0:T(8,128)S(1)}, u32[]{:S(2)}, u32[]{:S(2)}) collective-permute-start(f32[40,128]{1,0:T(8,128)S(1)} %get-tuple-element.61), channel_id=1, source_target_pairs={{0,4},{2,6},{4,0},{6,2},{1,5},{3,7},{5,1},{7,3},{8,12},{10,14},{12... | collective-permute-start | bytes 61448 | tf_op jit(solution)/shard_map/ppermute | solution.py:450
  27.9 4.1 %collective-permute-start.15 = (f32[40,128]{1,0:T(8,128)S(1)}, f32[40,128]{1,0:T(8,128)S(1)}, u32[]{:S(2)}, u32[]{:S(2)}) collective-permute-start(f32[40,128]{1,0:T(8,128)S(1)} %get-tuple-element.61), channel_id=1, source_target_pairs={{0,2},{2,0},{4,6},{6,4},{1,3},{3,1},{5,7},{7,5},{8,10},{10,8},{12,... | collective-permute-start | bytes 61448 | tf_op jit(solution)/shard_map/ppermute | solution.py:450
  28.4 4.7 %collective-permute-start.17 = (f32[40,128]{1,0:T(8,128)S(1)}, f32[40,128]{1,0:T(8,128)S(1)}, u32[]{:S(2)}, u32[]{:S(2)}) collective-permute-start(f32[40,128]{1,0:T(8,128)S(1)} %get-tuple-element.61), channel_id=1, source_target_pairs={{0,6},{2,4},{4,2},{6,0},{1,7},{3,5},{5,3},{7,1},{8,14},{10,12},{12... | collective-permute-start | bytes 61448 | tf_op jit(solution)/shard_map/ppermute | solution.py:450
  30.0 5.2 %collective-permute-start.11 = (f32[128,128]{1,0:T(8,128)S(1)}, f32[128,128]{1,0:T(8,128)S(1)}, u32[]{:S(2)}, u32[]{:S(2)}) collective-permute-start(f32[128,128]{1,0:T(8,128)S(1)} %pad_maximum_fusion.6), channel_id=1, source_target_pairs={{0,16},{8,24},{16,0},{24,8},{1,17},{9,25},{17,1},{25,9},{2,18},{10... | collective-permute-start | bytes 196616 | tf_op jit(solution)/shard_map/ppermute | solution.py:450
  33.1 5.7 %collective-permute-start.18 = (f32[4,40,128]{2,1,0:T(8,128)S(1)}, f32[4,40,128]{2,1,0:T(8,128)S(1)}, u32[]{:S(2)}, u32[]{:S(2)}) collective-permute-start(f32[4,40,128]{2,1,0:T(8,128)S(1)} %pad_maximum_fusion.2.own_ref), channel_id=1, source_target_pairs={{0,1},{1,0},{2,3},{3,2},{4,5},{5,4},{6,7},{7,6},{8,9},{9,8},{10,11... | collective-permute-start | bytes 245768 | tf_op jit(solution)/shard_map/ppermute | solution.py:446
  35.2 9.9 %collective-permute-start.14 = (f32[256,128]{1,0:T(8,128)S(1)}, f32[256,128]{1,0:T(8,128)S(1)}, u32[]{:S(2)}, u32[]{:S(2)}) collective-permute-start(f32[256,128]{1,0:T(8,128)S(1)} %pad_maximum_fusion.1), channel_id=1, source_target_pairs={{0,6},{2,4},{4,2},{6,0},{1,7},{3,5},{5,3},{7,1},{8,14},{10,12},{12... | collective-permute-start | bytes 393224 | tf_op jit(solution)/shard_map/ppermute | solution.py:450
  36.7 8.4 %collective-permute-start.13 = (f32[256,128]{1,0:T(8,128)S(1)}, f32[256,128]{1,0:T(8,128)S(1)}, u32[]{:S(2)}, u32[]{:S(2)}) collective-permute-start(f32[256,128]{1,0:T(8,128)S(1)} %pad_maximum_fusion.1), channel_id=1, source_target_pairs={{0,4},{2,6},{4,0},{6,2},{1,5},{3,7},{5,1},{7,3},{8,12},{10,14},{12... | collective-permute-start | bytes 393224 | tf_op jit(solution)/shard_map/ppermute | solution.py:450
  37.8 7.3 %collective-permute-start.12 = (f32[256,128]{1,0:T(8,128)S(1)}, f32[256,128]{1,0:T(8,128)S(1)}, u32[]{:S(2)}, u32[]{:S(2)}) collective-permute-start(f32[256,128]{1,0:T(8,128)S(1)} %pad_maximum_fusion.1), channel_id=1, source_target_pairs={{0,2},{2,0},{4,6},{6,4},{1,3},{3,1},{5,7},{7,5},{8,10},{10,8},{12,... | collective-permute-start | bytes 393224 | tf_op jit(solution)/shard_map/ppermute | solution.py:450
  38.8 6.5 %copy-start = (f32[384,1024]{1,0:T(8,128)S(1)}, f32[384,1024]{1,0:T(8,128)}, u32[]{:S(2)}) copy-start(f32[384,1024]{1,0:T(8,128)} %trail_ref.5) | copy-start | bytes 4718596
  45.2 2.0 %collective-permute-start.19 = (f32[4,256,128]{2,1,0:T(8,128)S(1)}, f32[4,256,128]{2,1,0:T(8,128)S(1)}, u32[]{:S(2)}, u32[]{:S(2)}) collective-permute-start(f32[4,256,128]{2,1,0:T(8,128)S(1)} %pad_maximum_fusion.cross_ref), channel_id=1, source_target_pairs={{0,1},{1,0},{2,3},{3,2},{4,5},{5,4},{6,7},{7,6},{8,9},{9,8},{10,11... | collective-permute-start | bytes 1572872 | tf_op jit(solution)/shard_map/ppermute | solution.py:446
